TPU v7x, 32 devices: a whole 2x2x4 slice. The times are simulated.
32 devices in a mesh: dp: 8 (over z, x), fsdp: 4 (over y, core).
Axes of the slice: x: 2, y: 2, z: 4, core: 2. Of those that a mesh axis runs over, the one named last changes fastest.
Arguments:
- tokens: bfloat16 [16, 2048, 768], P('dp', 'fsdp'), may hold values from -6 to 6
- teacher: bfloat16 [16, 2048, 768], P('dp', 'fsdp'), may hold values from -6 to 6
- lengths: int32 [16], replicated, may hold values from 256 to 2048, as said below
- dealing: int32 [16], replicated, may hold values from 0 to 15, as said below
- query_weight: bfloat16 [768, 768], P(('dp', 'fsdp')), may hold values from -0.4375 to 0.4375
- key_weight: bfloat16 [768, 768], P(('dp', 'fsdp')), may hold values from -0.21875 to 0.21875
- value_weight: bfloat16 [768, 768], P(('dp', 'fsdp')), may hold values from -0.21875 to 0.21875
- output_weight: bfloat16 [768, 768], P(('dp', 'fsdp')), may hold values from -0.875 to 0.875
- inner_weight: bfloat16 [768, 3072], P(('dp', 'fsdp')), may hold values from -0.21875 to 0.21875
- outer_weight: bfloat16 [3072, 768], P(('dp', 'fsdp')), may hold values from -0.109375 to 0.109375
- query_bias: bfloat16 [768], P(('dp', 'fsdp')), may hold values from -3 to 3
- value_bias: bfloat16 [768], P(('dp', 'fsdp')), may hold values from -3 to 3
- output_bias: bfloat16 [768], P(('dp', 'fsdp')), may hold values from -2 to 2
- norm_gain: bfloat16 [768], P(('dp', 'fsdp')), may hold values from 0.5 to 1.5
- norm_shift: bfloat16 [768], P(('dp', 'fsdp')), may hold values from -2 to 2
- inner_bias: bfloat16 [3072], P(('dp', 'fsdp')), may hold values from -3 to 3
- outer_bias: bfloat16 [768], P(('dp', 'fsdp')), may hold values from -2 to 2
- final_gain: bfloat16 [768], P(('dp', 'fsdp')), may hold values from 0.5 to 1.5
- final_shift: bfloat16 [768], P(('dp', 'fsdp')), may hold values from -2 to 2
Outputs:
- output: bfloat16 [16, 2048, 768], P('dp', 'fsdp')
- input_grad: bfloat16 [16, 2048, 768], P('dp', 'fsdp')
- grad_query_weight: float32 [768, 768], P(('dp', 'fsdp'))
- grad_key_weight: float32 [768, 768], P(('dp', 'fsdp'))
- grad_value_weight: float32 [768, 768], P(('dp', 'fsdp'))
- grad_output_weight: float32 [768, 768], P(('dp', 'fsdp'))
- grad_inner_weight: float32 [768, 3072], P(('dp', 'fsdp'))
- grad_outer_weight: float32 [3072, 768], P(('dp', 'fsdp'))
- grad_query_bias: float32 [768], P(('dp', 'fsdp'))
- grad_value_bias: float32 [768], P(('dp', 'fsdp'))
- grad_output_bias: float32 [768], P(('dp', 'fsdp'))
- grad_norm_gain: float32 [768], P(('dp', 'fsdp'))
- grad_norm_shift: float32 [768], P(('dp', 'fsdp'))
- grad_inner_bias: float32 [3072], P(('dp', 'fsdp'))
- grad_outer_bias: float32 [768], P(('dp', 'fsdp'))
- grad_final_gain: float32 [768], P(('dp', 'fsdp'))
- grad_final_shift: float32 [768], P(('dp', 'fsdp'))
Inputs may be any that keep to these rules, and one draw needn't show every extreme that they name: `lengths`: the longest sequence has exactly 2048 valid tokens. `dealing`: a permutation of the 16 sequences; slots 2 g and 2 g + 1 hold one of the longer half and one of the shorter half of the sequences.
All inputs are finite; a program needn't handle non-finite values.
Results may differ from a plain program's by a relative error of at most 0.019.
Values may be sent and summed in bfloat16 or wider, within the bound.
No kernel may reach another device: no remote copies, remote signals or barrier semaphores. Data moves between devices by JAX's collectives and lax.ppermute only.
A program may use at most 256 MiB of HBM per device.

v0:
```python
from functools import partial
import math

import jax
import jax.numpy as jnp
from jax import lax
from jax.sharding import PartitionSpec as P

HEADS = 12


epsilon = 1e-05
masked_score = -1e30


def layer_norm(resid, gain, shift):
    average = jnp.mean(resid, axis=-1, keepdims=True)
    centred = resid - average
    second = jnp.mean(centred * centred, axis=-1, keepdims=True)
    return centred * lax.rsqrt(second + epsilon) * gain + shift


def dense(left, right):
    return jnp.dot(left, right, preferred_element_type=jnp.float32)


def across_rows(left, right):
    return lax.dot_general(
        left, right, (((0,), (0,)), ((), ())), preferred_element_type=jnp.float32
    )


def across_cols(left, right):
    return lax.dot_general(
        left, right, (((1,), (1,)), ((), ())), preferred_element_type=jnp.float32
    )


def alive_keys(seq_lens, offset, block_len):
    positions = offset + lax.iota(jnp.int32, block_len)
    return (positions[None, :] < seq_lens[:, None])[:, None, None, :]


def attend_forward(query_heads, seq_lens, score_scale, running, shard_part):
    key_rows, value_rows = shard_part
    slot_count, key_count = (key_rows.shape[0], key_rows.shape[1])
    block_len = math.gcd(key_count, 512)
    head_count, head_dim = (query_heads.shape[2], query_heads.shape[3])

    def advance(number, status):
        row_max, denominator, numerator = status
        offset = number * block_len
        key_part = lax.dynamic_slice_in_dim(key_rows, offset, block_len, 1).reshape(
            slot_count, block_len, head_count, head_dim
        )
        value_part = lax.dynamic_slice_in_dim(value_rows, offset, block_len, 1).reshape(
            slot_count, block_len, head_count, head_dim
        )
        scores = (
            jnp.einsum("srhd,snhd->shrn", query_heads, key_part, preferred_element_type=jnp.float32)
            * score_scale
        )
        alive_mask = alive_keys(seq_lens, offset, block_len)
        scores = jnp.where(alive_mask, scores, masked_score)
        new_max = jnp.maximum(row_max, jnp.max(scores, axis=-1))
        weights = jnp.where(alive_mask, jnp.exp(scores - new_max[..., None]), 0.0)
        factor = jnp.exp(row_max - new_max)
        denominator = denominator * factor + jnp.sum(weights, axis=-1)
        gained = jnp.einsum(
            "shrn,snhd->srhd",
            weights.astype(jnp.bfloat16),
            value_part,
            preferred_element_type=jnp.float32,
        )
        numerator = numerator * jnp.transpose(factor, (0, 2, 1))[..., None] + gained
        return (new_max, denominator, numerator)

    return lax.fori_loop(0, key_count // block_len, advance, running)


def attend_query_back(
    query_heads, grad_heads, log_total, delta, seq_lens, score_scale, running, shard_part
):
    key_rows, value_rows = shard_part
    slot_count, key_count = (key_rows.shape[0], key_rows.shape[1])
    block_len = math.gcd(key_count, 512)
    head_count, head_dim = (query_heads.shape[2], query_heads.shape[3])

    def advance(number, grad_query):
        offset = number * block_len
        key_part = lax.dynamic_slice_in_dim(key_rows, offset, block_len, 1).reshape(
            slot_count, block_len, head_count, head_dim
        )
        value_part = lax.dynamic_slice_in_dim(value_rows, offset, block_len, 1).reshape(
            slot_count, block_len, head_count, head_dim
        )
        scores = (
            jnp.einsum("srhd,snhd->shrn", query_heads, key_part, preferred_element_type=jnp.float32)
            * score_scale
        )
        alive_mask = alive_keys(seq_lens, offset, block_len)
        probs = jnp.where(alive_mask, jnp.exp(scores - log_total[..., None]), 0.0)
        grad_probs = jnp.einsum(
            "srhd,snhd->shrn", grad_heads, value_part, preferred_element_type=jnp.float32
        )
        grad_scores = (probs * (grad_probs - delta[..., None])).astype(jnp.bfloat16)
        return (
            grad_query
            + jnp.einsum(
                "shrn,snhd->srhd", grad_scores, key_part, preferred_element_type=jnp.float32
            )
            * score_scale
        )

    return lax.fori_loop(0, key_count // block_len, advance, running)


def attend_key_back(
    key_heads, value_heads, key_alive, stats_whole, score_scale, running, shard_part
):
    query_rows, grad_rows = shard_part
    lse_whole, delta_whole = stats_whole
    slot_count, query_count = (query_rows.shape[0], query_rows.shape[1])
    block_len = math.gcd(query_count, 512)

    def advance(number, status):
        grad_keys, grad_values = status
        offset = number * block_len
        query_part = lax.dynamic_slice_in_dim(query_rows, offset, block_len, 1)
        grad_part = lax.dynamic_slice_in_dim(grad_rows, offset, block_len, 1)
        lse_part = jnp.transpose(
            lax.dynamic_slice_in_dim(lse_whole, offset, block_len, 1), (0, 2, 1)
        )
        delta_part = jnp.transpose(
            lax.dynamic_slice_in_dim(delta_whole, offset, block_len, 1), (0, 2, 1)
        )
        scores = (
            jnp.einsum("srhd,snhd->shrn", query_part, key_heads, preferred_element_type=jnp.float32)
            * score_scale
        )
        probs = jnp.where(key_alive, jnp.exp(scores - lse_part[..., None]), 0.0)
        grad_probs = jnp.einsum(
            "srhd,snhd->shrn", grad_part, value_heads, preferred_element_type=jnp.float32
        )
        grad_scores = (probs * (grad_probs - delta_part[..., None])).astype(jnp.bfloat16)
        grad_keys = (
            grad_keys
            + jnp.einsum(
                "shrn,srhd->snhd", grad_scores, query_part, preferred_element_type=jnp.float32
            )
            * score_scale
        )
        grad_values = grad_values + jnp.einsum(
            "shrn,srhd->snhd",
            probs.astype(jnp.bfloat16),
            grad_part,
            preferred_element_type=jnp.float32,
        )
        return (grad_keys, grad_values)

    return lax.fori_loop(0, query_count // block_len, advance, running)


def shards(
    tokens,
    teacher,
    lengths,
    dealing,
    query_weight,
    key_weight,
    value_weight,
    output_weight,
    inner_weight,
    outer_weight,
    query_bias,
    value_bias,
    output_bias,
    norm_gain,
    norm_shift,
    inner_bias,
    outer_bias,
    final_gain,
    final_shift,
):
    slot_count, row_count, model_width = tokens.shape
    fsdp_count = lax.axis_size("fsdp")
    seq_len = row_count * fsdp_count
    head_count = HEADS
    head_dim = model_width // head_count
    score_scale = 1.0 / math.sqrt(head_dim)
    token_count = slot_count * row_count
    seq_total = dealing.shape[0]
    spread_rows = lax.all_to_all(tokens, "dp", split_axis=1, concat_axis=0, tiled=True)
    spread_rows = jnp.take(spread_rows, dealing, axis=0)
    local_tokens = lax.all_to_all(spread_rows, "dp", split_axis=0, concat_axis=1, tiled=True)
    work_lens = jnp.take(lengths, dealing)
    seq_lens = lax.dynamic_slice_in_dim(work_lens, lax.axis_index("dp") * slot_count, slot_count)
    attn_params = (
        lax.all_gather(query_weight, ("dp", "fsdp"), axis=0, tiled=True),
        lax.all_gather(key_weight, ("dp", "fsdp"), axis=0, tiled=True),
        lax.all_gather(value_weight, ("dp", "fsdp"), axis=0, tiled=True),
        lax.all_gather(output_weight, ("dp", "fsdp"), axis=0, tiled=True),
        lax.all_gather(query_bias, ("dp", "fsdp"), axis=0, tiled=True),
        lax.all_gather(value_bias, ("dp", "fsdp"), axis=0, tiled=True),
        lax.all_gather(output_bias, ("dp", "fsdp"), axis=0, tiled=True),
        lax.all_gather(norm_gain, ("dp", "fsdp"), axis=0, tiled=True),
        lax.all_gather(norm_shift, ("dp", "fsdp"), axis=0, tiled=True),
    )
    ffn_params = (
        lax.all_gather(inner_weight, ("dp", "fsdp"), axis=0, tiled=True),
        lax.all_gather(outer_weight, ("dp", "fsdp"), axis=0, tiled=True),
        lax.all_gather(inner_bias, ("dp", "fsdp"), axis=0, tiled=True),
        lax.all_gather(outer_bias, ("dp", "fsdp"), axis=0, tiled=True),
        lax.all_gather(final_gain, ("dp", "fsdp"), axis=0, tiled=True),
        lax.all_gather(final_shift, ("dp", "fsdp"), axis=0, tiled=True),
    )
    w_query, w_key, w_value, w_output, b_query, b_value, b_output, gain_one, shift_one = attn_params
    w_inner, w_outer, b_inner, b_outer, gain_two, shift_two = ffn_params
    flat_tokens = local_tokens.reshape(token_count, model_width)
    query_rows = (dense(flat_tokens, w_query) + b_query).astype(jnp.bfloat16)
    key_rows = dense(flat_tokens, w_key).astype(jnp.bfloat16)
    value_rows = (dense(flat_tokens, w_value) + b_value).astype(jnp.bfloat16)
    query_heads = query_rows.reshape(slot_count, row_count, head_count, head_dim)
    key_slots = key_rows.reshape(slot_count, row_count, model_width)
    value_slots = value_rows.reshape(slot_count, row_count, model_width)
    start_state = (
        jnp.full((slot_count, head_count, row_count), masked_score, jnp.float32),
        jnp.zeros((slot_count, head_count, row_count), jnp.float32),
        jnp.zeros((slot_count, row_count, head_count, head_dim), jnp.float32),
    )
    row_max, denominator, numerator = attend_forward(
        query_heads,
        seq_lens,
        score_scale,
        start_state,
        (
            lax.all_gather(key_slots, "fsdp", axis=1, tiled=True),
            lax.all_gather(value_slots, "fsdp", axis=1, tiled=True),
        ),
    )
    attn_float = numerator / jnp.transpose(denominator, (0, 2, 1))[..., None]
    log_total = row_max + jnp.log(denominator)
    attn_rows = attn_float.reshape(token_count, model_width).astype(jnp.bfloat16)
    resid_one = flat_tokens.astype(jnp.float32) + dense(attn_rows, w_output) + b_output
    normed_one, norm_one_back = jax.vjp(
        layer_norm, resid_one, gain_one.astype(jnp.float32), shift_one.astype(jnp.float32)
    )
    hidden_rows = normed_one.astype(jnp.bfloat16)
    inner_rows = dense(hidden_rows, w_inner) + b_inner
    act_float, act_back = jax.vjp(partial(jax.nn.gelu, approximate=False), inner_rows)
    act_rows = act_float.astype(jnp.bfloat16)
    resid_two = hidden_rows.astype(jnp.float32) + dense(act_rows, w_outer) + b_outer
    final_rows, norm_two_back = jax.vjp(
        layer_norm, resid_two, gain_two.astype(jnp.float32), shift_two.astype(jnp.float32)
    )
    positions = lax.axis_index("fsdp") * row_count + lax.iota(jnp.int32, row_count)
    valid_rows = (
        (positions[None, :] < seq_lens[:, None]).astype(jnp.float32).reshape(token_count, 1)
    )
    loss_scale = seq_total * seq_len / jnp.sum(lengths).astype(jnp.float32)
    grad_final = (
        loss_scale
        * (final_rows - teacher.reshape(token_count, model_width).astype(jnp.float32))
        * valid_rows
    )
    d_two, grad_gain_two, grad_shift_two = norm_two_back(grad_final)
    attn_params = (
        lax.all_gather(query_weight, ("dp", "fsdp"), axis=0, tiled=True),
        lax.all_gather(key_weight, ("dp", "fsdp"), axis=0, tiled=True),
        lax.all_gather(value_weight, ("dp", "fsdp"), axis=0, tiled=True),
        lax.all_gather(output_weight, ("dp", "fsdp"), axis=0, tiled=True),
        lax.all_gather(query_bias, ("dp", "fsdp"), axis=0, tiled=True),
        lax.all_gather(value_bias, ("dp", "fsdp"), axis=0, tiled=True),
        lax.all_gather(output_bias, ("dp", "fsdp"), axis=0, tiled=True),
        lax.all_gather(norm_gain, ("dp", "fsdp"), axis=0, tiled=True),
        lax.all_gather(norm_shift, ("dp", "fsdp"), axis=0, tiled=True),
    )
    ffn_params = (
        lax.all_gather(inner_weight, ("dp", "fsdp"), axis=0, tiled=True),
        lax.all_gather(outer_weight, ("dp", "fsdp"), axis=0, tiled=True),
        lax.all_gather(inner_bias, ("dp", "fsdp"), axis=0, tiled=True),
        lax.all_gather(outer_bias, ("dp", "fsdp"), axis=0, tiled=True),
        lax.all_gather(final_gain, ("dp", "fsdp"), axis=0, tiled=True),
        lax.all_gather(final_shift, ("dp", "fsdp"), axis=0, tiled=True),
    )
    w_query, w_key, w_value, w_output, b_query, b_value, b_output, gain_one, shift_one = attn_params
    w_inner, w_outer, b_inner, b_outer, gain_two, shift_two = ffn_params
    d_out = d_two.astype(jnp.bfloat16)
    grad_outer = across_rows(act_rows, d_out)
    grad_outer_bias = jnp.sum(d_out.astype(jnp.float32), axis=0)
    d_act = across_cols(d_out, w_outer)
    (d_inner_float,) = act_back(d_act)
    d_inner = d_inner_float.astype(jnp.bfloat16)
    grad_inner = across_rows(hidden_rows, d_inner)
    grad_inner_bias = jnp.sum(d_inner.astype(jnp.float32), axis=0)
    d_hidden = d_two + across_cols(d_inner, w_inner)
    d_one, grad_gain_one, grad_shift_one = norm_one_back(d_hidden)
    d_mix = d_one.astype(jnp.bfloat16)
    grad_output = across_rows(attn_rows, d_mix)
    grad_output_bias = jnp.sum(d_mix.astype(jnp.float32), axis=0)
    d_attn = across_cols(d_mix, w_output).astype(jnp.bfloat16)
    grad_heads = d_attn.reshape(slot_count, row_count, head_count, head_dim)
    delta = jnp.einsum("srhd,srhd->shr", grad_heads.astype(jnp.float32), attn_float)
    query_state = jnp.zeros((slot_count, row_count, head_count, head_dim), jnp.float32)
    grad_query = attend_query_back(
        query_heads,
        grad_heads,
        log_total,
        delta,
        seq_lens,
        score_scale,
        query_state,
        (
            lax.all_gather(key_slots, "fsdp", axis=1, tiled=True),
            lax.all_gather(value_slots, "fsdp", axis=1, tiled=True),
        ),
    )
    stats_whole = (
        lax.all_gather(jnp.transpose(log_total, (0, 2, 1)), "fsdp", axis=1, tiled=True),
        lax.all_gather(jnp.transpose(delta, (0, 2, 1)), "fsdp", axis=1, tiled=True),
    )
    key_alive = (positions[None, :] < seq_lens[:, None])[:, None, None, :]
    key_heads = key_slots.reshape(slot_count, row_count, head_count, head_dim)
    value_heads = value_slots.reshape(slot_count, row_count, head_count, head_dim)
    key_state = (
        jnp.zeros((slot_count, row_count, head_count, head_dim), jnp.float32),
        jnp.zeros((slot_count, row_count, head_count, head_dim), jnp.float32),
    )
    grad_keys, grad_values = attend_key_back(
        key_heads,
        value_heads,
        key_alive,
        stats_whole,
        score_scale,
        key_state,
        (
            lax.all_gather(query_heads, "fsdp", axis=1, tiled=True),
            lax.all_gather(grad_heads, "fsdp", axis=1, tiled=True),
        ),
    )
    d_query = grad_query.reshape(token_count, model_width).astype(jnp.bfloat16)
    d_key = grad_keys.reshape(token_count, model_width).astype(jnp.bfloat16)
    d_value = grad_values.reshape(token_count, model_width).astype(jnp.bfloat16)
    grad_wq = across_rows(flat_tokens, d_query)
    grad_wk = across_rows(flat_tokens, d_key)
    grad_wv = across_rows(flat_tokens, d_value)
    grad_query_bias = jnp.sum(d_query.astype(jnp.float32), axis=0)
    grad_value_bias = jnp.sum(d_value.astype(jnp.float32), axis=0)
    grad_input = (
        d_one
        + across_cols(d_query, w_query)
        + across_cols(d_key, w_key)
        + across_cols(d_value, w_value)
    )
    attn_grads = (
        lax.psum_scatter(grad_wq, ("dp", "fsdp"), scatter_dimension=0, tiled=True),
        lax.psum_scatter(grad_wk, ("dp", "fsdp"), scatter_dimension=0, tiled=True),
        lax.psum_scatter(grad_wv, ("dp", "fsdp"), scatter_dimension=0, tiled=True),
        lax.psum_scatter(grad_output, ("dp", "fsdp"), scatter_dimension=0, tiled=True),
        lax.psum_scatter(grad_query_bias, ("dp", "fsdp"), scatter_dimension=0, tiled=True),
        lax.psum_scatter(grad_value_bias, ("dp", "fsdp"), scatter_dimension=0, tiled=True),
        lax.psum_scatter(grad_output_bias, ("dp", "fsdp"), scatter_dimension=0, tiled=True),
        lax.psum_scatter(grad_gain_one, ("dp", "fsdp"), scatter_dimension=0, tiled=True),
        lax.psum_scatter(grad_shift_one, ("dp", "fsdp"), scatter_dimension=0, tiled=True),
    )
    ffn_grads = (
        lax.psum_scatter(grad_inner, ("dp", "fsdp"), scatter_dimension=0, tiled=True),
        lax.psum_scatter(grad_outer, ("dp", "fsdp"), scatter_dimension=0, tiled=True),
        lax.psum_scatter(grad_inner_bias, ("dp", "fsdp"), scatter_dimension=0, tiled=True),
        lax.psum_scatter(grad_outer_bias, ("dp", "fsdp"), scatter_dimension=0, tiled=True),
        lax.psum_scatter(grad_gain_two, ("dp", "fsdp"), scatter_dimension=0, tiled=True),
        lax.psum_scatter(grad_shift_two, ("dp", "fsdp"), scatter_dimension=0, tiled=True),
    )
    out_rows = final_rows.astype(jnp.bfloat16).reshape(slot_count, row_count, model_width)
    grad_rows = grad_input.astype(jnp.bfloat16).reshape(slot_count, row_count, model_width)
    sent_out, sent_grad = (
        lax.all_to_all(out_rows, "dp", split_axis=1, concat_axis=0, tiled=True),
        lax.all_to_all(grad_rows, "dp", split_axis=1, concat_axis=0, tiled=True),
    )
    slot_ids = lax.iota(jnp.int32, seq_total)
    inverse = jnp.sum(
        jnp.where(dealing[None, :] == slot_ids[:, None], slot_ids[None, :], 0), axis=1
    )
    sent_out = jnp.take(sent_out, inverse, axis=0)
    sent_grad = jnp.take(sent_grad, inverse, axis=0)
    output_given, grad_given = (
        lax.all_to_all(sent_out, "dp", split_axis=0, concat_axis=1, tiled=True),
        lax.all_to_all(sent_grad, "dp", split_axis=0, concat_axis=1, tiled=True),
    )
    return (
        output_given,
        grad_given,
        attn_grads[0],
        attn_grads[1],
        attn_grads[2],
        attn_grads[3],
        ffn_grads[0],
        ffn_grads[1],
        attn_grads[4],
        attn_grads[5],
        attn_grads[6],
        attn_grads[7],
        attn_grads[8],
        ffn_grads[2],
        ffn_grads[3],
        ffn_grads[4],
        ffn_grads[5],
    )


def solution(mesh):
    placed = (
        P("dp", "fsdp", None),
        P("dp", "fsdp", None),
        P(),
        P(),
        P(("dp", "fsdp"), None),
        P(("dp", "fsdp"), None),
        P(("dp", "fsdp"), None),
        P(("dp", "fsdp"), None),
        P(("dp", "fsdp"), None),
        P(("dp", "fsdp"), None),
        P(("dp", "fsdp")),
        P(("dp", "fsdp")),
        P(("dp", "fsdp")),
        P(("dp", "fsdp")),
        P(("dp", "fsdp")),
        P(("dp", "fsdp")),
        P(("dp", "fsdp")),
        P(("dp", "fsdp")),
        P(("dp", "fsdp")),
    )
    return jax.shard_map(
        shards,
        mesh=mesh,
        in_specs=placed,
        out_specs=(
            P("dp", "fsdp", None),
            P("dp", "fsdp", None),
            P(("dp", "fsdp"), None),
            P(("dp", "fsdp"), None),
            P(("dp", "fsdp"), None),
            P(("dp", "fsdp"), None),
            P(("dp", "fsdp"), None),
            P(("dp", "fsdp"), None),
            P(("dp", "fsdp")),
            P(("dp", "fsdp")),
            P(("dp", "fsdp")),
            P(("dp", "fsdp")),
            P(("dp", "fsdp")),
            P(("dp", "fsdp")),
            P(("dp", "fsdp")),
            P(("dp", "fsdp")),
            P(("dp", "fsdp")),
        ),
        check_vma=False,
    )
```

profile of v0, /device:TPU:0, one launch (start us, length us, event | category | flops | bytes accessed | tf_op | source)
XLA Modules:
  0.0 1456.8 jit_solution(9602848840725132645)
XLA Ops:
  12.1 7.3 all-to-all-start
  20.8 37.7 %all-to-all-done = bf16[2,512,768]{2,0,1:T(2,128)(2,1)S(1)} async-done(((bf16[2,512,768]{2,0,1:T(2,128)(2,1)}), bf16[2,512,768]{2,0,1:T(2,128)(2,1)S(1)}, u32[]{:S(2)}, u32[]{:S(2)}) %all-to-all-start) | async-done | bytes 1572896 | tf_op jit(solution)/shard_map/all_to_all | solution.py:193
  67.5 57.7 %all-reduce.19 = (bf16[768]{0:T(1024)(128)(2,1)S(1)}, bf16[768]{0:T(1024)(128)(2,1)S(1)}, bf16[768]{0:T(1024)(128)(2,1)S(1)}, bf16[768]{0:T(1024)(128)(2,1)S(1)}...) all-reduce(bf16[768]{0:T(1024)(128)(2,1)S(1)} %dynamic-update-slice, ...), channel_id=1, replica_groups=mesh['dp'=8,'fsdp'=4] {'dp','fsdp'}, use_global_device_ids=true, to_apply=%add | all-reduce | flops 9216 | bytes 36864
  130.4 18.5 %all-gather.11.cloned.1.call-done = bf16[768,768]{1,0:T(8,128)(2,1)} async-done(((bf16[24,768]{1,0:T(8,128)(2,1)}), bf16[768,768]{1,0:T(8,128)(2,1)}) %all-gather.11.cloned.1.call-update) | async-done | bytes 1179664 | tf_op jit(solution)/shard_map/all_gather | solution.py:200
  162.1 42.8 %all-gather.15.cloned.1.call-done = bf16[768,768]{1,0:T(8,128)(2,1)} async-done(((bf16[24,768]{1,0:T(8,128)(2,1)}), bf16[768,768]{1,0:T(8,128)(2,1)}) %all-gather.15.cloned.1.call-update) | async-done | bytes 1179664 | tf_op jit(solution)/shard_map/all_gather | solution.py:199
  213.4 38.3 %all-gather.19.cloned.1.call-done = bf16[2,2048,768]{1,2,0:T(8,128)(2,1)} async-done(((bf16[2,512,768]{1,2,0:T(8,128)(2,1)}), bf16[2,2048,768]{1,2,0:T(8,128)(2,1)}) %all-gather.19.cloned.1.call-update) | async-done | bytes 6291472 | tf_op jit(solution)/shard_map/all_gather | solution.py:238
  251.7 47.8 %all-gather.13.cloned.1.call-done = bf16[2,2048,768]{1,2,0:T(8,128)(2,1)} async-done(((bf16[2,512,768]{1,2,0:T(8,128)(2,1)}), bf16[2,2048,768]{1,2,0:T(8,128)(2,1)}) %all-gather.13.cloned.1.call-update) | async-done | bytes 6291472 | tf_op jit(solution)/shard_map/all_gather | solution.py:237
  299.5 157.5 %while.48 = (s32[]{:T(128)}, f32[2,12,512]{2,1,0:T(8,128)S(1)}, f32[2,12,512]{2,1,0:T(8,128)S(1)}, f32[2,512,12,64]{1,3,2,0:T(8,128)}, s32[2]{0:T(128)S(1)}, /*i...) while((s32[]{:T(128)}, f32[2,12,512]{2,1,0:T(8,128)S(1)}, ...), condition=%wide.region_3.5_spmd.clone, body=%wide.region_0.4_spmd.clone.sunk | while | flops 1694836224 | bytes 93593784 | solution.py:78
  301.8 11.2 bitcast_reduce_fusion.2
  313.0 13.2 bitcast_add_fusion.8
  326.3 11.8 fusion.141
  340.3 11.2 bitcast_reduce_fusion.2
  351.6 14.2 bitcast_add_fusion.8
  365.8 11.8 fusion.141
  379.9 11.2 bitcast_reduce_fusion.2
  391.2 14.2 bitcast_add_fusion.8
  405.3 11.9 fusion.141
  419.5 11.2 bitcast_reduce_fusion.2
  430.7 14.3 bitcast_add_fusion.8
  444.9 11.8 fusion.141
  468.0 36.3 %multiply_convert_fusion.8 = (bf16[1024,3072]{1,0:T(8,128)(2,1)}, f32[1024,3072]{1,0:T(8,128)}, f32[1024,3072]{1,0:T(8,128)}) fusion(f32[3072]{0:T(1024)S(1)} %copy-done.54, bf16[768,3072]{1,0:T(8,128)(2,1)} %all-gather.23.cloned.1.call-done, f32[1024,768]{1,0:T(8,128)S(1)} %get-tuple-element.829, f32[768]{0:T(1024)S(1)} %copy-done.42, ...), kind=kOutput, calls=%fused_computation.68 | convolution fusion | flops 5043388416 | bytes 39348224 | tf_op jit(solution)/shard_map/dot_general | solution.py:24
  504.3 8.9 fusion.61
  523.0 18.7 %convert_reduce_fusion = (f32[3072]{0:T(1024)}, bf16[1024,3072]{1,0:T(8,128)(2,1)}) fusion(f32[1024,3072]{1,0:T(8,128)} %get-tuple-element.812, bf16[1024,768]{1,0:T(8,128)(2,1)} %get-tuple-element.800, bf16[3072,768]{1,0:T(8,128)(2,1)} %all-gather.25.cloned.1.call-done, f32[1024,3072]{1,0:T(8,128)} %get-tuple-element.830, f32[3072]{0:T(1024)S(1)} %copy-done.54), kind=kOutput, calls=%fused_computation.66 | convolution fusion | flops 4885312512 | bytes 37773312 | tf_op jit(solution)/shard_map/dot_general | solution.py:34
  541.7 10.1 multiply_reduce_fusion.2
  568.2 121.8 %while.49 = (s32[]{:T(128)}, f32[2,512,12,64]{1,3,2,0:T(8,128)}, bf16[2,2048,768]{1,2,0:T(8,128)(2,1)}, s32[2]{0:T(128)S(1)}, bf16[2,512,12,64]{1,3,2,0:T(8,128)...) while((s32[]{:T(128)}, f32[2,512,12,64]{1,3,2,0:T(8,128)}, ...), condition=%wide.region_15.17_spmd.clone, body=%wide.region_14.16_spmd.clone.sunk | while | flops 2456028672 | bytes 70883520 | solution.py:115
  571.6 11.7 fusion.148
  583.3 16.2 %bitcast_add_fusion.9 = f32[2,512,12,64]{1,3,2,0:T(8,128)} fusion(f32[2,512,12,64]{1,3,2,0:T(8,128)} %get-tuple-element.1126, bf16[2,512,12,64]{1,3,2,0:T(8,128)(2,1)S(1)} %bitcast.200, f32[2,12,512,512]{3,2,1,0:T(8,128)} %fusion.148, f32[2,12,512]{2,1,0:T(8,128)S(1)} %get-tuple-element.1146, f32[2,12,512]{2,1,0:T(8,128)S(1)} %get-tuple-element.1143, ...), kind=kOutput, calls=%fused_computation.33.clone.1 | convolution fusion | flops 1650720768 | bytes 36275200 | tf_op jit(solution)/shard_map/while/body/eval_jaxpr/shrn,snhd->srhd/dot_general | solution.py:109
  602.8 10.1 fusion.148
  613.1 16.7 %bitcast_add_fusion.9 = f32[2,512,12,64]{1,3,2,0:T(8,128)} fusion(f32[2,512,12,64]{1,3,2,0:T(8,128)} %get-tuple-element.1126, bf16[2,512,12,64]{1,3,2,0:T(8,128)(2,1)S(1)} %bitcast.200, f32[2,12,512,512]{3,2,1,0:T(8,128)} %fusion.148, f32[2,12,512]{2,1,0:T(8,128)S(1)} %get-tuple-element.1146, f32[2,12,512]{2,1,0:T(8,128)S(1)} %get-tuple-element.1143, ...), kind=kOutput, calls=%fused_computation.33.clone.1 | convolution fusion | flops 1650720768 | bytes 36275200 | tf_op jit(solution)/shard_map/while/body/eval_jaxpr/shrn,snhd->srhd/dot_general | solution.py:109
  633.2 10.1 fusion.148
  643.4 16.5 %bitcast_add_fusion.9 = f32[2,512,12,64]{1,3,2,0:T(8,128)} fusion(f32[2,512,12,64]{1,3,2,0:T(8,128)} %get-tuple-element.1126, bf16[2,512,12,64]{1,3,2,0:T(8,128)(2,1)S(1)} %bitcast.200, f32[2,12,512,512]{3,2,1,0:T(8,128)} %fusion.148, f32[2,12,512]{2,1,0:T(8,128)S(1)} %get-tuple-element.1146, f32[2,12,512]{2,1,0:T(8,128)S(1)} %get-tuple-element.1143, ...), kind=kOutput, calls=%fused_computation.33.clone.1 | convolution fusion | flops 1650720768 | bytes 36275200 | tf_op jit(solution)/shard_map/while/body/eval_jaxpr/shrn,snhd->srhd/dot_general | solution.py:109
  663.2 10.1 fusion.148
  673.4 16.5 %bitcast_add_fusion.9 = f32[2,512,12,64]{1,3,2,0:T(8,128)} fusion(f32[2,512,12,64]{1,3,2,0:T(8,128)} %get-tuple-element.1126, bf16[2,512,12,64]{1,3,2,0:T(8,128)(2,1)S(1)} %bitcast.200, f32[2,12,512,512]{3,2,1,0:T(8,128)} %fusion.148, f32[2,12,512]{2,1,0:T(8,128)S(1)} %get-tuple-element.1146, f32[2,12,512]{2,1,0:T(8,128)S(1)} %get-tuple-element.1143, ...), kind=kOutput, calls=%fused_computation.33.clone.1 | convolution fusion | flops 1650720768 | bytes 36275200 | tf_op jit(solution)/shard_map/while/body/eval_jaxpr/shrn,snhd->srhd/dot_general | solution.py:109
  698.9 4.8 fusion.69
  703.8 10.9 fusion.62
  729.9 5.9 all-to-all-start.2
  735.9 5.8 all_gather.91
  741.7 6.3 all_gather.89
  748.1 10.2 fusion.70
  759.6 4.4 fusion.64
  764.1 192.7 %while.50 = (s32[]{:T(128)}, f32[2,512,12,64]{1,3,2,0:T(8,128)}, f32[2,512,12,64]{1,3,2,0:T(8,128)}, bf16[2,2048,12,64]{1,0,3,2:T(2,128)(2,1)}, bf16[2,512,12,64...) while((s32[]{:T(128)}, f32[2,512,12,64]{1,3,2,0:T(8,128)}, ...), condition=%wide.region_17.19_spmd.clone, body=%wide.region_16.18_spmd.clone.sunk | while | flops 3288073216 | bytes 104158416 | solution.py:161
  764.5 6.1 constant_dynamic-slice_fusion.11
  770.6 10.3 fusion.156
  781.9 13.2 bitcast_add_fusion.11
  795.0 16.0 %bitcast_add_fusion.10 = f32[2,512,12,64]{1,3,2,0:T(8,128)} fusion(f32[2,512,12,64]{1,3,2,0:T(8,128)} %get-tuple-element.1083, f32[2,12,512,512]{3,2,1,0:T(8,128)} %fusion.156, f32[2,12,512]{2,1,0:T(8,128)S(1)} %get-tuple-element.1028, f32[2,12,512]{2,1,0:T(8,128)S(1)} %get-tuple-element.1029, pred[2,512]{1,0:T(4,128)(4,1)S(1)} %compare_bitcast_fusion.2, ...), kind=kOutput, calls=%fused_computation.49.clone.1 | convolution fusion | flops 1650720768 | bytes 36275200 | tf_op jit(solution)/shard_map/while/body/eval_jaxpr/shrn,srhd->snhd/dot_general | solution.py:148
  811.0 6.1 constant_dynamic-slice_fusion.11
  817.0 10.4 fusion.156
  828.4 14.3 bitcast_add_fusion.11
  842.7 16.5 %bitcast_add_fusion.10 = f32[2,512,12,64]{1,3,2,0:T(8,128)} fusion(f32[2,512,12,64]{1,3,2,0:T(8,128)} %get-tuple-element.1083, f32[2,12,512,512]{3,2,1,0:T(8,128)} %fusion.156, f32[2,12,512]{2,1,0:T(8,128)S(1)} %get-tuple-element.1028, f32[2,12,512]{2,1,0:T(8,128)S(1)} %get-tuple-element.1029, pred[2,512]{1,0:T(4,128)(4,1)S(1)} %compare_bitcast_fusion.2, ...), kind=kOutput, calls=%fused_computation.49.clone.1 | convolution fusion | flops 1650720768 | bytes 36275200 | tf_op jit(solution)/shard_map/while/body/eval_jaxpr/shrn,srhd->snhd/dot_general | solution.py:148
  859.2 6.1 constant_dynamic-slice_fusion.11
  865.2 10.4 fusion.156
  876.5 14.1 bitcast_add_fusion.11
  890.6 16.4 %bitcast_add_fusion.10 = f32[2,512,12,64]{1,3,2,0:T(8,128)} fusion(f32[2,512,12,64]{1,3,2,0:T(8,128)} %get-tuple-element.1083, f32[2,12,512,512]{3,2,1,0:T(8,128)} %fusion.156, f32[2,12,512]{2,1,0:T(8,128)S(1)} %get-tuple-element.1028, f32[2,12,512]{2,1,0:T(8,128)S(1)} %get-tuple-element.1029, pred[2,512]{1,0:T(4,128)(4,1)S(1)} %compare_bitcast_fusion.2, ...), kind=kOutput, calls=%fused_computation.49.clone.1 | convolution fusion | flops 1650720768 | bytes 36275200 | tf_op jit(solution)/shard_map/while/body/eval_jaxpr/shrn,srhd->snhd/dot_general | solution.py:148
  907.0 6.1 constant_dynamic-slice_fusion.11
  913.1 10.2 fusion.156
  924.2 15.2 %bitcast_add_fusion.11 = f32[2,512,12,64]{1,3,2,0:T(8,128)} fusion(f32[2,512,12,64]{1,3,2,0:T(8,128)} %get-tuple-element.1084, f32[2,12,512,512]{3,2,1,0:T(8,128)} %fusion.156, f32[2,12,512]{2,1,0:T(8,128)S(1)} %get-tuple-element.1029, pred[2,512]{1,0:T(4,128)(4,1)S(1)} %compare_bitcast_fusion.2, pred[]{:T(512)S(6)} %compare.11, ...), kind=kOutput, calls=%fused_computation.48.clone.1 | convolution fusion | flops 832045056 | bytes 33080320 | tf_op jit(solution)/shard_map/while/body/eval_jaxpr/shrn,srhd->snhd/dot_general | solution.py:153
  939.3 17.4 %bitcast_add_fusion.10 = f32[2,512,12,64]{1,3,2,0:T(8,128)} fusion(f32[2,512,12,64]{1,3,2,0:T(8,128)} %get-tuple-element.1083, f32[2,12,512,512]{3,2,1,0:T(8,128)} %fusion.156, f32[2,12,512]{2,1,0:T(8,128)S(1)} %get-tuple-element.1028, f32[2,12,512]{2,1,0:T(8,128)S(1)} %get-tuple-element.1029, pred[2,512]{1,0:T(4,128)(4,1)S(1)} %compare_bitcast_fusion.2, ...), kind=kOutput, calls=%fused_computation.49.clone.1 | convolution fusion | flops 1650720768 | bytes 36275200 | tf_op jit(solution)/shard_map/while/body/eval_jaxpr/shrn,srhd->snhd/dot_general | solution.py:148
  971.5 5.9 all-to-all-start.4
  985.7 47.4 %all-to-all-done.4 = bf16[2,512,768]{2,0,1:T(2,128)(2,1)S(1)} async-done(((bf16[2,512,768]{2,0,1:T(2,128)(2,1)}), bf16[2,512,768]{2,0,1:T(2,128)(2,1)S(1)}, u32[]{:S(2)}, u32[]{:S(2)}) %all-to-all-start.4) | async-done | bytes 1572896 | tf_op jit(solution)/shard_map/all_to_all | solution.py:378
  1046.9 49.9 %all-to-all-done.3 = bf16[16,64,768]{2,1,0:T(8,128)(2,1)S(1)} async-done(((bf16[16,64,768]{2,1,0:T(8,128)(2,1)}), bf16[16,64,768]{2,1,0:T(8,128)(2,1)S(1)}, u32[]{:S(2)}, u32[]{:S(2)}) %all-to-all-start.3) | async-done | bytes 1572896 | tf_op jit(solution)/shard_map/all_to_all | solution.py:387
  1100.6 57.6 %all-reduce.18 = (f32[768]{0:T(1024)S(1)}, f32[768]{0:T(1024)S(1)}, f32[768]{0:T(1024)S(1)}, f32[768]{0:T(1024)S(1)}, f32[768]{0:T(1024)S(1)}, /*index=5*/f32[30...) all-reduce(f32[768]{0:T(1024)S(1)} %reduce_sum.231, ...), channel_id=8, replica_groups=mesh['dp'=8,'fsdp'=4] {'dp','fsdp'}, use_global_device_ids=true, to_apply=%region_25.27.clone | all-reduce | flops 9216 | bytes 73728
  1166.0 75.8 %reduce-scatter.17.cloned.1.call-done = f32[96,768]{1,0:T(8,128)} async-done(((f32[3072,768]{1,0:T(8,128)}), f32[96,768]{1,0:T(8,128)}) %reduce-scatter.17.cloned.1.call-update) | async-done | bytes 294928 | tf_op jit(solution)/shard_map/reduce_scatter | solution.py:368
  1241.8 103.7 %reduce-scatter.11.cloned.1.call-done = f32[24,768]{1,0:T(8,128)} async-done(((f32[768,768]{1,0:T(8,128)}), f32[24,768]{1,0:T(8,128)}) %reduce-scatter.11.cloned.1.call-update) | async-done | bytes 73744 | tf_op jit(solution)/shard_map/reduce_scatter | solution.py:358
  1345.5 104.6 %reduce-scatter.9.cloned.1.call-done = f32[24,768]{1,0:T(8,128)} async-done(((f32[768,768]{1,0:T(8,128)}), f32[24,768]{1,0:T(8,128)}) %reduce-scatter.9.cloned.1.call-update) | async-done | bytes 73744 | tf_op jit(solution)/shard_map/reduce_scatter | solution.py:357
  (365 shorter events, 177.9 us)
Async XLA Ops:
  7.2 118.3 %all-gather.17.cloned.1.call-start = ((), (), s32[]{:S(2)}) async-start(), calls=%async_computation.15 | async-start | bytes 1216512 | tf_op jit(solution)/shard_map/all_gather | solution.py:201
  7.9 12.2 copy-start.60
  7.9 12.2 copy-start
  12.1 46.4 %all-to-all-start = ((bf16[2,512,768]{2,0,1:T(2,128)(2,1)}), bf16[2,512,768]{2,0,1:T(2,128)(2,1)S(1)}, u32[]{:S(2)}, u32[]{:S(2)}) async-start(bf16[2,512,768]{2,0,1:T(2,128)(2,1)} %copy.117), calls=%async_computation | async-start | bytes 3145728 | tf_op jit(solution)/shard_map/all_to_all | solution.py:193
  19.4 129.6 %all-gather.11.cloned.1.call-start = ((), (), s32[]{:S(2)}) async-start(), calls=%async_computation.12 | async-start | bytes 1216512 | tf_op jit(solution)/shard_map/all_gather | solution.py:200
  59.5 5.9 copy-start.64
  59.5 6.1 copy-start.65
  59.5 6.4 copy-start.66
  59.5 6.6 copy-start.67
  59.5 6.8 copy-start.68
  59.5 7.0 copy-start.69
  59.6 7.3 copy-start.70
  59.6 7.5 copy-start.71
  59.6 7.7 copy-start.72
  61.0 64.3 %all-to-all-start.1 = ((bf16[16,64,768]{2,1,0:T(8,128)(2,1)}), bf16[16,64,768]{2,1,0:T(8,128)(2,1)S(1)}, u32[]{:S(2)}, u32[]{:S(2)}) async-start(bf16[16,64,768]{2,1,0:T(8,128)(2,1)} %broadcast_select_fusion.2), calls=%async_computation.1 | async-start | bytes 3145728 | tf_op jit(solution)/shard_map/all_to_all | solution.py:195
  64.6 140.3 %all-gather.15.cloned.1.call-start = ((), (), s32[]{:S(2)}) async-start(), calls=%async_computation.14 | async-start | bytes 1216512 | tf_op jit(solution)/shard_map/all_gather | solution.py:199
  65.3 186.4 %all-gather.19.cloned.1.call-start = ((), (), s32[]{:S(2)}) async-start(), calls=%async_computation.16 | async-start | bytes 7864320 | tf_op jit(solution)/shard_map/all_gather | solution.py:238
  128.7 23.4 %copy-start.13 = (bf16[1024,768]{1,0:T(8,128)(2,1)}, bf16[1024,768]{1,0:T(8,128)(2,1)S(1)}, u32[]{:S(2)}) copy-start(bf16[1024,768]{1,0:T(8,128)(2,1)S(1)} %add_convert_fusion.3) | copy-start | bytes 4718596
  130.4 169.1 %all-gather.13.cloned.1.call-start = ((), (), s32[]{:S(2)}) async-start(), calls=%async_computation.13 | async-start | bytes 7864320 | tf_op jit(solution)/shard_map/all_gather | solution.py:237
  152.1 52.8 %copy-start.24 = (bf16[2,8,64,768]{3,2,1,0:T(8,128)(2,1)S(1)}, bf16[2,8,64,768]{3,2,1,0:T(8,128)(2,1)}, u32[]{:S(2)}) copy-start(bf16[2,8,64,768]{3,2,1,0:T(8,128)(2,1)} %copy-done.23) | copy-start | bytes 4718596
  153.7 309.6 %all-gather.21.cloned.1.call-start = ((), (), s32[]{:S(2)}) async-start(), calls=%async_computation.17 | async-start | bytes 1216512 | tf_op jit(solution)/shard_map/all_gather | solution.py:202
  154.3 313.4 %all-gather.23.cloned.1.call-start = ((), (), s32[]{:S(2)}) async-start(), calls=%async_computation.18 | async-start | bytes 4866048 | tf_op jit(solution)/shard_map/all_gather | solution.py:210
  155.1 349.2 %all-gather.25.cloned.1.call-start = ((), (), s32[]{:S(2)}) async-start(), calls=%async_computation.19 | async-start | bytes 4866048 | tf_op jit(solution)/shard_map/all_gather | solution.py:211
  155.8 608.3 %all-gather.27.cloned.1.call-start = ((), (), s32[]{:S(2)}) async-start(), calls=%async_computation.20 | async-start | bytes 7864320 | tf_op jit(solution)/shard_map/all_gather | solution.py:337
  160.8 48.0 %copy-start.40 = (s32[512]{0:T(512)}, s32[512]{0:T(512)S(1)}, u32[]{:S(2)}) copy-start(s32[512]{0:T(512)S(1)} %iota_add_fusion.2) | copy-start | bytes 6148
  212.8 551.3 %all-gather.29.cloned.1.call-start = ((), (), s32[]{:S(2)}) async-start(), calls=%async_computation.21 | async-start | bytes 7864320 | tf_op jit(solution)/shard_map/all_gather | solution.py:338
  457.0 4.6 copy-start.1
  457.0 4.6 copy-start.10
  457.0 4.6 copy-start.19
  457.0 4.6 copy-start.37
  467.1 84.7 %copy-start.3 = (f32[1024,768]{1,0:T(8,128)}, f32[1024,768]{1,0:T(8,128)S(1)}, u32[]{:S(2)}) copy-start(f32[1024,768]{1,0:T(8,128)S(1)} %get-tuple-element.829) | copy-start | bytes 9437188
  467.7 36.6 %copy-start.56 = (f32[768]{0:T(1024)S(1)}, f32[768]{0:T(1024)}, u32[]{:S(2)}) copy-start(f32[768]{0:T(1024)} %convert_element_type.175) | copy-start | bytes 9220
  553.3 5.1 copy-start.44
  560.1 4.8 copy-start.11
  560.1 4.8 copy-start.20
  567.7 598.2 %reduce-scatter.7.cloned.1.call-start = ((), (), s32[]{:S(2)}) async-start(), calls=%async_computation.22 | async-start | bytes 2433024 | tf_op jit(solution)/shard_map/reduce_scatter | solution.py:356
  689.9 4.4 copy-start.33
  689.9 4.4 copy-start.35
  698.8 5.0 copy-start.4
  698.8 5.0 copy-start.43
  698.8 467.1 %reduce-scatter.13.cloned.1.call-start = ((), (), s32[]{:S(2)}) async-start(), calls=%async_computation.25 | async-start | bytes 2433024 | tf_op jit(solution)/shard_map/reduce_scatter | solution.py:359
  703.7 462.2 %reduce-scatter.15.cloned.1.call-start = ((), (), s32[]{:S(2)}) async-start(), calls=%async_computation.26 | async-start | bytes 9732096 | tf_op jit(solution)/shard_map/reduce_scatter | solution.py:367
  722.9 4.1 copy-start.17
  727.1 8.9 copy-start.34
  727.1 14.6 %copy-start.36 = (f32[2,12,512]{2,1,0:T(8,128)S(1)}, f32[2,12,512]{2,1,0:T(8,128)}, u32[]{:S(2)}) copy-start(f32[2,12,512]{2,1,0:T(8,128)} %copy-done.35) | copy-start | bytes 147460
  729.9 18.1 %copy-start.30 = (bf16[1024,768]{1,0:T(8,128)(2,1)S(1)}, bf16[1024,768]{1,0:T(8,128)(2,1)}, u32[]{:S(2)}) copy-start(bf16[1024,768]{1,0:T(8,128)(2,1)} %get-tuple-element.800) | copy-start | bytes 4718596
  729.9 241.5 %all-to-all-start.2 = ((bf16[2,512,768]{2,0,1:T(2,128)(2,1)}), bf16[2,512,768]{2,0,1:T(2,128)(2,1)}, u32[]{:S(2)}, u32[]{:S(2)}) async-start(bf16[2,512,768]{2,0,1:T(2,128)(2,1)} %copy.126), calls=%async_computation.2 | async-start | bytes 3145728 | tf_op jit(solution)/shard_map/all_to_all | solution.py:377
  735.9 505.9 %reduce-scatter.17.cloned.1.call-start = ((), (), s32[]{:S(2)}) async-start(), calls=%async_computation.27 | async-start | bytes 9732096 | tf_op jit(solution)/shard_map/reduce_scatter | solution.py:368
  759.6 4.5 copy-start.41
  968.7 8.9 copy-start.61
  971.5 61.6 %all-to-all-start.4 = ((bf16[2,512,768]{2,0,1:T(2,128)(2,1)}), bf16[2,512,768]{2,0,1:T(2,128)(2,1)S(1)}, u32[]{:S(2)}, u32[]{:S(2)}) async-start(bf16[2,512,768]{2,0,1:T(2,128)(2,1)} %copy.142), calls=%async_computation.4 | async-start | bytes 3145728 | tf_op jit(solution)/shard_map/all_to_all | solution.py:378
  977.4 368.1 %reduce-scatter.11.cloned.1.call-start = ((), (), s32[]{:S(2)}) async-start(), calls=%async_computation.24 | async-start | bytes 2433024 | tf_op jit(solution)/shard_map/reduce_scatter | solution.py:358
  1038.6 3.8 copy-start.26
  1038.6 58.1 %all-to-all-start.3 = ((bf16[16,64,768]{2,1,0:T(8,128)(2,1)}), bf16[16,64,768]{2,1,0:T(8,128)(2,1)S(1)}, u32[]{:S(2)}, u32[]{:S(2)}) async-start(bf16[16,64,768]{2,1,0:T(8,128)(2,1)} %get-tuple-element.827), calls=%async_computation.3 | async-start | bytes 3145728 | tf_op jit(solution)/shard_map/all_to_all | solution.py:387
  1042.4 407.7 %reduce-scatter.9.cloned.1.call-start = ((), (), s32[]{:S(2)}) async-start(), calls=%async_computation.23 | async-start | bytes 2433024 | tf_op jit(solution)/shard_map/reduce_scatter | solution.py:357
  1046.8 53.5 %copy-start.49 = (f32[12,64]{1,0:T(8,128)S(1)}, f32[12,64]{1,0:T(8,128)}, u32[]{:S(2)}) copy-start(f32[12,64]{1,0:T(8,128)} %get-tuple-element.805) | copy-start | bytes 9220
  1046.8 53.7 %copy-start.50 = (f32[768]{0:T(1024)S(1)}, f32[768]{0:T(1024)}, u32[]{:S(2)}) copy-start(f32[768]{0:T(1024)} %get-tuple-element.719) | copy-start | bytes 9220
  1046.8 53.7 %copy-start.51 = (f32[768]{0:T(1024)S(1)}, f32[768]{0:T(1024)}, u32[]{:S(2)}) copy-start(f32[768]{0:T(1024)} %get-tuple-element.721) | copy-start | bytes 9220
  1046.8 53.7 %copy-start.52 = (f32[768]{0:T(1024)S(1)}, f32[768]{0:T(1024)}, u32[]{:S(2)}) copy-start(f32[768]{0:T(1024)} %get-tuple-element.799) | copy-start | bytes 9220
  1046.9 53.7 %copy-start.53 = (f32[768]{0:T(1024)S(1)}, f32[768]{0:T(1024)}, u32[]{:S(2)}) copy-start(f32[768]{0:T(1024)} %get-tuple-element.801) | copy-start | bytes 9220
  1046.9 53.7 %copy-start.55 = (f32[3072]{0:T(1024)S(1)}, f32[3072]{0:T(1024)}, u32[]{:S(2)}) copy-start(f32[3072]{0:T(1024)} %get-tuple-element.834) | copy-start | bytes 36868
  1046.9 53.7 %copy-start.58 = (f32[768]{0:T(1024)S(1)}, f32[768]{0:T(1024)}, u32[]{:S(2)}) copy-start(f32[768]{0:T(1024)} %get-tuple-element.717) | copy-start | bytes 9220
  1046.9 53.7 %copy-start.59 = (f32[768]{0:T(1024)S(1)}, f32[768]{0:T(1024)}, u32[]{:S(2)}) copy-start(f32[768]{0:T(1024)} %get-tuple-element.722) | copy-start | bytes 9220
  1096.8 67.9 %all-to-all-start.5 = ((bf16[16,64,768]{2,1,0:T(8,128)(2,1)}), bf16[16,64,768]{2,1,0:T(8,128)(2,1)S(1)}, u32[]{:S(2)}, u32[]{:S(2)}) async-start(bf16[16,64,768]{2,1,0:T(8,128)(2,1)} %get-tuple-element.826), calls=%async_computation.5 | async-start | bytes 3145728 | tf_op jit(solution)/shard_map/all_to_all | solution.py:388
  (31 other events, 63.2 us)
Sparse Core Ops, SparseCore 0:
  10.9 72.6 all-gather.16
  86.6 62.3 all-gather.10
  151.8 53.0 all-gather.14
  206.3 45.3 all-gather.18
  253.1 46.3 all-gather.12
  302.3 54.0 all-gather.20
  359.3 62.5 all-gather.22
  424.8 62.3 all-gather.24
  489.4 46.0 all-gather.26
  567.8 47.6 all-gather.28
  698.9 110.0 reduce-scatter.6
  815.6 98.0 reduce-scatter.12
  920.1 180.5 reduce-scatter.14
  1108.1 133.6 reduce-scatter.16
  1247.5 97.9 reduce-scatter.10
  1352.1 97.9 reduce-scatter.8
where the time goes:
time: 1470 us; the launch traced here: 1460 us
  waiting for transfers between devices  571 us (39%)
  matrix products  508 us (35%)
  blocking collectives  127 us (9%)
  local copies, waits for them, and re-layouts  122 us (8%)
  other arithmetic  80.5 us (5%)
  starting transfers between devices  31.4 us (2%)
  between operations  16.1 us (1%)
    unnamed x2, blocking collectives  115 us
    reduce_scatter x1, waiting for transfers between devices, shards(): lax.psum_scatter(grad_wk, ('dp', 'fsdp'), scatter_dimension=0, tiled=True)  105 us
    reduce_scatter x1, waiting for transfers between devices, shards(): lax.psum_scatter(grad_wv, ('dp', 'fsdp'), scatter_dimension=0, tiled=True)  104 us
    dot_general x8, matrix products, advance(): jnp.einsum('srhd,snhd->shrn', query_heads, key_part, preferred_element_ty...  87 us
    reduce_scatter x1, waiting for transfers between devices, shards(): lax.psum_scatter(grad_outer, ('dp', 'fsdp'), scatter_dimension=0, tiled=T...  75.8 us
    dot_general x4, matrix products, advance(): jnp.einsum('shrn,srhd->snhd', grad_scores, query_part, preferred_element_...  66.2 us
    dot_general x4, matrix products, advance(): jnp.einsum('shrn,snhd->srhd', grad_scores, key_part, preferred_element_ty...  65.9 us
    dot_general x6, matrix products, dense(): return jnp.dot(left, right, preferred_element_type=jnp.float32)  59.1 us
  transfers between devices with their start and end apart: 22, of which 10 were waited for; matrix products, arithmetic and copies ran while one was open for 48% of the time, Pallas kernels for 0%

commit v1 on v0

v1 whole, which is shorter than its diff:
```python
import functools
import math

import jax
import jax.numpy as jnp
from jax import lax
from jax.experimental import pallas as pl
from jax.experimental.pallas import tpu as pltpu
from jax.sharding import PartitionSpec as P

HEADS = 12
EPSILON = 1e-05
MASKED = -1e30
LOG2E = 1.4426950408889634
BOTH = ("dp", "fsdp")
NN = (((1,), (0,)), ((), ()))
NT = (((1,), (1,)), ((), ()))
TN = (((0,), (0,)), ((), ()))
f32 = jnp.float32
bf16 = jnp.bfloat16
LANES = 128


def dot(left, right, dims=NN, precision=None):
    return lax.dot_general(left, right, dims, preferred_element_type=f32, precision=precision)


def attend_kernel(q_ref, k_ref, v_ref, bias_ref, o_ref, lse_ref, k_even, k_odd, v_even, v_odd, *, scale):
    half = LANES // 2

    @pl.when(pl.program_id(1) == 0)
    def _():
        k, v, bias = k_ref[...], v_ref[...], bias_ref[...]
        low = lax.broadcasted_iota(jnp.int32, k.shape, 1) < half
        one = jnp.ones_like(v)
        k_even[...] = jnp.where(low, k, bias)
        k_odd[...] = jnp.where(low, bias, k)
        v_even[...] = jnp.where(low, v, one)
        v_odd[...] = jnp.where(low, one, v)

    q = q_ref[...]
    lane = lax.broadcasted_iota(jnp.int32, q.shape, 1)
    low = lane < half
    scaled = q * jnp.asarray(scale, bf16)
    one, zero = jnp.ones_like(q), jnp.zeros_like(q)
    q_even = jnp.where(low, scaled, jnp.where(lane == half, one, zero))
    q_odd = jnp.where(low, jnp.where(lane == 0, one, zero), scaled)

    def head(queries, keys, values):
        scores = dot(queries, keys[...], NT)
        top = jnp.max(scores, axis=1, keepdims=True)
        weights = jnp.exp2((scores - top) * LOG2E)
        return dot(weights.astype(bf16), values[...]), top

    out_even, top_even = head(q_even, k_even, v_even)
    out_odd, top_odd = head(q_odd, k_odd, v_odd)
    out = jnp.where(low, out_even, out_odd)
    total = jnp.where(low, pltpu.roll(out_even, half, 1), pltpu.roll(out_odd, half, 1))
    o_ref[...] = (out / total).astype(o_ref.dtype)
    lse = (jnp.where(low, top_even, top_odd) + jnp.log(total)) * LOG2E
    row = lax.broadcasted_iota(jnp.int32, (8, LANES), 0)
    col = lax.broadcasted_iota(jnp.int32, (8, LANES), 1)
    pick = jnp.where(col == row * half, 1.0, 0.0).astype(f32)
    lse_ref[0] = dot(pick, lse, NT, lax.Precision.HIGHEST)


def attend(qkv, bias, width, scale, block):
    rows = qkv.shape[0]
    pairs = width // LANES
    spec = lambda part: pl.BlockSpec((rows, LANES), lambda h, i: (0, part * pairs + h))
    return pl.pallas_call(
        functools.partial(attend_kernel, scale=scale),
        grid=(pairs, rows // block),
        in_specs=[
            pl.BlockSpec((block, LANES), lambda h, i: (i, h)),
            spec(1),
            spec(2),
            pl.BlockSpec((rows, LANES), lambda h, i: (0, 0)),
        ],
        out_specs=[
            pl.BlockSpec((block, LANES), lambda h, i: (i, h)),
            pl.BlockSpec((1, 8, block), lambda h, i: (h, 0, i)),
        ],
        out_shape=[
            jax.ShapeDtypeStruct((rows, width), bf16),
            jax.ShapeDtypeStruct((pairs, 8, rows), f32),
        ],
        scratch_shapes=[pltpu.VMEM((rows, LANES), bf16)] * 4,
        compiler_params=pltpu.CompilerParams(vmem_limit_bytes=56 << 20),
        cost_estimate=pl.CostEstimate(
            flops=4 * rows * rows * width * 4,
            bytes_accessed=8 * rows * width,
            transcendentals=rows * rows * pairs * 2,
        ),
        name="attend",
    )(qkv, qkv, qkv, bias)


def attend_back_kernel(
    q_ref, k_ref, v_ref, bias_ref, do_ref, o_ref, lse_ref,
    dq_ref, dk_ref, dv_ref,
    q_even, q_odd, z_even, z_odd, d_even, d_odd, delta, dq_turned,
    *, scale, block,
):
    half = LANES // 2
    step = pl.program_id(1)
    rows = q_ref.shape[0]

    @pl.when(step == 0)
    def _():
        lane = lax.broadcasted_iota(jnp.int32, q_ref.shape, 1)
        low = lane < half
        scaled = q_ref[...] * jnp.asarray(scale, bf16)
        one, zero = jnp.ones_like(scaled), jnp.zeros_like(scaled)
        q_even[...] = jnp.where(low, scaled, jnp.where(lane == half, one, zero))
        q_odd[...] = jnp.where(low, jnp.where(lane == 0, one, zero), scaled)
        z_even[...] = jnp.where(low, scaled, zero)
        z_odd[...] = jnp.where(low, zero, scaled)
        grad = do_ref[...]
        d_even[...] = jnp.where(low, grad, zero)
        d_odd[...] = jnp.where(low, zero, grad)
        row = lax.broadcasted_iota(jnp.int32, (8, LANES), 0)
        col = lax.broadcasted_iota(jnp.int32, (8, LANES), 1)
        select = jnp.where(lax.div(col, half) == row, 1.0, 0.0).astype(f32)
        product = grad.astype(f32) * o_ref[...].astype(f32)
        delta[...] = dot(select, product, NT, lax.Precision.HIGHEST)
        dq_turned[...] = jnp.zeros_like(dq_turned)

    k, v, bias = k_ref[...], v_ref[...], bias_ref[...]
    low = lax.broadcasted_iota(jnp.int32, k.shape, 1) < half
    k_even = jnp.where(low, k, bias)
    k_odd = jnp.where(low, bias, k)
    k_turned = k.T
    dk = jnp.zeros(k.shape, f32)
    dv = jnp.zeros(k.shape, f32)
    heads = ((k_even, q_even, z_even, d_even), (k_odd, q_odd, z_odd, d_odd))
    for first in range(0, rows, block):
        part = slice(first, first + block)
        for h, (keys, queries, plain, grads) in enumerate(heads):
            scores = dot(keys, queries[part, :], NT)
            weights = jnp.exp2(scores * LOG2E - lse_ref[0, h : h + 1, part])
            d_weights = dot(v, grads[part, :], NT)
            d_scores = (weights * (d_weights - delta[h : h + 1, part])).astype(bf16)
            dv += dot(weights.astype(bf16), grads[part, :])
            dk += dot(d_scores, plain[part, :])
            dq_turned[h * half : (h + 1) * half, part] += dot(
                k_turned[h * half : (h + 1) * half, :], d_scores
            )
    dk_ref[...] = dk.astype(bf16)
    dv_ref[...] = dv.astype(bf16)

    @pl.when(step == pl.num_programs(1) - 1)
    def _():
        dq_ref[...] = (dq_turned[...] * scale).T.astype(bf16)


def attend_back(qkv, bias, grads, out, lse, width, scale, key_block, block):
    rows = qkv.shape[0]
    pairs = width // LANES
    whole = lambda: pl.BlockSpec((rows, LANES), lambda h, j: (0, h))
    part = lambda n: pl.BlockSpec((key_block, LANES), lambda h, j: (j, n * pairs + h))
    return pl.pallas_call(
        functools.partial(attend_back_kernel, scale=scale, block=block),
        grid=(pairs, rows // key_block),
        in_specs=[
            whole(),
            part(1),
            part(2),
            pl.BlockSpec((key_block, LANES), lambda h, j: (j, 0)),
            whole(),
            whole(),
            pl.BlockSpec((1, 8, rows), lambda h, j: (h, 0, 0)),
        ],
        out_specs=[whole(), part(0), part(0)],
        out_shape=[jax.ShapeDtypeStruct((rows, width), bf16)] * 3,
        scratch_shapes=[pltpu.VMEM((rows, LANES), bf16)] * 6
        + [pltpu.VMEM((8, rows), f32), pltpu.VMEM((LANES, rows), f32)],
        compiler_params=pltpu.CompilerParams(vmem_limit_bytes=56 << 20),
        cost_estimate=pl.CostEstimate(
            flops=10 * rows * rows * width * 4,
            bytes_accessed=16 * rows * width,
            transcendentals=rows * rows * pairs * 2,
        ),
        name="attend_back",
    )(qkv, qkv, qkv, bias, grads, out, lse)


DIGITS = {"z": (4, 8), "x": (2, 4), "y": (2, 2), "c": (2, 1)}


def digit(name):
    size, stride = DIGITS[name]
    number = lax.axis_index("dp") * 4 + lax.axis_index("fsdp")
    return lax.rem(lax.div(number, stride), size)


def shift(value, name, amount):
    size, stride = DIGITS[name]
    pairs = []
    for source in range(32):
        place = source // stride % size
        pairs.append((source, source + ((place + amount) % size - place) * stride))
    return lax.ppermute(value, BOTH, pairs)


def gather_z(part):
    ring = [part] + [shift(part, "z", amount) for amount in (3, 2, 1)]
    ring = jnp.stack(ring + ring[:-1])
    return lax.dynamic_slice_in_dim(ring, lax.rem(4 - digit("z"), 4), 4, 0)


def spread(part, order):
    held = {(): gather_z(part)}
    for name in order:
        arrived = {key + (1,): shift(value, name, 1) for key, value in held.items()}
        held = {key + (0,): value for key, value in held.items()}
        held.update(arrived)
    return held


def put_together(held, order):
    first = next(iter(held.values()))
    out = jnp.zeros((4, 2, 2, 2) + first.shape[1:], first.dtype)
    own = {name: digit(name) for name in "xyc"}
    for key, value in held.items():
        place = {name: own[name] ^ rel for name, rel in zip(order, key)}
        start = (0, place["x"], place["y"], place["c"]) + (0,) * (first.ndim - 1)
        out = lax.dynamic_update_slice(out, value[:, None, None, None], start)
    return out.reshape((32 * first.shape[1],) + first.shape[2:])


def gather_rows(part, order):
    if lax.axis_size("dp") == 8 and lax.axis_size("fsdp") == 4:
        return put_together(spread(part, order + "c"), order + "c")
    return lax.all_gather(part, BOTH, axis=0, tiled=True)


def pick(value, axis, index):
    return lax.squeeze(lax.dynamic_slice_in_dim(value, index, 1, axis), (axis,))


def halve(value, axes, name):
    axis = axes.index(name)
    own = digit(name)
    arrived = shift(pick(value, axis, 1 - own).astype(bf16), name, 1)
    kept = pick(value, axis, own).astype(f32) + arrived.astype(f32)
    return kept, axes[:axis] + axes[axis + 1 :]


def scatter_rows(value, order):
    if not (lax.axis_size("dp") == 8 and lax.axis_size("fsdp") == 4):
        return lax.psum_scatter(value, BOTH, scatter_dimension=0, tiled=True)
    rows = value.shape[0] // 32
    value = value.reshape((4, 2, 2, 2, rows, value.shape[1]))
    axes = "zxyc"
    for name in "c" + order:
        value, axes = halve(value, axes, name)
    return scatter_z(value)


def scatter_z(value):
    own = digit("z")
    total = pick(value, 0, own).astype(f32)
    for amount in (1, 2, 3):
        piece = pick(value, 0, lax.rem(own + amount, 4)).astype(bf16)
        total = total + shift(piece, "z", amount).astype(f32)
    return total


def normalize(resid):
    average = jnp.mean(resid, axis=-1, keepdims=True)
    centred = resid - average
    second = jnp.mean(centred * centred, axis=-1, keepdims=True)
    inverse = lax.rsqrt(second + EPSILON)
    return centred * inverse, inverse


def normalize_back(grad, unit, inverse, gain):
    scaled = grad * gain
    along = jnp.mean(scaled * unit, axis=-1, keepdims=True)
    return inverse * (scaled - jnp.mean(scaled, axis=-1, keepdims=True) - unit * along)


def shards(
    tokens, teacher, lengths, dealing,
    query_weight, key_weight, value_weight, output_weight, inner_weight, outer_weight,
    query_bias, value_bias, output_bias, norm_gain, norm_shift, inner_bias, outer_bias,
    final_gain, final_shift,
):
    slots, row_count, width = tokens.shape
    sections = lax.axis_size("fsdp")
    dp_count = lax.axis_size("dp")
    ranks = sections // 2
    fast = dp_count == 8 and sections == 4
    hidden_units = inner_weight.shape[1]
    head_width = width // HEADS
    scale = 1.0 / math.sqrt(head_width)
    seq_total = lengths.shape[0]
    seq_len = row_count * sections
    share = width // ranks
    padded = -(-share // LANES) * LANES
    rows = 2 * row_count

    place = lax.axis_index("fsdp")
    side = lax.div(place, ranks)
    rank = lax.rem(place, ranks)
    across = [(f, (f + ranks) % sections) for f in range(sections)]
    groups = [[g * ranks + r for r in range(ranks)] for g in range(2)]
    partner = [(f, f ^ 1) for f in range(sections)]
    length = lax.dynamic_index_in_dim(
        lengths, lax.axis_index("dp") * slots + side, keepdims=False
    )

    def swap_in(whole):
        kept = lax.dynamic_index_in_dim(whole, side, 0, keepdims=False)
        sent = lax.dynamic_index_in_dim(whole, 1 - side, 0, keepdims=False)
        return jnp.concatenate([kept, lax.ppermute(sent, "fsdp", across)], axis=0)

    def swap_out(local):
        kept = local[:row_count]
        arrived = lax.ppermute(local[row_count:], "fsdp", across)
        return jnp.where(side == 0, jnp.stack([kept, arrived]), jnp.stack([arrived, kept]))

    def gather_group(local):
        if ranks == 2:
            return jnp.concatenate([local, lax.ppermute(local, "fsdp", partner)], axis=0)
        return lax.all_gather(local, "fsdp", axis=0, tiled=True, axis_index_groups=groups)

    if ranks == 2:
        rank_order = [rank, 1 - rank]
    else:
        rank_order = [jnp.int32(r) for r in range(ranks)]
    block_ids = []
    for r in rank_order:
        block_ids += [side * ranks + r, (1 - side) * ranks + r]
    within = lax.iota(jnp.int32, row_count)
    positions = jnp.concatenate([b * row_count + within for b in block_ids])
    bias = jnp.where(positions < length, 0.0, MASKED).astype(bf16)
    key_bias = jnp.broadcast_to(bias[:, None], (rows * ranks, LANES))

    def heads_to_rows(part):
        if ranks == 2:
            kept = part[:rows]
            arrived = lax.ppermute(part[rows:], "fsdp", partner)
            return jnp.where(
                rank == 0,
                jnp.concatenate([kept, arrived], axis=1),
                jnp.concatenate([arrived, kept], axis=1),
            )
        return lax.all_to_all(
            part, "fsdp", split_axis=0, concat_axis=1, tiled=True, axis_index_groups=groups
        )

    def rows_to_heads(part):
        if ranks == 2:
            kept = lax.dynamic_slice_in_dim(part, rank * share, share, 1)
            sent = lax.dynamic_slice_in_dim(part, (1 - rank) * share, share, 1)
            return jnp.concatenate([kept, lax.ppermute(sent, "fsdp", partner)], axis=0)
        return lax.all_to_all(
            part, "fsdp", split_axis=1, concat_axis=0, tiled=True, axis_index_groups=groups
        )

    vectors = [
        query_bias, value_bias, output_bias, norm_gain, norm_shift, outer_bias, final_gain,
        final_shift, inner_bias,
    ]
    packed = jnp.concatenate(vectors)
    small = query_weight.shape[0]
    if fast:
        per_row = packed.shape[0] // small
        packed = jnp.pad(packed.reshape(small, per_row), ((0, 0), (0, LANES - per_row)))
        first = jnp.concatenate([query_weight, key_weight, value_weight, packed], axis=1)
        held = spread(first, "xy")

        def mine(block, which):
            parts = [
                lax.dynamic_slice_in_dim(block, n * width + which * share, share, 2)
                for n in range(3)
            ]
            return jnp.concatenate(parts + [block[:, :, 3 * width :]], axis=2)

        last = {}
        for key, block in held.items():
            last[key + (0,)] = mine(block, rank)
            last[key + (1,)] = shift(mine(block, 1 - rank), "c", 1)
        whole = put_together(last, "xyc")
        qkv_weight = whole[:, : 3 * share]
        packed = whole[:, 3 * share : 3 * share + per_row].reshape(32, small * per_row)
    else:
        whole = [
            lax.all_gather(w, BOTH, axis=0, tiled=True)
            for w in (query_weight, key_weight, value_weight)
        ]
        whole = [lax.dynamic_slice_in_dim(w, rank * share, share, 1) for w in whole]
        qkv_weight = jnp.concatenate(whole, axis=1)
        packed = lax.all_gather(packed, BOTH, axis=0, tiled=False).reshape(
            dp_count * sections, packed.shape[0]
        )
    unpacked = []
    start = 0
    for vector in vectors:
        count = vector.shape[0]
        unpacked.append(packed[:, start : start + count].reshape(-1).astype(f32))
        start += count
    b_query, b_value, b_output, gain_one, shift_one, b_outer, gain_two, shift_two, b_inner = unpacked
    w_output = gather_rows(output_weight, "xy")
    w_inner = gather_rows(inner_weight, "xy")
    w_outer = gather_rows(outer_weight, "yx")

    local = swap_in(tokens)
    gathered = gather_group(local)
    b_qkv = jnp.concatenate(
        [
            lax.dynamic_slice_in_dim(b_query, rank * share, share),
            jnp.zeros((share,), f32),
            lax.dynamic_slice_in_dim(b_value, rank * share, share),
        ]
    )
    qkv = (dot(gathered, qkv_weight) + b_qkv).astype(bf16)
    if padded != share:
        fill = ((0, 0), (0, 0), (0, padded - share))
        qkv = jnp.pad(qkv.reshape(-1, 3, share), fill).reshape(-1, 3 * padded)
    heads_out, lse = attend(qkv, key_bias, padded, scale, 1024)
    attn_rows = heads_to_rows(heads_out[:, :share])

    resid_one = local.astype(f32) + dot(attn_rows, w_output) + b_output
    unit_one, inverse_one = normalize(resid_one)
    hidden = (unit_one * gain_one + shift_one).astype(bf16)
    inner = dot(hidden, w_inner) + b_inner
    normal = 0.5 + 0.5 * lax.erf(inner * math.sqrt(0.5))
    act = (inner * normal).astype(bf16)
    slope = (normal + inner * jnp.exp(-0.5 * inner * inner) * (1.0 / math.sqrt(2 * math.pi))).astype(bf16)
    resid_two = hidden.astype(f32) + dot(act, w_outer) + b_outer
    unit_two, inverse_two = normalize(resid_two)
    final = unit_two * gain_two + shift_two
    output = swap_out(final.astype(bf16))

    slot_ids = lax.iota(jnp.int32, seq_total)
    inverse = jnp.sum(
        jnp.where(dealing[None, :] == slot_ids[:, None], slot_ids[None, :], 0), axis=1
    )
    target = lax.all_to_all(teacher, "dp", split_axis=1, concat_axis=0, tiled=True)
    target = jnp.take(target, inverse, axis=0)
    target = lax.all_to_all(target, "dp", split_axis=0, concat_axis=1, tiled=True)
    target = swap_in(target)

    valid = (positions[:rows] < length).astype(f32)[:, None] if ranks == 2 else None
    if valid is None:
        own = jnp.concatenate(
            [b * row_count + within for b in (side * ranks + rank, (1 - side) * ranks + rank)]
        )
        valid = (own < length).astype(f32)[:, None]
    loss_scale = seq_total * seq_len / jnp.sum(lengths).astype(f32)
    grad_final = loss_scale * (final - target.astype(f32)) * valid
    grad_gain_two = jnp.sum(grad_final * unit_two, axis=0)
    grad_shift_two = jnp.sum(grad_final, axis=0)
    d_two = normalize_back(grad_final, unit_two, inverse_two, gain_two)
    d_out = d_two.astype(bf16)
    grad_outer_bias = jnp.sum(d_out.astype(f32), axis=0)
    d_inner = (dot(d_out, w_outer, NT) * slope.astype(f32)).astype(bf16)
    grad_inner_bias = jnp.sum(d_inner.astype(f32), axis=0)
    d_hidden = d_two + dot(d_inner, w_inner, NT)
    grad_gain_one = jnp.sum(d_hidden * unit_one, axis=0)
    grad_shift_one = jnp.sum(d_hidden, axis=0)
    d_one = normalize_back(d_hidden, unit_one, inverse_one, gain_one)
    d_mix = d_one.astype(bf16)
    grad_output_bias = jnp.sum(d_mix.astype(f32), axis=0)
    d_attn = dot(d_mix, w_output, NT).astype(bf16)
    heads_grad = rows_to_heads(d_attn)

    grad_outer = scatter_rows(dot(act, d_out, TN), "yx")
    grad_inner = scatter_rows(dot(hidden, d_inner, TN), "xy")
    grad_output = scatter_rows(dot(attn_rows, d_mix, TN), "yx")

    if padded != share:
        heads_grad = jnp.pad(heads_grad, ((0, 0), (0, padded - share)))
    d_query, d_key, d_value = attend_back(
        qkv, key_bias, heads_grad, heads_out, lse, padded, scale, 512, 1024
    )
    d_query, d_key, d_value = d_query[:, :share], d_key[:, :share], d_value[:, :share]
    d_qkv = jnp.concatenate([d_query, d_key, d_value], axis=1)
    grad_qkv = dot(gathered, d_qkv, TN)
    bias_query = jnp.sum(d_query.astype(f32), axis=0)
    bias_value = jnp.sum(d_value.astype(f32), axis=0)
    d_gathered = dot(d_qkv, qkv_weight, NT)
    if ranks == 2:
        arrived = lax.ppermute(d_gathered[rows:].astype(bf16), "fsdp", partner)
        d_local = d_gathered[:rows] + arrived.astype(f32)
    else:
        d_local = lax.psum_scatter(
            d_gathered, "fsdp", scatter_dimension=0, tiled=True, axis_index_groups=groups
        )
    input_grad = swap_out((d_one + d_local).astype(bf16))

    def place_share(part):
        empty = jnp.zeros(part.shape[:-1] + (width,), part.dtype)
        return lax.dynamic_update_slice_in_dim(empty, part, rank * share, part.ndim - 1)

    sums = [
        place_share(bias_query), place_share(bias_value), grad_output_bias, grad_gain_one,
        grad_shift_one, grad_outer_bias, grad_gain_two, grad_shift_two, grad_inner_bias,
    ]
    sums = jnp.concatenate([s.reshape(dp_count * sections, -1) for s in sums], axis=1)
    if fast:
        value = grad_qkv.reshape(4, 2, 2, 2 * small, 3 * share)
        axes = "zxy"
        for name in "xy":
            value, axes = halve(value, axes, name)
        value = scatter_z(value).reshape(2, small, 3, share)
        own = pick(value, 0, rank)
        arrived = shift(pick(value, 0, 1 - rank), "c", 1)
        value = jnp.where(
            rank == 0,
            jnp.concatenate([own, arrived], axis=2),
            jnp.concatenate([arrived, own], axis=2),
        )
        grad_query, grad_key, grad_value = value[:, 0], value[:, 1], value[:, 2]
        small_sums = sums.reshape(4, 2, 2, 2, 1, sums.shape[1])
        axes = "zxyc"
        for name in "cxy":
            axis = axes.index(name)
            own = digit(name)
            small_sums = pick(small_sums, axis, own) + shift(
                pick(small_sums, axis, 1 - own), name, 1
            )
            axes = axes[:axis] + axes[axis + 1 :]
        own = digit("z")
        total = pick(small_sums, 0, own)
        for amount in (1, 2, 3):
            total = total + shift(
                pick(small_sums, 0, lax.rem(own + amount, 4)), "z", amount
            )
        sums = total.reshape(-1)
    else:
        parts = [place_share(grad_qkv[:, n * share : (n + 1) * share]) for n in range(3)]
        grad_query, grad_key, grad_value = [
            lax.psum_scatter(p, BOTH, scatter_dimension=0, tiled=True) for p in parts
        ]
        sums = lax.psum_scatter(sums, BOTH, scatter_dimension=0, tiled=True).reshape(-1)
    split = []
    start = 0
    for vector in vectors:
        count = vector.shape[0]
        split.append(sums[start : start + count])
        start += count
    return (
        output, input_grad, grad_query, grad_key, grad_value, grad_output, grad_inner, grad_outer,
        split[0], split[1], split[2], split[3], split[4], split[8], split[5], split[6], split[7],
    )


def solution(mesh):
    act = P("dp", "fsdp", None)
    matrix = P(BOTH, None)
    vector = P(BOTH)
    return jax.shard_map(
        shards,
        mesh=mesh,
        in_specs=(act, act, P(), P()) + (matrix,) * 6 + (vector,) * 9,
        out_specs=(act, act) + (matrix,) * 6 + (vector,) * 9,
        check_vma=False,
    )
```

time: 1470 us -> 611 us (0.42)
  matrix products: 508 us -> 85.8 us
  waiting for transfers between devices: 571 us -> 159 us
  blocking collectives: 127 us -> 0 us
  Pallas kernels: 0 us -> 119 us
  starting transfers between devices: 31.4 us -> 91.1 us
  other arithmetic: 80.5 us -> 45.2 us
  local copies, waits for them, and re-layouts: 122 us -> 98.9 us
    dot_general x46 -> x12, matrix products: 508 us -> 85.8 us  [dot(): lax.dot_general(left, right, dims, preferred_element_type=f32, precision=...]
    reduce_scatter x6 -> x0, waiting for transfers between devices: 284 us -> none  [the longest x1 105 us: shards(): lax.psum_scatter(grad_wk, ('dp', 'fsdp'), scatter_dimension=0, tiled=True)]
    all_gather x10 -> x0, waiting for transfers between devices: 147 us -> none  [the longest x1 47.8 us: shards(): lax.all_gather(key_slots, 'fsdp', axis=1, tiled=True)]
    ppermute x0 -> x78, waiting for transfers between devices: none -> 143 us  [the longest x70 123 us: shift(): return lax.ppermute(value, BOTH, pairs)]
    pallas_call x0 -> x2, Pallas kernels: none -> 119 us  [the longest x1 72.3 us: attend_back(): pl.pallas_call(functools.partial(attend_back_kernel, scale=scale, block=b...]
    all_to_all x6 -> x2, waiting for transfers between devices: 135 us -> 16.4 us  [the longest x1 16.4 us: shards(): lax.all_to_all(target, 'dp', split_axis=0, concat_axis=1, tiled=True)]
    unnamed x2 -> x0, blocking collectives: 115 us -> none
    ppermute x0 -> x78, starting transfers between devices: none -> 83.2 us  [the longest x70 78.6 us: shift(): return lax.ppermute(value, BOTH, pairs)]
  transfers between devices with their start and end apart: 22 -> 80, of which waited for: 10 -> 29; matrix products, arithmetic and copies ran while one was open for 48% -> 30% of each run, Pallas kernels for 0% -> 20%
where the time goes in v1:
time: 611 us; the launch traced here: 602 us
  waiting for transfers between devices  159 us (26%)
  Pallas kernels  119 us (19%)
  local copies, waits for them, and re-layouts  98.9 us (16%)
  starting transfers between devices  91.1 us (15%)
  matrix products  85.8 us (14%)
  other arithmetic  45.2 us (7%)
    ppermute x70, waiting for transfers between devices, shift(): return lax.ppermute(value, BOTH, pairs)  123 us
    dot_general x12, matrix products, dot(): lax.dot_general(left, right, dims, preferred_element_type=f32, precision=...  85.8 us
    ppermute x70, starting transfers between devices, shift(): return lax.ppermute(value, BOTH, pairs)  78.6 us
    pallas_call x1, Pallas kernels, attend_back(): pl.pallas_call(functools.partial(attend_back_kernel, scale=scale, block=b...  72.3 us
    pallas_call x1, Pallas kernels, attend(): pl.pallas_call(functools.partial(attend_kernel, scale=scale), grid=(pairs...  46.9 us
    dynamic_update_slice x28, local copies, waits for them, and re-layouts, put_together(): out = lax.dynamic_update_slice(out, value[:, None, None, None], start)  29.1 us
    unnamed x109, local copies, waits for them, and re-layouts  21.4 us
    all_to_all x1, waiting for transfers between devices, shards(): lax.all_to_all(target, 'dp', split_axis=0, concat_axis=1, tiled=True)  16.4 us
  transfers between devices with their start and end apart: 80, of which 29 were waited for; matrix products, arithmetic and copies ran while one was open for 30% of the time, Pallas kernels for 20%

profile of v1, /device:TPU:0, one launch (start us, length us, event | category | flops | bytes accessed | tf_op | source)
XLA Modules:
  0.0 602.3 jit_solution(13878387414534722628)
XLA Ops:
  0.8 5.1 collective-permute-start.33
  7.0 2.8 collective-permute-start.13
  10.9 4.2 copy.220
  15.1 4.0 all-to-all-start
  25.0 2.1 collective-permute-start.15
  27.7 3.3 collective-permute-start.2
  31.6 17.8 %collective-permute-done.15 = bf16[24,768]{1,0:T(8,128)(2,1)S(1)} collective-permute-done((bf16[24,768]{1,0:T(8,128)(2,1)S(1)}, bf16[24,768]{1,0:T(8,128)(2,1)S(1)}, u32[]{:S(2)}, u32[]{:S(2)}) %collective-permute-start.15) | collective-permute-done | bytes 36896 | tf_op jit(solution)/shard_map/ppermute | solution.py:203
  49.5 11.6 %collective-permute-start.3 = (bf16[24,2432]{1,0:T(8,128)(2,1)S(1)}, bf16[24,2432]{1,0:T(8,128)(2,1)S(1)}, u32[]{:S(2)}, u32[]{:S(2)}) collective-permute-start(bf16[24,2432]{1,0:T(8,128)(2,1)S(1)} %fusion.45), channel_id=1, source_target_pairs={{0,16},{1,17},{2,18},{3,19},{4,20},{5,21},{6,22},{7,23},{8,24},{9,... | collective-permute-start | bytes 350216 | tf_op jit(solution)/shard_map/ppermute | solution.py:203
  65.6 3.0 collective-permute-start.23
  68.6 4.1 collective-permute-done.4
  83.8 2.8 broadcast_in_dim.191
  87.8 2.7 broadcast_in_dim.200
  92.2 5.7 collective-permute-done.18
  110.0 4.5 collective-permute-done.36
  114.5 2.0 bitcast_dynamic-update-slice_fusion.5
  116.5 13.1 %collective-permute-done.26 = bf16[4,24,3072]{2,1,0:T(8,128)(2,1)S(1)} collective-permute-done((bf16[4,24,3072]{2,1,0:T(8,128)(2,1)}, bf16[4,24,3072]{2,1,0:T(8,128)(2,1)S(1)}, u32[]{:S(2)}, u32[]{:S(2)}) %collective-permute-start.26) | collective-permute-done | bytes 589856 | tf_op jit(solution)/shard_map/ppermute | solution.py:203
  133.3 1.9 bitcast_dynamic-update-slice_fusion.4
  140.6 3.9 all-to-all-start.1
  153.2 10.9 %collective-permute-done.28 = bf16[4,24,3072]{2,1,0:T(8,128)(2,1)S(1)} collective-permute-done((bf16[4,24,3072]{2,1,0:T(8,128)(2,1)S(1)}, bf16[4,24,3072]{2,1,0:T(8,128)(2,1)S(1)}, u32[]{:S(2)}, u32[]{:S(2)}) %collective-permute-start.28) | collective-permute-done | bytes 589856 | tf_op jit(solution)/shard_map/ppermute | solution.py:203
  165.1 16.4 %all-to-all-done.1 = bf16[16,64,768]{2,1,0:T(8,128)(2,1)S(1)} async-done(((bf16[16,64,768]{2,1,0:T(8,128)(2,1)}), bf16[16,64,768]{2,1,0:T(8,128)(2,1)S(1)}, u32[]{:S(2)}, u32[]{:S(2)}) %all-to-all-start.1) | async-done | bytes 1572896 | tf_op jit(solution)/shard_map/all_to_all | solution.py:444
  189.2 1.9 bitcast_dynamic-update-slice_fusion.2
  193.3 9.7 %collective-permute-done = bf16[512,768]{0,1:T(8,128)(2,1)} collective-permute-done((bf16[512,768]{0,1:T(8,128)(2,1)}, bf16[512,768]{0,1:T(8,128)(2,1)}, u32[]{:S(2)}, u32[]{:S(2)}) %collective-permute-start) | collective-permute-done | bytes 786464 | tf_op jit(solution)/shard_map/ppermute | solution.py:317
  206.9 2.0 bitcast_dynamic-update-slice_fusion.7
  208.8 1.9 bitcast_dynamic-update-slice_fusion.6
  210.8 8.9 %add_convert_fusion.q_ref.k_ref.v_ref = bf16[2048,1152]{1,0:T(8,128)(2,1)} fusion(f32[1152]{0:T(1024)S(1)} %pad_maximum_fusion.13, bf16[768,1280]{1,0:T(8,128)(2,1)} %bitcast.21, bf16[1024,768]{0,1:T(8,128)(2,1)S(1)} %collective-permute-done.1, bf16[512,768]{0,1:T(8,128)(2,1)} %collective-permute-done, bf16[512,768]{0,1:T(8,128)(2,1)S(1)} %bitcast.376), kind=kOutput, calls=%fused_computation.11 | convolution fusion | flops 3638034432 | bytes 9638400 | tf_op jit(solution)/shard_map/dot_general | solution.py:25
  220.8 46.9 %attend.1 = (bf16[2048,384]{1,0:T(8,128)(2,1)}, f32[3,8,2048]{2,1,0:T(8,128)}) custom-call(bf16[2048,1152]{1,0:T(8,128)(2,1)} %add_convert_fusion.q_ref.k_ref.v_ref, bf16[2048,1152]{1,0:T(8,128)(2,1)} %add_convert_fusion.q_ref.k_ref.v_ref, bf16[2048,1152]{1,0:T(8,128)(2,1)} %add_convert_fusion.q_ref.k_ref.v_ref, bf16[2048,128]{1,0:T(8,128)(2,1)} %broadcast_in_dim.181.bias_ref), custom_call_target="tpu_custom_call" | custom-call | flops 25769803776 | bytes 6291456 | tf_op jit(solution)/shard_map/attend/pallas_call | solution.py:71
  267.7 2.6 fusion.82
  270.4 1.9 bitcast_dynamic-update-slice_fusion.12
  274.8 4.1 fusion.83
  279.4 12.1 %multiply_convert_fusion.1 = (bf16[1024,3072]{1,0:T(8,128)(2,1)S(1)}, f32[1024,3072]{1,0:T(8,128)}) fusion(f32[3072]{0:T(1024)S(1)} %reshape.294, bf16[768,3072]{1,0:T(8,128)(2,1)} %bitcast.60, f32[1024,768]{0,1:T(8,128)S(1)} %get-tuple-element.204, f32[768]{0:T(1024)S(1)} %reshape.293, f32[768]{0:T(1024)S(1)} %reshape.292, f32[1024]{0:T(1024)S(1)} %add_rsqrt_fusion.1, ...), kind=kOutput, calls=%fused_computation.9 | convolution fusion | flops 4854644736 | bytes 26765312 | tf_op jit(solution)/shard_map/dot_general | solution.py:25
  291.5 7.4 %fusion.84 = (f32[1024]{0:T(1024)S(1)}, f32[1024,768]{0,1:T(8,128)S(1)}) fusion(f32[768]{0:T(1024)S(1)} %reshape.295, bf16[1024,3072]{1,0:T(8,128)(2,1)S(1)} %get-tuple-element.205, bf16[3072,768]{1,0:T(8,128)(2,1)} %bitcast.79, f32[768]{0:T(1024)S(1)} %reshape.293, f32[768]{0:T(1024)S(1)} %reshape.292, f32[1024]{0:T(1024)S(1)} %add_rsqrt_fusion.1, ...), kind=kOutput, calls=%fused_computation.332 | convolution fusion | flops 4838915072 | bytes 17323008 | tf_op jit(solution)/shard_map/dot_general | solution.py:25
  299.3 2.2 fusion.81
  301.6 3.0 convert_reduce_fusion.1
  304.6 7.7 %fusion.78 = f32[3072,768]{1,0:T(8,128)} fusion(bf16[1024,3072]{1,0:T(8,128)(2,1)S(1)} %get-tuple-element.205, f32[1024,768]{0,1:T(8,128)S(1)} %get-tuple-element.121), kind=kOutput, calls=%fused_computation.326 | convolution fusion | flops 4832624640 | bytes 18874368 | tf_op jit(solution)/shard_map/dot_general | solution.py:25
  312.3 12.3 %convert_reduce_fusion = (f32[3072]{0:T(1024)S(1)}, bf16[1024,3072]{1,0:T(8,128)(2,1)S(1)}) fusion(f32[1024,3072]{1,0:T(8,128)} %get-tuple-element.206, f32[3072]{0:T(1024)S(1)} %reshape.294, bf16[3072,768]{1,0:T(8,128)(2,1)} %bitcast.79, f32[1024,768]{0,1:T(8,128)S(1)} %get-tuple-element.121), kind=kOutput, calls=%fused_computation.7 | convolution fusion | flops 4879807488 | bytes 26763264 | tf_op jit(solution)/shard_map/dot_general | solution.py:25
  324.6 8.0 %multiply_reduce_fusion.1 = (f32[768]{0:T(1024)S(1)}, f32[1024]{0:T(1024)S(1)}, f32[1024]{0:T(1024)S(1)}, f32[768]{0:T(1024)S(1)}, f32[1024,768]{0,1:T(8,128)S(1)}) fusion(f32[1024,768]{0,1:T(8,128)S(1)} %get-tuple-element.204, f32[1024]{0:T(1024)S(1)} %add_rsqrt_fusion.1, f32[1024]{0:T(1024)S(1)} %broadcast_multiply_fusion.5, f32[768]{0:T(1024)S(1)} %reshape.292, ...), kind=kOutput, calls=%fused_computation.23 | convolution fusion | flops 4839698432 | bytes 20472832 | tf_op jit(solution)/shard_map/dot_general | solution.py:25
  332.5 8.3 %fusion.85 = f32[768,3072]{1,0:T(8,128)} fusion(bf16[1024,3072]{1,0:T(8,128)(2,1)S(1)} %get-tuple-element.211, f32[1024,768]{0,1:T(8,128)S(1)} %get-tuple-element.204, f32[768]{0:T(1024)S(1)} %reshape.293, f32[768]{0:T(1024)S(1)} %reshape.292, f32[1024]{0:T(1024)S(1)} %add_rsqrt_fusion.1, f32[1024]{0:T(1024)S(1)} %broadcast_multiply_fusion.5), kind=kOutput, calls=%fused_computation.333 | convolution fusion | flops 4835770368 | bytes 18888704 | tf_op jit(solution)/shard_map/dot_general | solution.py:25
  347.7 4.1 fusion.9
  352.0 2.9 fusion.26
  358.3 4.1 fusion.8
  363.7 2.4 pad_maximum_fusion.2.do_ref
  366.1 72.3 %attend_back.1 = (bf16[2048,384]{1,0:T(8,128)(2,1)}, bf16[2048,384]{1,0:T(8,128)(2,1)}, bf16[2048,384]{1,0:T(8,128)(2,1)}) custom-call(bf16[2048,1152]{1,0:T(8,128)(2,1)} %add_convert_fusion.q_ref.k_ref.v_ref, bf16[2048,1152]{1,0:T(8,128)(2,1)} %add_convert_fusion.q_ref.k_ref.v_ref, bf16[2048,1152]{1,0:T(8,128)(2,1)} %add_convert_fusion.q_ref.k_ref.v_ref, ...), custom_call_target="tpu_custom_call" | custom-call | flops 64424509440 | bytes 12582912 | tf_op jit(solution)/shard_map/attend_back/pallas_call | solution.py:162
  440.1 2.7 constant_dynamic-update-slice_fusion.9
  447.8 2.8 constant_dynamic-update-slice_fusion.8
  452.0 6.8 %fusion.10 = f32[2048,768]{0,1:T(8,128)S(1)} fusion(bf16[2048,1152]{1,0:T(8,128)(2,1)} %constant_dynamic-update-slice_fusion.7, bf16[768,1280]{1,0:T(8,128)(2,1)} %bitcast.21), kind=kOutput, calls=%fused_computation.59 | convolution fusion | flops 3623878656 | bytes 12779520 | tf_op jit(solution)/shard_map/dot_general | solution.py:25
  460.7 5.9 fusion.13
  470.5 3.1 collective-permute-start.76
  474.3 2.8 maximum_select_fusion.1
  478.4 2.6 copy.239
  482.1 8.4 %collective-permute-done.55 = bf16[4,2,24,768]{3,2,0,1:T(8,128)(2,1)S(1)} collective-permute-done((bf16[4,2,24,768]{3,2,0,1:T(8,128)(2,1)S(1)}, bf16[4,2,24,768]{3,2,0,1:T(8,128)(2,1)S(1)}, u32[]{:S(2)}, u32[]{:S(2)}) %collective-permute-start.55) | collective-permute-done | bytes 294944 | tf_op jit(solution)/shard_map/ppermute | solution.py:203
  499.3 6.8 %collective-permute-done.49 = bf16[4,48,1152]{2,1,0:T(8,128)(2,1)S(1)} collective-permute-done((bf16[4,48,1152]{2,1,0:T(8,128)(2,1)S(1)}, bf16[4,48,1152]{2,1,0:T(8,128)(2,1)S(1)}, u32[]{:S(2)}, u32[]{:S(2)}) %collective-permute-start.49) | collective-permute-done | bytes 442400 | tf_op jit(solution)/shard_map/ppermute | solution.py:203
  515.3 2.9 collective-permute-done.51
  520.2 3.6 bitcast_add_fusion
  524.1 3.9 bitcast_add_fusion.1
  529.8 2.4 fusion.6
  533.7 19.1 %collective-permute-done.67 = bf16[4,2,96,768]{3,2,0,1:T(8,128)(2,1)S(1)} collective-permute-done((bf16[4,2,96,768]{3,2,0,1:T(8,128)(2,1)S(1)}, bf16[4,2,96,768]{3,2,0,1:T(8,128)(2,1)S(1)}, u32[]{:S(2)}, u32[]{:S(2)}) %collective-permute-start.67) | collective-permute-done | bytes 1179680 | tf_op jit(solution)/shard_map/ppermute | solution.py:203
  554.1 2.9 collective-permute-done.61
  559.9 9.7 %collective-permute-done.47 = bf16[512,768]{0,1:T(8,128)(2,1)S(1)} collective-permute-done((bf16[512,768]{0,1:T(8,128)(2,1)S(1)}, bf16[512,768]{0,1:T(8,128)(2,1)S(1)}, u32[]{:S(2)}, u32[]{:S(2)}) %collective-permute-start.47) | collective-permute-done | bytes 786464 | tf_op jit(solution)/shard_map/ppermute | solution.py:321
  571.0 2.6 copy.240
  575.3 2.0 collective-permute-start.69
  579.7 2.2 collective-permute-done.62
  583.2 2.0 collective-permute-start.63
  587.7 6.2 %collective-permute-done.70 = bf16[96,768]{1,0:T(8,128)(2,1)S(1)} collective-permute-done((bf16[96,768]{1,0:T(8,128)(2,1)S(1)}, bf16[96,768]{1,0:T(8,128)(2,1)S(1)}, u32[]{:S(2)}, u32[]{:S(2)}) %collective-permute-start.70) | collective-permute-done | bytes 147488 | tf_op jit(solution)/shard_map/ppermute | solution.py:203
  594.6 6.7 %collective-permute-done.64 = bf16[24,3072]{1,0:T(8,128)(2,1)S(1)} collective-permute-done((bf16[24,3072]{1,0:T(8,128)(2,1)S(1)}, bf16[24,3072]{1,0:T(8,128)(2,1)S(1)}, u32[]{:S(2)}, u32[]{:S(2)}) %collective-permute-start.64) | collective-permute-done | bytes 147488 | tf_op jit(solution)/shard_map/ppermute | solution.py:203
  (402 shorter events, 142.3 us)
Async XLA Ops:
  0.8 74.5 %collective-permute-start.33 = (bf16[96,768]{1,0:T(8,128)(2,1)}, bf16[96,768]{1,0:T(8,128)(2,1)S(1)}, u32[]{:S(2)}, u32[]{:S(2)}) collective-permute-start(bf16[96,768]{1,0:T(8,128)(2,1)} %param.28), channel_id=1, source_target_pairs={{0,24},{1,25},{2,26},{3,27},{4,28},{5,29},{6,30},{7,31},{8,0},{9,1... | collective-permute-start | bytes 442376 | tf_op jit(solution)/shard_map/ppermute | solution.py:203
  5.9 71.0 %collective-permute-start.34 = (bf16[96,768]{1,0:T(8,128)(2,1)}, bf16[96,768]{1,0:T(8,128)(2,1)S(1)}, u32[]{:S(2)}, u32[]{:S(2)}) collective-permute-start(bf16[96,768]{1,0:T(8,128)(2,1)} %param.28), channel_id=1, source_target_pairs={{0,16},{1,17},{2,18},{3,19},{4,20},{5,21},{6,22},{7,23},{8,24},{9,... | collective-permute-start | bytes 442376 | tf_op jit(solution)/shard_map/ppermute | solution.py:203
  5.9 72.6 %collective-permute-start.35 = (bf16[96,768]{1,0:T(8,128)(2,1)}, bf16[96,768]{1,0:T(8,128)(2,1)S(1)}, u32[]{:S(2)}, u32[]{:S(2)}) collective-permute-start(bf16[96,768]{1,0:T(8,128)(2,1)} %param.28), channel_id=1, source_target_pairs={{0,8},{1,9},{2,10},{3,11},{4,12},{5,13},{6,14},{7,15},{8,16},{9,17... | collective-permute-start | bytes 442376 | tf_op jit(solution)/shard_map/ppermute | solution.py:203
  7.0 18.0 %collective-permute-start.13 = (bf16[24,768]{1,0:T(8,128)(2,1)}, bf16[24,768]{1,0:T(8,128)(2,1)S(1)}, u32[]{:S(2)}, u32[]{:S(2)}) collective-permute-start(bf16[24,768]{1,0:T(8,128)(2,1)} %param.26), channel_id=1, source_target_pairs={{0,24},{1,25},{2,26},{3,27},{4,28},{5,29},{6,30},{7,31},{8,0},{9,1... | collective-permute-start | bytes 110600 | tf_op jit(solution)/shard_map/ppermute | solution.py:203
  9.8 17.9 %collective-permute-start.14 = (bf16[24,768]{1,0:T(8,128)(2,1)}, bf16[24,768]{1,0:T(8,128)(2,1)S(1)}, u32[]{:S(2)}, u32[]{:S(2)}) collective-permute-start(bf16[24,768]{1,0:T(8,128)(2,1)} %param.26), channel_id=1, source_target_pairs={{0,16},{1,17},{2,18},{3,19},{4,20},{5,21},{6,22},{7,23},{8,24},{9,... | collective-permute-start | bytes 110600 | tf_op jit(solution)/shard_map/ppermute | solution.py:203
  15.1 123.2 %all-to-all-start = ((bf16[2,512,768]{2,0,1:T(2,128)(2,1)}), bf16[2,512,768]{2,0,1:T(2,128)(2,1)S(1)}, u32[]{:S(2)}, u32[]{:S(2)}) async-start(bf16[2,512,768]{2,0,1:T(2,128)(2,1)} %copy.220), calls=%async_computation | async-start | bytes 3145728 | tf_op jit(solution)/shard_map/all_to_all | solution.py:442
  25.0 24.5 %collective-permute-start.15 = (bf16[24,768]{1,0:T(8,128)(2,1)S(1)}, bf16[24,768]{1,0:T(8,128)(2,1)S(1)}, u32[]{:S(2)}, u32[]{:S(2)}) collective-permute-start(bf16[24,768]{1,0:T(8,128)(2,1)S(1)} %copy-done.25), channel_id=1, source_target_pairs={{0,8},{1,9},{2,10},{3,11},{4,12},{5,13},{6,14},{7,15},{8,16},{9,17... | collective-permute-start | bytes 110600 | tf_op jit(solution)/shard_map/ppermute | solution.py:203
  27.7 37.0 %collective-permute-start.2 = (bf16[24,2432]{1,0:T(8,128)(2,1)S(1)}, bf16[24,2432]{1,0:T(8,128)(2,1)S(1)}, u32[]{:S(2)}, u32[]{:S(2)}) collective-permute-start(bf16[24,2432]{1,0:T(8,128)(2,1)S(1)} %fusion.45), channel_id=1, source_target_pairs={{0,24},{1,25},{2,26},{3,27},{4,28},{5,29},{6,30},{7,31},{8,0},{9,1... | collective-permute-start | bytes 350216 | tf_op jit(solution)/shard_map/ppermute | solution.py:203
  49.5 16.1 %collective-permute-start.3 = (bf16[24,2432]{1,0:T(8,128)(2,1)S(1)}, bf16[24,2432]{1,0:T(8,128)(2,1)S(1)}, u32[]{:S(2)}, u32[]{:S(2)}) collective-permute-start(bf16[24,2432]{1,0:T(8,128)(2,1)S(1)} %fusion.45), channel_id=1, source_target_pairs={{0,16},{1,17},{2,18},{3,19},{4,20},{5,21},{6,22},{7,23},{8,24},{9,... | collective-permute-start | bytes 350216 | tf_op jit(solution)/shard_map/ppermute | solution.py:203
  64.6 8.1 %collective-permute-start.4 = (bf16[24,2432]{1,0:T(8,128)(2,1)S(1)}, bf16[24,2432]{1,0:T(8,128)(2,1)S(1)}, u32[]{:S(2)}, u32[]{:S(2)}) collective-permute-start(bf16[24,2432]{1,0:T(8,128)(2,1)S(1)} %fusion.45), channel_id=1, source_target_pairs={{0,8},{1,9},{2,10},{3,11},{4,12},{5,13},{6,14},{7,15},{8,16},{9,17... | collective-permute-start | bytes 350216 | tf_op jit(solution)/shard_map/ppermute | solution.py:203
  65.6 9.7 %collective-permute-start.23 = (bf16[24,3072]{1,0:T(8,128)(2,1)S(1)}, bf16[24,3072]{1,0:T(8,128)(2,1)S(1)}, u32[]{:S(2)}, u32[]{:S(2)}) collective-permute-start(bf16[24,3072]{1,0:T(8,128)(2,1)S(1)} %copy-done.18), channel_id=1, source_target_pairs={{0,24},{1,25},{2,26},{3,27},{4,28},{5,29},{6,30},{7,31},{8,0},{9,1... | collective-permute-start | bytes 442376 | tf_op jit(solution)/shard_map/ppermute | solution.py:203
  75.3 16.3 %collective-permute-start.16 = (bf16[4,24,768]{2,1,0:T(8,128)(2,1)S(1)}, bf16[4,24,768]{2,1,0:T(8,128)(2,1)S(1)}, u32[]{:S(2)}, u32[]{:S(2)}) collective-permute-start(bf16[4,24,768]{2,1,0:T(8,128)(2,1)S(1)} %get-tuple-element.129), channel_id=1, source_target_pairs={{0,4},{1,5},{2,6},{3,7},{4,0},{5,1},{6,2},{7,3},{8,12},{9,13},{10,... | collective-permute-start | bytes 442376 | tf_op jit(solution)/shard_map/ppermute | solution.py:203
  76.9 14.7 %collective-permute-start.17 = (bf16[4,24,768]{2,1,0:T(8,128)(2,1)S(1)}, bf16[4,24,768]{2,1,0:T(8,128)(2,1)S(1)}, u32[]{:S(2)}, u32[]{:S(2)}) collective-permute-start(bf16[4,24,768]{2,1,0:T(8,128)(2,1)S(1)} %get-tuple-element.129), channel_id=1, source_target_pairs={{0,2},{1,3},{2,0},{3,1},{4,6},{5,7},{6,4},{7,5},{8,10},{9,11},{10,... | collective-permute-start | bytes 442376 | tf_op jit(solution)/shard_map/ppermute | solution.py:203
  78.5 20.0 %collective-permute-start.19 = (bf16[4,24,768]{2,1,0:T(8,128)(2,1)S(1)}, bf16[4,24,768]{2,1,0:T(8,128)(2,1)S(1)}, u32[]{:S(2)}, u32[]{:S(2)}) collective-permute-start(bf16[4,24,768]{2,1,0:T(8,128)(2,1)S(1)} %get-tuple-element.129), channel_id=1, source_target_pairs={{0,1},{1,0},{2,3},{3,2},{4,5},{5,4},{6,7},{7,6},{8,9},{9,8},{10,11... | collective-permute-start | bytes 442376 | tf_op jit(solution)/shard_map/ppermute | solution.py:203
  80.0 25.9 %collective-permute-start.6 = (bf16[4,24,2432]{2,1,0:T(8,128)(2,1)S(1)}, bf16[4,24,2432]{2,1,0:T(8,128)(2,1)}, u32[]{:S(2)}, u32[]{:S(2)}) collective-permute-start(bf16[4,24,2432]{2,1,0:T(8,128)(2,1)S(1)} %constant_dynamic-slice_fusion.49), channel_id=1, source_target_pairs={{0,4},{1,5},{2,6},{3,7},{4,0},{5,1},{6,2},{7,3},{8,12},{9,13},{10,... | collective-permute-start | bytes 1400840 | tf_op jit(solution)/shard_map/ppermute | solution.py:203
  82.2 22.2 %collective-permute-start.8 = (bf16[4,24,2432]{2,1,0:T(8,128)(2,1)S(1)}, bf16[4,24,2432]{2,1,0:T(8,128)(2,1)S(1)}, u32[]{:S(2)}, u32[]{:S(2)}) collective-permute-start(bf16[4,24,2432]{2,1,0:T(8,128)(2,1)S(1)} %constant_dynamic-slice_fusion.49), channel_id=1, source_target_pairs={{0,2},{1,3},{2,0},{3,1},{4,6},{5,7},{6,4},{7,5},{8,10},{9,11},{10,... | collective-permute-start | bytes 1400840 | tf_op jit(solution)/shard_map/ppermute | solution.py:203
  91.6 11.2 %collective-permute-start.5 = (bf16[4,24,1280]{2,1,0:T(8,128)(2,1)S(1)}, bf16[4,24,1280]{2,1,0:T(8,128)(2,1)S(1)}, u32[]{:S(2)}, u32[]{:S(2)}) collective-permute-start(bf16[4,24,1280]{2,1,0:T(8,128)(2,1)S(1)} %pad_maximum_fusion.5), channel_id=1, source_target_pairs={{0,1},{1,0},{2,3},{3,2},{4,5},{5,4},{6,7},{7,6},{8,9},{9,8},{10,11... | collective-permute-start | bytes 737288 | tf_op jit(solution)/shard_map/ppermute | solution.py:203
  98.0 16.5 %collective-permute-start.36 = (bf16[4,96,768]{2,1,0:T(8,128)(2,1)}, bf16[4,96,768]{2,1,0:T(8,128)(2,1)}, u32[]{:S(2)}, u32[]{:S(2)}) collective-permute-start(bf16[4,96,768]{2,1,0:T(8,128)(2,1)} %get-tuple-element.125), channel_id=1, source_target_pairs={{0,2},{1,3},{2,0},{3,1},{4,6},{5,7},{6,4},{7,5},{8,10},{9,11},{10,... | collective-permute-start | bytes 1769480 | tf_op jit(solution)/shard_map/ppermute | solution.py:203
  101.3 30.5 %collective-permute-start.37 = (bf16[4,96,768]{2,1,0:T(8,128)(2,1)}, bf16[4,96,768]{2,1,0:T(8,128)(2,1)}, u32[]{:S(2)}, u32[]{:S(2)}) collective-permute-start(bf16[4,96,768]{2,1,0:T(8,128)(2,1)} %get-tuple-element.125), channel_id=1, source_target_pairs={{0,4},{1,5},{2,6},{3,7},{4,0},{5,1},{6,2},{7,3},{8,12},{9,13},{10,... | collective-permute-start | bytes 1769480 | tf_op jit(solution)/shard_map/ppermute | solution.py:203
  104.3 84.4 %collective-permute-start.39 = (bf16[4,96,768]{2,1,0:T(8,128)(2,1)}, bf16[4,96,768]{2,1,0:T(8,128)(2,1)}, u32[]{:S(2)}, u32[]{:S(2)}) collective-permute-start(bf16[4,96,768]{2,1,0:T(8,128)(2,1)} %get-tuple-element.125), channel_id=1, source_target_pairs={{0,1},{1,0},{2,3},{3,2},{4,5},{5,4},{6,7},{7,6},{8,9},{9,8},{10,11... | collective-permute-start | bytes 1769480 | tf_op jit(solution)/shard_map/ppermute | solution.py:203
  104.4 25.1 %collective-permute-start.26 = (bf16[4,24,3072]{2,1,0:T(8,128)(2,1)}, bf16[4,24,3072]{2,1,0:T(8,128)(2,1)S(1)}, u32[]{:S(2)}, u32[]{:S(2)}) collective-permute-start(bf16[4,24,3072]{2,1,0:T(8,128)(2,1)} %get-tuple-element.127), channel_id=1, source_target_pairs={{0,4},{1,5},{2,6},{3,7},{4,0},{5,1},{6,2},{7,3},{8,12},{9,13},{10,... | collective-permute-start | bytes 1769480 | tf_op jit(solution)/shard_map/ppermute | solution.py:203
  105.9 24.6 %collective-permute-start.27 = (bf16[4,24,3072]{2,1,0:T(8,128)(2,1)}, bf16[4,24,3072]{2,1,0:T(8,128)(2,1)S(1)}, u32[]{:S(2)}, u32[]{:S(2)}) collective-permute-start(bf16[4,24,3072]{2,1,0:T(8,128)(2,1)} %get-tuple-element.127), channel_id=1, source_target_pairs={{0,2},{1,3},{2,0},{3,1},{4,6},{5,7},{6,4},{7,5},{8,10},{9,11},{10,... | collective-permute-start | bytes 1769480 | tf_op jit(solution)/shard_map/ppermute | solution.py:203
  114.5 70.0 %collective-permute-start.29 = (bf16[4,24,3072]{2,1,0:T(8,128)(2,1)}, bf16[4,24,3072]{2,1,0:T(8,128)(2,1)}, u32[]{:S(2)}, u32[]{:S(2)}) collective-permute-start(bf16[4,24,3072]{2,1,0:T(8,128)(2,1)} %get-tuple-element.127), channel_id=1, source_target_pairs={{0,1},{1,0},{2,3},{3,2},{4,5},{5,4},{6,7},{7,6},{8,9},{9,8},{10,11... | collective-permute-start | bytes 1769480 | tf_op jit(solution)/shard_map/ppermute | solution.py:203
  129.6 17.3 %collective-permute-start.9 = (bf16[4,24,1280]{2,1,0:T(8,128)(2,1)}, bf16[4,24,1280]{2,1,0:T(8,128)(2,1)S(1)}, u32[]{:S(2)}, u32[]{:S(2)}) collective-permute-start(bf16[4,24,1280]{2,1,0:T(8,128)(2,1)} %pad_maximum_fusion.9), channel_id=1, source_target_pairs={{0,1},{1,0},{2,3},{3,2},{4,5},{5,4},{6,7},{7,6},{8,9},{9,8},{10,11... | collective-permute-start | bytes 737288 | tf_op jit(solution)/shard_map/ppermute | solution.py:203
  131.8 13.1 %collective-permute-start.10 = (bf16[4,24,2432]{2,1,0:T(8,128)(2,1)}, bf16[4,24,2432]{2,1,0:T(8,128)(2,1)}, u32[]{:S(2)}, u32[]{:S(2)}) collective-permute-start(bf16[4,24,2432]{2,1,0:T(8,128)(2,1)} %collective-permute-done.6), channel_id=1, source_target_pairs={{0,2},{1,3},{2,0},{3,1},{4,6},{5,7},{6,4},{7,5},{8,10},{9,11},{10,... | collective-permute-start | bytes 1400840 | tf_op jit(solution)/shard_map/ppermute | solution.py:203
  135.3 51.5 %collective-permute-start.38 = (bf16[4,96,768]{2,1,0:T(8,128)(2,1)}, bf16[4,96,768]{2,1,0:T(8,128)(2,1)}, u32[]{:S(2)}, u32[]{:S(2)}) collective-permute-start(bf16[4,96,768]{2,1,0:T(8,128)(2,1)} %collective-permute-done.36), channel_id=1, source_target_pairs={{0,4},{1,5},{2,6},{3,7},{4,0},{5,1},{6,2},{7,3},{8,12},{9,13},{10,... | collective-permute-start | bytes 1769480 | tf_op jit(solution)/shard_map/ppermute | solution.py:203
  140.6 40.9 %all-to-all-start.1 = ((bf16[16,64,768]{2,1,0:T(8,128)(2,1)}), bf16[16,64,768]{2,1,0:T(8,128)(2,1)S(1)}, u32[]{:S(2)}, u32[]{:S(2)}) async-start(bf16[16,64,768]{2,1,0:T(8,128)(2,1)} %broadcast_select_fusion), calls=%async_computation.1 | async-start | bytes 3145728 | tf_op jit(solution)/shard_map/all_to_all | solution.py:444
  144.9 46.2 %collective-permute-start.40 = (bf16[4,96,768]{2,1,0:T(8,128)(2,1)}, bf16[4,96,768]{2,1,0:T(8,128)(2,1)}, u32[]{:S(2)}, u32[]{:S(2)}) collective-permute-start(bf16[4,96,768]{2,1,0:T(8,128)(2,1)} %collective-permute-done.36), channel_id=1, source_target_pairs={{0,1},{1,0},{2,3},{3,2},{4,5},{5,4},{6,7},{7,6},{8,9},{9,8},{10,11... | collective-permute-start | bytes 1769480 | tf_op jit(solution)/shard_map/ppermute | solution.py:203
  148.9 15.3 %collective-permute-start.28 = (bf16[4,24,3072]{2,1,0:T(8,128)(2,1)S(1)}, bf16[4,24,3072]{2,1,0:T(8,128)(2,1)S(1)}, u32[]{:S(2)}, u32[]{:S(2)}) collective-permute-start(bf16[4,24,3072]{2,1,0:T(8,128)(2,1)S(1)} %copy-done.14), channel_id=1, source_target_pairs={{0,2},{1,3},{2,0},{3,1},{4,6},{5,7},{6,4},{7,5},{8,10},{9,11},{10,... | collective-permute-start | bytes 1769480 | tf_op jit(solution)/shard_map/ppermute | solution.py:203
  164.2 40.2 %collective-permute-start.41 = (bf16[4,96,768]{2,1,0:T(8,128)(2,1)}, bf16[4,96,768]{2,1,0:T(8,128)(2,1)}, u32[]{:S(2)}, u32[]{:S(2)}) collective-permute-start(bf16[4,96,768]{2,1,0:T(8,128)(2,1)} %collective-permute-done.37), channel_id=1, source_target_pairs={{0,1},{1,0},{2,3},{3,2},{4,5},{5,4},{6,7},{7,6},{8,9},{9,8},{10,11... | collective-permute-start | bytes 1769480 | tf_op jit(solution)/shard_map/ppermute | solution.py:203
  184.5 18.5 %collective-permute-start = (bf16[512,768]{0,1:T(8,128)(2,1)}, bf16[512,768]{0,1:T(8,128)(2,1)}, u32[]{:S(2)}, u32[]{:S(2)}) collective-permute-start(bf16[512,768]{0,1:T(8,128)(2,1)} %bitcast.385), channel_id=1, source_target_pairs={{0,2},{1,3},{2,0},{3,1},{4,6},{5,7},{6,4},{7,5},{8,10},{9,11},{10,... | collective-permute-start | bytes 2359304 | tf_op jit(solution)/shard_map/ppermute | solution.py:317
  186.7 20.2 %collective-permute-start.30 = (bf16[4,24,3072]{2,1,0:T(8,128)(2,1)}, bf16[4,24,3072]{2,1,0:T(8,128)(2,1)}, u32[]{:S(2)}, u32[]{:S(2)}) collective-permute-start(bf16[4,24,3072]{2,1,0:T(8,128)(2,1)} %copy-done.13), channel_id=1, source_target_pairs={{0,1},{1,0},{2,3},{3,2},{4,5},{5,4},{6,7},{7,6},{8,9},{9,8},{10,11... | collective-permute-start | bytes 1769480 | tf_op jit(solution)/shard_map/ppermute | solution.py:203
  188.6 20.2 %collective-permute-start.31 = (bf16[4,24,3072]{2,1,0:T(8,128)(2,1)}, bf16[4,24,3072]{2,1,0:T(8,128)(2,1)}, u32[]{:S(2)}, u32[]{:S(2)}) collective-permute-start(bf16[4,24,3072]{2,1,0:T(8,128)(2,1)} %copy-done.15), channel_id=1, source_target_pairs={{0,1},{1,0},{2,3},{3,2},{4,5},{5,4},{6,7},{7,6},{8,9},{9,8},{10,11... | collective-permute-start | bytes 1769480 | tf_op jit(solution)/shard_map/ppermute | solution.py:203
  191.1 79.2 %collective-permute-start.42 = (bf16[4,96,768]{2,1,0:T(8,128)(2,1)}, bf16[4,96,768]{2,1,0:T(8,128)(2,1)}, u32[]{:S(2)}, u32[]{:S(2)}) collective-permute-start(bf16[4,96,768]{2,1,0:T(8,128)(2,1)} %collective-permute-done.38), channel_id=1, source_target_pairs={{0,1},{1,0},{2,3},{3,2},{4,5},{5,4},{6,7},{7,6},{8,9},{9,8},{10,11... | collective-permute-start | bytes 1769480 | tf_op jit(solution)/shard_map/ppermute | solution.py:203
  203.0 69.3 %collective-permute-start.32 = (bf16[4,24,3072]{2,1,0:T(8,128)(2,1)}, bf16[4,24,3072]{2,1,0:T(8,128)(2,1)S(1)}, u32[]{:S(2)}, u32[]{:S(2)}) collective-permute-start(bf16[4,24,3072]{2,1,0:T(8,128)(2,1)} %copy-done.16), channel_id=1, source_target_pairs={{0,1},{1,0},{2,3},{3,2},{4,5},{5,4},{6,7},{7,6},{8,9},{9,8},{10,11... | collective-permute-start | bytes 1769480 | tf_op jit(solution)/shard_map/ppermute | solution.py:203
  274.3 25.0 %collective-permute-start.44 = (bf16[512,768]{0,1:T(8,128)(2,1)}, bf16[512,768]{0,1:T(8,128)(2,1)S(1)}, u32[]{:S(2)}, u32[]{:S(2)}) collective-permute-start(bf16[512,768]{0,1:T(8,128)(2,1)} %bitcast.386), channel_id=1, source_target_pairs={{0,2},{1,3},{2,0},{3,1},{4,6},{5,7},{6,4},{7,5},{8,10},{9,11},{10,... | collective-permute-start | bytes 2359304 | tf_op jit(solution)/shard_map/ppermute | solution.py:317
  344.9 18.8 %collective-permute-start.45 = (bf16[1024,384]{1,0:T(8,128)(2,1)}, bf16[1024,384]{1,0:T(8,128)(2,1)}, u32[]{:S(2)}, u32[]{:S(2)}) collective-permute-start(bf16[1024,384]{1,0:T(8,128)(2,1)} %get-tuple-element.134), channel_id=1, source_target_pairs={{0,1},{1,0},{2,3},{3,2},{4,5},{5,4},{6,7},{7,6},{8,9},{9,8},{10,11... | collective-permute-start | bytes 2359304 | tf_op jit(solution)/shard_map/ppermute | solution.py:358
  351.8 168.4 %collective-permute-start.66 = (bf16[4,2,2,96,768]{4,3,0,1,2:T(8,128)(2,1)}, bf16[4,2,2,96,768]{4,3,0,1,2:T(8,128)(2,1)}, u32[]{:S(2)}, u32[]{:S(2)}) collective-permute-start(bf16[4,2,2,96,768]{4,3,0,1,2:T(8,128)(2,1)} %fusion.9), channel_id=1, source_target_pairs={{0,1},{1,0},{2,3},{3,2},{4,5},{5,4},{6,7},{7,6},{8,9},{9,8},{10,11... | collective-permute-start | bytes 7077896 | tf_op jit(solution)/shard_map/ppermute | solution.py:203
  356.6 116.9 %collective-permute-start.43 = (bf16[512,768]{0,1:T(8,128)(2,1)}, bf16[512,768]{0,1:T(8,128)(2,1)}, u32[]{:S(2)}, u32[]{:S(2)}) collective-permute-start(bf16[512,768]{0,1:T(8,128)(2,1)} %get-tuple-element.138), channel_id=1, source_target_pairs={{0,2},{1,3},{2,0},{3,1},{4,6},{5,7},{6,4},{7,5},{8,10},{9,11},{10,... | collective-permute-start | bytes 2359304 | tf_op jit(solution)/shard_map/ppermute | solution.py:321
  447.7 11.2 %collective-permute-start.72 = (f32[4,2,2,1,288]{4,3,2,1,0:T(1,128)S(1)}, f32[4,2,2,1,288]{4,3,2,1,0:T(1,128)S(1)}, u32[]{:S(2)}, u32[]{:S(2)}) collective-permute-start(f32[4,2,2,1,288]{4,3,2,1,0:T(1,128)S(1)} %fusion.56), channel_id=1, source_target_pairs={{0,1},{1,0},{2,3},{3,2},{4,5},{5,4},{6,7},{7,6},{8,9},{9,8},{10,11... | collective-permute-start | bytes 55304 | tf_op jit(solution)/shard_map/ppermute | solution.py:203
  468.5 24.0 %collective-permute-start.48 = (bf16[4,2,48,1152]{3,2,0,1:T(8,128)(2,1)}, bf16[4,2,48,1152]{3,2,0,1:T(8,128)(2,1)}, u32[]{:S(2)}, u32[]{:S(2)}) collective-permute-start(bf16[4,2,48,1152]{3,2,0,1:T(8,128)(2,1)} %fusion.16), channel_id=1, source_target_pairs={{0,4},{1,5},{2,6},{3,7},{4,0},{5,1},{6,2},{7,3},{8,12},{9,13},{10,... | collective-permute-start | bytes 2654216 | tf_op jit(solution)/shard_map/ppermute | solution.py:203
  470.4 10.6 %collective-permute-start.75 = (f32[1,288]{1,0:T(1,128)S(1)}, f32[1,288]{1,0:T(1,128)S(1)}, u32[]{:S(2)}, u32[]{:S(2)}) collective-permute-start(f32[1,288]{1,0:T(1,128)S(1)} %get-tuple-element.192), channel_id=1, source_target_pairs={{0,8},{1,9},{2,10},{3,11},{4,12},{5,13},{6,14},{7,15},{8,16},{9,17... | collective-permute-start | bytes 3464 | tf_op jit(solution)/shard_map/ppermute | solution.py:203
  470.5 10.6 %collective-permute-start.76 = (f32[1,288]{1,0:T(1,128)S(1)}, f32[1,288]{1,0:T(1,128)S(1)}, u32[]{:S(2)}, u32[]{:S(2)}) collective-permute-start(f32[1,288]{1,0:T(1,128)S(1)} %get-tuple-element.194), channel_id=1, source_target_pairs={{0,16},{1,17},{2,18},{3,19},{4,20},{5,21},{6,22},{7,23},{8,24},{9,... | collective-permute-start | bytes 3464 | tf_op jit(solution)/shard_map/ppermute | solution.py:203
  473.5 7.9 %collective-permute-start.77 = (f32[1,288]{1,0:T(1,128)S(1)}, f32[1,288]{1,0:T(1,128)S(1)}, u32[]{:S(2)}, u32[]{:S(2)}) collective-permute-start(f32[1,288]{1,0:T(1,128)S(1)} %get-tuple-element.193), channel_id=1, source_target_pairs={{0,24},{1,25},{2,26},{3,27},{4,28},{5,29},{6,30},{7,31},{8,0},{9,1... | collective-permute-start | bytes 3464 | tf_op jit(solution)/shard_map/ppermute | solution.py:203
  481.0 43.1 %collective-permute-start.60 = (bf16[4,2,2,24,3072]{4,3,0,2,1:T(8,128)(2,1)}, bf16[4,2,2,24,3072]{4,3,0,2,1:T(8,128)(2,1)}, u32[]{:S(2)}, u32[]{:S(2)}) collective-permute-start(bf16[4,2,2,24,3072]{4,3,0,2,1:T(8,128)(2,1)} %fusion.8), channel_id=1, source_target_pairs={{0,1},{1,0},{2,3},{3,2},{4,5},{5,4},{6,7},{7,6},{8,9},{9,8},{10,11... | collective-permute-start | bytes 7077896 | tf_op jit(solution)/shard_map/ppermute | solution.py:203
  481.0 9.4 %collective-permute-start.55 = (bf16[4,2,24,768]{3,2,0,1:T(8,128)(2,1)S(1)}, bf16[4,2,24,768]{3,2,0,1:T(8,128)(2,1)S(1)}, u32[]{:S(2)}, u32[]{:S(2)}) collective-permute-start(bf16[4,2,24,768]{3,2,0,1:T(8,128)(2,1)S(1)} %fusion.21), channel_id=1, source_target_pairs={{0,2},{1,3},{2,0},{3,1},{4,6},{5,7},{6,4},{7,5},{8,10},{9,11},{10,... | collective-permute-start | bytes 884744 | tf_op jit(solution)/shard_map/ppermute | solution.py:203
  494.4 11.6 %collective-permute-start.49 = (bf16[4,48,1152]{2,1,0:T(8,128)(2,1)S(1)}, bf16[4,48,1152]{2,1,0:T(8,128)(2,1)S(1)}, u32[]{:S(2)}, u32[]{:S(2)}) collective-permute-start(bf16[4,48,1152]{2,1,0:T(8,128)(2,1)S(1)} %fusion.20), channel_id=1, source_target_pairs={{0,2},{1,3},{2,0},{3,1},{4,6},{5,7},{6,4},{7,5},{8,10},{9,11},{10,... | collective-permute-start | bytes 1327112 | tf_op jit(solution)/shard_map/ppermute | solution.py:203
  497.2 10.2 %collective-permute-start.57 = (bf16[24,768]{1,0:T(8,128)(2,1)S(1)}, bf16[24,768]{1,0:T(8,128)(2,1)S(1)}, u32[]{:S(2)}, u32[]{:S(2)}) collective-permute-start(bf16[24,768]{1,0:T(8,128)(2,1)S(1)} %get-tuple-element.176), channel_id=1, source_target_pairs={{0,8},{1,9},{2,10},{3,11},{4,12},{5,13},{6,14},{7,15},{8,16},{9,17... | collective-permute-start | bytes 110600 | tf_op jit(solution)/shard_map/ppermute | solution.py:203
  498.5 9.8 %collective-permute-start.58 = (bf16[24,768]{1,0:T(8,128)(2,1)S(1)}, bf16[24,768]{1,0:T(8,128)(2,1)S(1)}, u32[]{:S(2)}, u32[]{:S(2)}) collective-permute-start(bf16[24,768]{1,0:T(8,128)(2,1)S(1)} %get-tuple-element.178), channel_id=1, source_target_pairs={{0,16},{1,17},{2,18},{3,19},{4,20},{5,21},{6,22},{7,23},{8,24},{9,... | collective-permute-start | bytes 110600 | tf_op jit(solution)/shard_map/ppermute | solution.py:203
  507.4 7.8 %collective-permute-start.50 = (bf16[48,1152]{1,0:T(8,128)(2,1)S(1)}, bf16[48,1152]{1,0:T(8,128)(2,1)S(1)}, u32[]{:S(2)}, u32[]{:S(2)}) collective-permute-start(bf16[48,1152]{1,0:T(8,128)(2,1)S(1)} %get-tuple-element.149), channel_id=1, source_target_pairs={{0,8},{1,9},{2,10},{3,11},{4,12},{5,13},{6,14},{7,15},{8,16},{9,17... | collective-permute-start | bytes 331784 | tf_op jit(solution)/shard_map/ppermute | solution.py:203
  508.3 9.9 %collective-permute-start.51 = (bf16[48,1152]{1,0:T(8,128)(2,1)S(1)}, bf16[48,1152]{1,0:T(8,128)(2,1)S(1)}, u32[]{:S(2)}, u32[]{:S(2)}) collective-permute-start(bf16[48,1152]{1,0:T(8,128)(2,1)S(1)} %get-tuple-element.151), channel_id=1, source_target_pairs={{0,16},{1,17},{2,18},{3,19},{4,20},{5,21},{6,22},{7,23},{8,24},{9,... | collective-permute-start | bytes 331784 | tf_op jit(solution)/shard_map/ppermute | solution.py:203
  515.3 14.5 %collective-permute-start.46 = (bf16[1024,768]{0,1:T(8,128)(2,1)}, bf16[1024,768]{0,1:T(8,128)(2,1)}, u32[]{:S(2)}, u32[]{:S(2)}) collective-permute-start(bf16[1024,768]{0,1:T(8,128)(2,1)} %slice.250), channel_id=1, source_target_pairs={{0,1},{1,0},{2,3},{3,2},{4,5},{5,4},{6,7},{7,6},{8,9},{9,8},{10,11... | collective-permute-start | bytes 4718600 | tf_op jit(solution)/shard_map/ppermute | solution.py:487
  520.1 9.6 %collective-permute-start.53 = (f32[24,3,384]{2,0,1:T(8,128)S(1)}, f32[24,3,384]{2,0,1:T(8,128)S(1)}, u32[]{:S(2)}, u32[]{:S(2)}) collective-permute-start(f32[24,3,384]{2,0,1:T(8,128)S(1)} %bitcast.389), channel_id=1, source_target_pairs={{0,1},{1,0},{2,3},{3,2},{4,5},{5,4},{6,7},{7,6},{8,9},{9,8},{10,11... | collective-permute-start | bytes 331784 | tf_op jit(solution)/shard_map/ppermute | solution.py:203
  524.0 28.8 %collective-permute-start.67 = (bf16[4,2,96,768]{3,2,0,1:T(8,128)(2,1)S(1)}, bf16[4,2,96,768]{3,2,0,1:T(8,128)(2,1)S(1)}, u32[]{:S(2)}, u32[]{:S(2)}) collective-permute-start(bf16[4,2,96,768]{3,2,0,1:T(8,128)(2,1)S(1)} %fusion.15), channel_id=1, source_target_pairs={{0,2},{1,3},{2,0},{3,1},{4,6},{5,7},{6,4},{7,5},{8,10},{9,11},{10,... | collective-permute-start | bytes 3538952 | tf_op jit(solution)/shard_map/ppermute | solution.py:203
  528.2 28.9 %collective-permute-start.61 = (bf16[4,2,24,3072]{3,2,0,1:T(8,128)(2,1)S(1)}, bf16[4,2,24,3072]{3,2,0,1:T(8,128)(2,1)S(1)}, u32[]{:S(2)}, u32[]{:S(2)}) collective-permute-start(bf16[4,2,24,3072]{3,2,0,1:T(8,128)(2,1)S(1)} %fusion.14), channel_id=1, source_target_pairs={{0,4},{1,5},{2,6},{3,7},{4,0},{5,1},{6,2},{7,3},{8,12},{9,13},{10,... | collective-permute-start | bytes 3538952 | tf_op jit(solution)/shard_map/ppermute | solution.py:203
  532.3 37.3 %collective-permute-start.47 = (bf16[512,768]{0,1:T(8,128)(2,1)S(1)}, bf16[512,768]{0,1:T(8,128)(2,1)S(1)}, u32[]{:S(2)}, u32[]{:S(2)}) collective-permute-start(bf16[512,768]{0,1:T(8,128)(2,1)S(1)} %get-tuple-element.132), channel_id=1, source_target_pairs={{0,2},{1,3},{2,0},{3,1},{4,6},{5,7},{6,4},{7,5},{8,10},{9,11},{10,... | collective-permute-start | bytes 2359304 | tf_op jit(solution)/shard_map/ppermute | solution.py:321
  553.1 20.5 %collective-permute-start.68 = (bf16[4,96,768]{2,1,0:T(8,128)(2,1)S(1)}, bf16[4,96,768]{2,1,0:T(8,128)(2,1)}, u32[]{:S(2)}, u32[]{:S(2)}) collective-permute-start(bf16[4,96,768]{2,1,0:T(8,128)(2,1)S(1)} %fusion.18), channel_id=1, source_target_pairs={{0,4},{1,5},{2,6},{3,7},{4,0},{5,1},{6,2},{7,3},{8,12},{9,13},{10,... | collective-permute-start | bytes 1769480 | tf_op jit(solution)/shard_map/ppermute | solution.py:203
  557.4 24.6 %collective-permute-start.62 = (bf16[4,24,3072]{2,1,0:T(8,128)(2,1)S(1)}, bf16[4,24,3072]{2,1,0:T(8,128)(2,1)}, u32[]{:S(2)}, u32[]{:S(2)}) collective-permute-start(bf16[4,24,3072]{2,1,0:T(8,128)(2,1)S(1)} %fusion.17), channel_id=1, source_target_pairs={{0,2},{1,3},{2,0},{3,1},{4,6},{5,7},{6,4},{7,5},{8,10},{9,11},{10,... | collective-permute-start | bytes 1769480 | tf_op jit(solution)/shard_map/ppermute | solution.py:203
  575.3 11.5 %collective-permute-start.69 = (bf16[96,768]{1,0:T(8,128)(2,1)S(1)}, bf16[96,768]{1,0:T(8,128)(2,1)S(1)}, u32[]{:S(2)}, u32[]{:S(2)}) collective-permute-start(bf16[96,768]{1,0:T(8,128)(2,1)S(1)} %get-tuple-element.143), channel_id=1, source_target_pairs={{0,8},{1,9},{2,10},{3,11},{4,12},{5,13},{6,14},{7,15},{8,16},{9,17... | collective-permute-start | bytes 442376 | tf_op jit(solution)/shard_map/ppermute | solution.py:203
  577.3 16.6 %collective-permute-start.70 = (bf16[96,768]{1,0:T(8,128)(2,1)S(1)}, bf16[96,768]{1,0:T(8,128)(2,1)S(1)}, u32[]{:S(2)}, u32[]{:S(2)}) collective-permute-start(bf16[96,768]{1,0:T(8,128)(2,1)S(1)} %get-tuple-element.145), channel_id=1, source_target_pairs={{0,16},{1,17},{2,18},{3,19},{4,20},{5,21},{6,22},{7,23},{8,24},{9,... | collective-permute-start | bytes 442376 | tf_op jit(solution)/shard_map/ppermute | solution.py:203
  578.8 15.1 %collective-permute-start.71 = (bf16[96,768]{1,0:T(8,128)(2,1)S(1)}, bf16[96,768]{1,0:T(8,128)(2,1)S(1)}, u32[]{:S(2)}, u32[]{:S(2)}) collective-permute-start(bf16[96,768]{1,0:T(8,128)(2,1)S(1)} %get-tuple-element.144), channel_id=1, source_target_pairs={{0,24},{1,25},{2,26},{3,27},{4,28},{5,29},{6,30},{7,31},{8,0},{9,1... | collective-permute-start | bytes 442376 | tf_op jit(solution)/shard_map/ppermute | solution.py:203
  583.2 11.4 %collective-permute-start.63 = (bf16[24,3072]{1,0:T(8,128)(2,1)S(1)}, bf16[24,3072]{1,0:T(8,128)(2,1)S(1)}, u32[]{:S(2)}, u32[]{:S(2)}) collective-permute-start(bf16[24,3072]{1,0:T(8,128)(2,1)S(1)} %get-tuple-element.146), channel_id=1, source_target_pairs={{0,8},{1,9},{2,10},{3,11},{4,12},{5,13},{6,14},{7,15},{8,16},{9,17... | collective-permute-start | bytes 442376 | tf_op jit(solution)/shard_map/ppermute | solution.py:203
  585.3 16.1 %collective-permute-start.64 = (bf16[24,3072]{1,0:T(8,128)(2,1)S(1)}, bf16[24,3072]{1,0:T(8,128)(2,1)S(1)}, u32[]{:S(2)}, u32[]{:S(2)}) collective-permute-start(bf16[24,3072]{1,0:T(8,128)(2,1)S(1)} %get-tuple-element.148), channel_id=1, source_target_pairs={{0,16},{1,17},{2,18},{3,19},{4,20},{5,21},{6,22},{7,23},{8,24},{9,... | collective-permute-start | bytes 442376 | tf_op jit(solution)/shard_map/ppermute | solution.py:203
  586.8 14.6 %collective-permute-start.65 = (bf16[24,3072]{1,0:T(8,128)(2,1)S(1)}, bf16[24,3072]{1,0:T(8,128)(2,1)S(1)}, u32[]{:S(2)}, u32[]{:S(2)}) collective-permute-start(bf16[24,3072]{1,0:T(8,128)(2,1)S(1)} %get-tuple-element.147), channel_id=1, source_target_pairs={{0,24},{1,25},{2,26},{3,27},{4,28},{5,29},{6,30},{7,31},{8,0},{9,1... | collective-permute-start | bytes 442376 | tf_op jit(solution)/shard_map/ppermute | solution.py:203
  (57 other events, 692.5 us)

commit v2 on v1

v2 whole, which is shorter than its diff:
```python
import functools
import math

import jax
import jax.numpy as jnp
from jax import lax
from jax.experimental import pallas as pl
from jax.experimental.pallas import tpu as pltpu
from jax.sharding import PartitionSpec as P

HEADS = 12
EPSILON = 1e-05
MASKED = -1e30
LOG2E = 1.4426950408889634
BOTH = ("dp", "fsdp")
NN = (((1,), (0,)), ((), ()))
NT = (((1,), (1,)), ((), ()))
TN = (((0,), (0,)), ((), ()))
f32 = jnp.float32
bf16 = jnp.bfloat16
LANES = 128


def dot(left, right, dims=NN, precision=None):
    return lax.dot_general(left, right, dims, preferred_element_type=f32, precision=precision)


def attend_kernel(q_ref, k_ref, v_ref, bias_ref, o_ref, lse_ref, k_even, k_odd, v_even, v_odd, *, scale):
    half = LANES // 2

    @pl.when(pl.program_id(1) == 0)
    def _():
        k, v, bias = k_ref[...], v_ref[...], bias_ref[...]
        low = lax.broadcasted_iota(jnp.int32, k.shape, 1) < half
        one = jnp.ones_like(v)
        k_even[...] = jnp.where(low, k, bias)
        k_odd[...] = jnp.where(low, bias, k)
        v_even[...] = jnp.where(low, v, one)
        v_odd[...] = jnp.where(low, one, v)

    q = q_ref[...]
    lane = lax.broadcasted_iota(jnp.int32, q.shape, 1)
    low = lane < half
    scaled = q * jnp.asarray(scale, bf16)
    one, zero = jnp.ones_like(q), jnp.zeros_like(q)
    q_even = jnp.where(low, scaled, jnp.where(lane == half, one, zero))
    q_odd = jnp.where(low, jnp.where(lane == 0, one, zero), scaled)

    def head(queries, keys, values):
        scores = dot(queries, keys[...], NT)
        top = jnp.max(scores, axis=1, keepdims=True)
        weights = jnp.exp2((scores - top) * LOG2E)
        return dot(weights.astype(bf16), values[...]), top

    out_even, top_even = head(q_even, k_even, v_even)
    out_odd, top_odd = head(q_odd, k_odd, v_odd)
    out = jnp.where(low, out_even, out_odd)
    total = jnp.where(low, pltpu.roll(out_even, half, 1), pltpu.roll(out_odd, half, 1))
    o_ref[...] = (out / total).astype(o_ref.dtype)
    lse = (jnp.where(low, top_even, top_odd) + jnp.log(total)) * LOG2E
    row = lax.broadcasted_iota(jnp.int32, (8, LANES), 0)
    col = lax.broadcasted_iota(jnp.int32, (8, LANES), 1)
    pick = jnp.where(col == row * half, 1.0, 0.0).astype(f32)
    lse_ref[0] = dot(pick, lse, NT, lax.Precision.HIGHEST)


def attend(qkv, bias, first, count, scale, block):
    rows = qkv.shape[0]
    whole = lambda n: pl.BlockSpec((rows, LANES), lambda h, i: (0, 3 * (first + h) + n))
    return pl.pallas_call(
        functools.partial(attend_kernel, scale=scale),
        grid=(count, rows // block),
        in_specs=[
            pl.BlockSpec((block, LANES), lambda h, i: (i, 3 * (first + h))),
            whole(1),
            whole(2),
            pl.BlockSpec((rows, LANES), lambda h, i: (0, 0)),
        ],
        out_specs=[
            pl.BlockSpec((block, LANES), lambda h, i: (i, h)),
            pl.BlockSpec((1, 8, block), lambda h, i: (h, 0, i)),
        ],
        out_shape=[
            jax.ShapeDtypeStruct((rows, count * LANES), bf16),
            jax.ShapeDtypeStruct((count, 8, rows), f32),
        ],
        scratch_shapes=[pltpu.VMEM((rows, LANES), bf16)] * 4,
        compiler_params=pltpu.CompilerParams(vmem_limit_bytes=56 << 20),
        cost_estimate=pl.CostEstimate(
            flops=16 * rows * rows * LANES * count,
            bytes_accessed=8 * rows * LANES * count,
            transcendentals=rows * rows * 2 * count,
        ),
        name="attend",
    )(qkv, qkv, qkv, bias)


def attend_back_kernel(
    q_ref, k_ref, v_ref, bias_ref, do_ref, o_ref, lse_ref, x_ref, *rest, scale, block,
):
    grad_ref, weight_ref, q_even, q_odd, z_even, z_odd, d_even, d_odd, delta, dq_turned, x_here, arrival = rest[-12:]
    fetch = pltpu.make_async_copy(x_ref, x_here, arrival)
    half = LANES // 2
    step = pl.program_id(0)
    rows = q_ref.shape[0]

    @pl.when(step == 0)
    def _():
        fetch.start()
        lane = lax.broadcasted_iota(jnp.int32, q_ref.shape, 1)
        low = lane < half
        scaled = q_ref[...] * jnp.asarray(scale, bf16)
        one, zero = jnp.ones_like(scaled), jnp.zeros_like(scaled)
        q_even[...] = jnp.where(low, scaled, jnp.where(lane == half, one, zero))
        q_odd[...] = jnp.where(low, jnp.where(lane == 0, one, zero), scaled)
        z_even[...] = jnp.where(low, scaled, zero)
        z_odd[...] = jnp.where(low, zero, scaled)
        grad = do_ref[...]
        d_even[...] = jnp.where(low, grad, zero)
        d_odd[...] = jnp.where(low, zero, grad)
        row = lax.broadcasted_iota(jnp.int32, (8, LANES), 0)
        col = lax.broadcasted_iota(jnp.int32, (8, LANES), 1)
        select = jnp.where(lax.div(col, half) == row, 1.0, 0.0).astype(f32)
        product = grad.astype(f32) * o_ref[...].astype(f32)
        delta[...] = dot(select, product, NT, lax.Precision.HIGHEST)
        dq_turned[...] = jnp.zeros_like(dq_turned)

    k, v, bias = k_ref[...], v_ref[...], bias_ref[...]
    low = lax.broadcasted_iota(jnp.int32, k.shape, 1) < half
    k_even = jnp.where(low, k, bias)
    k_odd = jnp.where(low, bias, k)
    k_turned = k.T
    dk = jnp.zeros(k.shape, f32)
    dv = jnp.zeros(k.shape, f32)
    heads = ((k_even, q_even, z_even, d_even), (k_odd, q_odd, z_odd, d_odd))
    for first in range(0, rows, block):
        part = slice(first, first + block)
        for h, (keys, queries, plain, grads) in enumerate(heads):
            scores = dot(keys, queries[part, :], NT)
            weights = jnp.exp2(scores * LOG2E - lse_ref[0, h : h + 1, part])
            d_weights = dot(v, grads[part, :], NT)
            d_scores = (weights * (d_weights - delta[h : h + 1, part])).astype(bf16)
            dv += dot(weights.astype(bf16), grads[part, :])
            dk += dot(d_scores, plain[part, :])
            dq_turned[h * half : (h + 1) * half, part] += dot(
                k_turned[h * half : (h + 1) * half, :], d_scores
            )
    here = pl.ds(pl.multiple_of(step * k.shape[0], k.shape[0]), k.shape[0])
    grad_ref[here, LANES : 2 * LANES] = dk.astype(bf16)
    grad_ref[here, 2 * LANES :] = dv.astype(bf16)

    @pl.when(step == pl.num_programs(0) - 1)
    def _():
        grad_ref[:, :LANES] = (dq_turned[...] * scale).T.astype(bf16)
        fetch.wait()
        weight_ref[...] = dot(x_here[...], grad_ref[...])


def attend_back(qkv, bias, grads, out, lse, turned, held, pair, within, scale, key_block, block):
    rows = qkv.shape[0]
    features = turned.shape[0]
    whole = lambda n: pl.BlockSpec((rows, LANES), lambda j: (0, n))
    part = lambda n: pl.BlockSpec((key_block, LANES), lambda j: (j, n))
    return pl.pallas_call(
        functools.partial(attend_back_kernel, scale=scale, block=block),
        grid=(rows // key_block,),
        in_specs=[
            whole(3 * pair),
            part(3 * pair + 1),
            part(3 * pair + 2),
            part(0),
            whole(pair),
            whole(within),
            pl.BlockSpec((1, 8, rows), lambda j: (within, 0, 0)),
        ]
        + [pl.BlockSpec(memory_space=pl.ANY)] * (1 + len(held)),
        out_specs=[
            pl.BlockSpec((rows, 3 * LANES), lambda j: (0, pair)),
            pl.BlockSpec((features, 3 * LANES), lambda j: (0, 0)),
        ],
        out_shape=[
            jax.ShapeDtypeStruct(qkv.shape, bf16),
            jax.ShapeDtypeStruct((features, 3 * LANES), f32),
        ],
        input_output_aliases={8: 0} if held else {},
        scratch_shapes=[pltpu.VMEM((rows, LANES), bf16)] * 6
        + [pltpu.VMEM((8, rows), f32), pltpu.VMEM((LANES, rows), f32)]
        + [pltpu.VMEM(turned.shape, bf16), pltpu.SemaphoreType.DMA(())],
        compiler_params=pltpu.CompilerParams(vmem_limit_bytes=56 << 20),
        cost_estimate=pl.CostEstimate(
            flops=40 * rows * rows * LANES,
            bytes_accessed=16 * rows * LANES,
            transcendentals=rows * rows * 2,
        ),
        name="attend_back",
    )(qkv, qkv, qkv, bias, grads, out, lse, turned, *held)


BITS = {"zh": 16, "zl": 8, "x": 4, "y": 2, "c": 1}


def number():
    return lax.axis_index("dp") * 4 + lax.axis_index("fsdp")


def bit(name):
    return jnp.minimum(lax.bitwise_and(number(), BITS[name]), 1)


def flip(value, name):
    return lax.ppermute(value, BOTH, [(n, n ^ BITS[name]) for n in range(32)])


def after(value, *others):
    return lax.optimization_barrier((value,) + others)[0]


def grow(block, name):
    return jnp.concatenate([block, flip(block, name)], axis=0)


def in_order(block, names):
    chip = lax.div(number(), 2)
    every = lax.iota(jnp.int32, block.shape[0])
    relative = lax.bitwise_xor(every, chip)
    index = lax.rem(lax.div(chip, 4) - lax.div(every, 4) + 4, 4)
    for place, name in enumerate(names):
        index = index + jnp.minimum(lax.bitwise_and(relative, BITS[name] // 2), 1) * (4 << place)
    return jnp.take(block, index, axis=0)


def pick(value, axis, index):
    return lax.squeeze(lax.dynamic_slice_in_dim(value, index, 1, axis), (axis,))


def along_z(value, amount):
    pairs = []
    for n in range(32):
        place = n // 8
        pairs.append((n, n + ((place + amount) % 4 - place) * 8))
    return lax.ppermute(value, BOTH, pairs)


def z_place():
    return lax.div(number(), 8)


class Falling:
    def __init__(self, value, axes=("z", "x", "y")):
        self.axes = list(axes)
        if value.ndim == 2:
            value = value.reshape((4, 2, 2, value.shape[0] // 16) + value.shape[1:])
        self.value = value
        self.held = [("value", 1)]

    def arrays(self, new=None):
        if new is not None:
            for name, count in self.held:
                part, new = new[:count], new[count:]
                setattr(self, name, part[0] if name in ("value", "kept") else part)
        return [
            array
            for name, _ in self.held
            for array in (
                [getattr(self, name)] if name in ("value", "kept") else getattr(self, name)
            )
        ]

    def cut(self, name):
        axis = self.axes.index(name)
        self.axes.pop(axis)
        if name == "z":
            own = z_place()
            self.pieces = [
                pick(self.value, axis, lax.rem(own + n, 4)).astype(bf16) for n in (1, 2, 3)
            ]
        else:
            own = bit(name)
            self.pieces = [pick(self.value, axis, 1 - own).astype(bf16)]
        self.kept = pick(self.value, axis, own)
        self.name = name
        self.held = [("pieces", len(self.pieces)), ("kept", 1)]

    def send(self):
        if self.name == "z":
            self.arrived = [along_z(p, n) for n, p in zip((1, 2, 3), self.pieces)]
        else:
            self.arrived = [flip(self.pieces[0], self.name)]
        self.held = [("arrived", len(self.arrived)), ("kept", 1)]

    def add(self):
        total = self.kept.astype(f32)
        for part in self.arrived:
            total = total + part.astype(f32)
        self.value = total.astype(bf16) if self.axes else total
        self.held = [("value", 1)]


def fence(values, falls=()):
    flat = list(values)
    for f in falls:
        flat += f.arrays()
    flat = list(lax.optimization_barrier(tuple(flat)))
    values, flat = flat[: len(values)], flat[len(values) :]
    for f in falls:
        count = len(f.arrays())
        f.arrays(flat[:count])
        flat = flat[count:]
    return values


def normalize(resid):
    average = jnp.mean(resid, axis=-1, keepdims=True)
    centred = resid - average
    second = jnp.mean(centred * centred, axis=-1, keepdims=True)
    inverse = lax.rsqrt(second + EPSILON)
    return centred * inverse, inverse


def normalize_back(grad, unit, inverse, gain):
    scaled = grad * gain
    along = jnp.mean(scaled * unit, axis=-1, keepdims=True)
    return inverse * (scaled - jnp.mean(scaled, axis=-1, keepdims=True) - unit * along)


def shards(
    tokens, teacher, lengths, dealing,
    query_weight, key_weight, value_weight, output_weight, inner_weight, outer_weight,
    query_bias, value_bias, output_bias, norm_gain, norm_shift, inner_bias, outer_bias,
    final_gain, final_shift,
):
    slots, row_count, width = tokens.shape
    sections = lax.axis_size("fsdp")
    dp_count = lax.axis_size("dp")
    devices = dp_count * sections
    ranks = sections // 2
    fast = dp_count == 8 and sections == 4
    hidden_units = inner_weight.shape[1]
    head_width = width // HEADS
    scale = 1.0 / math.sqrt(head_width)
    seq_total = lengths.shape[0]
    seq_len = row_count * sections
    share = width // ranks
    pairs = -(-share // LANES)
    rows = 2 * row_count
    small = query_weight.shape[0]

    place = lax.axis_index("fsdp")
    side = lax.div(place, ranks)
    rank = lax.rem(place, ranks)
    across = [(f, (f + ranks) % sections) for f in range(sections)]
    groups = [[g * ranks + r for r in range(ranks)] for g in range(2)]
    partner = [(f, f ^ 1) for f in range(sections)]
    length = lax.dynamic_index_in_dim(
        lengths, lax.axis_index("dp") * slots + side, keepdims=False
    )

    def to_swap(whole):
        kept = lax.dynamic_index_in_dim(whole, side, 0, keepdims=False)
        sent = lax.dynamic_index_in_dim(whole, 1 - side, 0, keepdims=False)
        return kept, sent

    def swap_in(whole):
        kept, sent = to_swap(whole)
        return jnp.concatenate([kept, lax.ppermute(sent, "fsdp", across)], axis=0)

    def swap_out(local):
        arrived = lax.ppermute(local[row_count:], "fsdp", across)
        kept = local[:row_count]
        whole = jnp.where(side == 0, jnp.stack([kept, arrived]), jnp.stack([arrived, kept]))
        return whole, arrived

    def other(value):
        return lax.ppermute(value, "fsdp", partner)

    def in_rank_order(mine, theirs, axis):
        return jnp.where(
            rank == 0,
            jnp.concatenate([mine, theirs], axis=axis),
            jnp.concatenate([theirs, mine], axis=axis),
        )

    def by_pairs(value):
        fill = pairs * LANES - share
        if fill:
            value = jnp.pad(value, ((0, 0),) * (value.ndim - 1) + ((0, fill),))
        return value.reshape(value.shape[:-1] + (pairs, LANES))

    if ranks == 2:
        rank_order = [rank, 1 - rank]
    else:
        rank_order = [jnp.int32(r) for r in range(ranks)]
    within = lax.iota(jnp.int32, row_count)

    def positions_of(r):
        return jnp.concatenate(
            [(side * ranks + r) * row_count + within, ((1 - side) * ranks + r) * row_count + within]
        )

    positions = jnp.concatenate([positions_of(r) for r in rank_order])
    bias = jnp.where(positions < length, 0.0, MASKED).astype(bf16)
    key_bias = jnp.broadcast_to(bias[:, None], (rows * ranks, LANES))

    vectors = [
        query_bias, value_bias, output_bias, norm_gain, norm_shift, outer_bias, final_gain,
        final_shift, inner_bias,
    ]
    lines = jnp.concatenate([v.reshape(-1, small) for v in vectors], axis=0)
    if fast:

        def columns(which):
            parts = [
                lax.dynamic_slice_in_dim(w, which * share + p * LANES, LANES, 1)
                for p in range(pairs)
                for w in (query_weight, key_weight, value_weight)
            ]
            spare = ((0, small - lines.shape[0]), (0, LANES - small))
            return jnp.concatenate(parts + [jnp.pad(lines, spare)], axis=1)

        mine, theirs = columns(rank), other(columns(1 - rank))
        first = jnp.where(rank == 0, jnp.stack([mine, theirs]), jnp.stack([theirs, mine]))[None]
        kept, sent = to_swap(tokens)
        first, sent = fence([first, sent])
        around = [along_z(first, n) for n in (1, 2, 3)]
        arrived = lax.ppermute(sent, "fsdp", across)
        *around, arrived = fence([*around, arrived])
        risen = jnp.concatenate([first] + around, axis=0)
        local = jnp.concatenate([kept, arrived], axis=0)
        cut = 5 * LANES
        left, right, local, teacher = fence([risen[..., :cut], risen[..., cut:], local, teacher])
        l_arrived, r_arrived, gathered = flip(left, "x"), flip(right, "y"), other(local)
        l_arrived, r_arrived, gathered = fence([l_arrived, r_arrived, gathered])
        gathered = jnp.concatenate([local, gathered], axis=0)
        left, right = fence(
            [jnp.concatenate([left, l_arrived], axis=0), jnp.concatenate([right, r_arrived], axis=0)]
        )
        left = grow(left, "y")
        right = grow(right, "x")
        whole = jnp.concatenate(
            [in_order(left, ["x", "y"]), in_order(right, ["y", "x"])], axis=3
        ).reshape(width, 3 * share + LANES)
        qkv_weight = whole[:, : 3 * share]
        lines = whole[:, 3 * share :].reshape(devices, small, LANES)[:, : lines.shape[0], :small]
    else:
        local = swap_in(tokens)
        gathered = lax.all_gather(
            local, "fsdp", axis=0, tiled=True, axis_index_groups=groups
        )
        whole = [
            lax.all_gather(w, BOTH, axis=0, tiled=True)
            for w in (query_weight, key_weight, value_weight)
        ]
        whole = [
            by_pairs(lax.dynamic_slice_in_dim(w, rank * share, share, 1)) for w in whole
        ]
        qkv_weight = jnp.stack(whole, axis=2).reshape(width, pairs * 3 * LANES)
        lines = lax.all_gather(lines, BOTH, axis=0, tiled=False)
    unpacked = []
    start = 0
    for vector in vectors:
        count = vector.shape[0] // small
        unpacked.append(lines[:, start : start + count].reshape(-1).astype(f32))
        start += count
    b_query, b_value, b_output, gain_one, shift_one, b_outer, gain_two, shift_two, b_inner = unpacked
    ratio = hidden_units // width
    late = jnp.concatenate(
        [output_weight]
        + [inner_weight[:, n * width : (n + 1) * width] for n in range(ratio)]
        + [outer_weight],
        axis=0,
    )
    late = lax.all_gather(late, BOTH, axis=0, tiled=False)
    w_output = late[:, :small].reshape(width, width)
    w_inner = jnp.concatenate(
        [
            late[:, (n + 1) * small : (n + 2) * small].reshape(width, width)
            for n in range(ratio)
        ],
        axis=1,
    )
    w_outer = late[:, (ratio + 1) * small :].reshape(hidden_units, width)

    slot_ids = lax.iota(jnp.int32, seq_total)
    inverse = jnp.sum(
        jnp.where(dealing[None, :] == slot_ids[:, None], slot_ids[None, :], 0), axis=1
    )
    target = lax.all_to_all(teacher, "dp", split_axis=1, concat_axis=0, tiled=True)

    b_own = [
        by_pairs(lax.dynamic_slice_in_dim(b, rank * share, share)) for b in (b_query, b_value)
    ]
    b_qkv = jnp.stack([b_own[0], jnp.zeros_like(b_own[0]), b_own[1]], axis=1).reshape(-1)
    qkv = (dot(gathered, qkv_weight) + b_qkv).astype(bf16)
    early = min(2, pairs)
    outs = [attend(qkv, key_bias, 0, early, scale, min(1024, rows * ranks))]
    if pairs > early:
        target, qkv = fence([jnp.take(after(target, outs[0][0]), inverse, axis=0), qkv])
        outs.append(attend(qkv, key_bias, early, pairs - early, scale, min(1024, rows * ranks)))
    else:
        target = jnp.take(target, inverse, axis=0)
    heads_out = jnp.concatenate([o for o, _ in outs], axis=1)[:, :share]
    if ranks == 2:
        attn_rows = in_rank_order(heads_out[:rows], other(heads_out[rows:]), 1)
    else:
        attn_rows = lax.all_to_all(
            heads_out, "fsdp", split_axis=0, concat_axis=1, tiled=True, axis_index_groups=groups
        )
    target = lax.all_to_all(target, "dp", split_axis=0, concat_axis=1, tiled=True)

    resid_one = local.astype(f32) + dot(attn_rows, w_output) + b_output
    unit_one, inverse_one = normalize(resid_one)
    hidden = (unit_one * gain_one + shift_one).astype(bf16)
    target = swap_in(after(target, hidden))
    inner = dot(hidden, w_inner) + b_inner
    normal = 0.5 + 0.5 * lax.erf(inner * math.sqrt(0.5))
    act = (inner * normal).astype(bf16)
    slope = (
        normal + inner * jnp.exp(-0.5 * inner * inner) * (1.0 / math.sqrt(2 * math.pi))
    ).astype(bf16)
    resid_two = hidden.astype(f32) + dot(act, w_outer) + b_outer
    unit_two, inverse_two = normalize(resid_two)
    final = unit_two * gain_two + shift_two
    output, output_arrived = swap_out(final.astype(bf16))

    valid = (positions_of(rank) < length).astype(f32)[:, None]
    loss_scale = seq_total * seq_len / jnp.sum(lengths).astype(f32)
    grad_final = loss_scale * (final - target.astype(f32)) * valid
    grad_gain_two = jnp.sum(grad_final * unit_two, axis=0)
    grad_shift_two = jnp.sum(grad_final, axis=0)
    d_two = normalize_back(grad_final, unit_two, inverse_two, gain_two)
    d_out = d_two.astype(bf16)
    grad_outer_bias = jnp.sum(d_out.astype(f32), axis=0)
    outer_sum = dot(act, d_out, TN).astype(bf16)
    grad_outer = lax.psum_scatter(outer_sum, BOTH, scatter_dimension=0, tiled=True).astype(f32)
    d_inner = (dot(d_out, w_outer, NT) * slope.astype(f32)).astype(bf16)
    grad_inner_bias = jnp.sum(d_inner.astype(f32), axis=0)
    d_hidden = d_two + dot(d_inner, w_inner, NT)
    grad_gain_one = jnp.sum(d_hidden * unit_one, axis=0)
    grad_shift_one = jnp.sum(d_hidden, axis=0)
    d_one = normalize_back(d_hidden, unit_one, inverse_one, gain_one)
    d_mix = d_one.astype(bf16)
    grad_output_bias = jnp.sum(d_mix.astype(f32), axis=0)
    d_attn = dot(d_mix, w_output, NT).astype(bf16)
    if ranks == 2:
        cut = lambda r: lax.dynamic_slice_in_dim(d_attn, r * share, share, 1)
        heads_grad = jnp.concatenate([cut(rank), other(cut(1 - rank))], axis=0)
    else:
        heads_grad = lax.all_to_all(
            d_attn, "fsdp", split_axis=1, concat_axis=0, tiled=True, axis_index_groups=groups
        )
    heads_grad = by_pairs(heads_grad).reshape(rows * ranks, pairs * LANES)

    if fast:
        def halves(left, right):
            wide = right.shape[1] // 2
            cut = lambda r: lax.dynamic_slice_in_dim(right, r * wide, wide, 1)
            sent = other(dot(left, cut(1 - rank), TN).astype(bf16))
            return (dot(left, cut(rank), TN) + sent.astype(f32)).astype(bf16)

        inner_half = halves(hidden, d_inner)
        output_half = halves(attn_rows, d_mix)
        cut_at = hidden_units // 4 + 2 * LANES
        falls = [
            Falling(inner_half[:, :cut_at]),
            Falling(jnp.concatenate([inner_half[:, cut_at:], output_half], axis=1)),
        ]
        moves = [(falls[0], "x"), (falls[1], "y")]
        keep = [outer_sum, output_arrived]
    else:
        grad_inner = lax.psum_scatter(
            dot(hidden, d_inner, TN), BOTH, scatter_dimension=0, tiled=True
        )
        grad_output = lax.psum_scatter(
            dot(attn_rows, d_mix, TN), BOTH, scatter_dimension=0, tiled=True
        )

    turned = jnp.concatenate([gathered.T, jnp.ones((16, rows * ranks), bf16)], axis=0)
    held = []
    weight_falls, parts = [], []
    for pair in range(pairs):
        out, lse = outs[pair // early]
        if fast:
            for f, name in moves:
                f.cut(name)
            everything = falls + weight_falls
            heads_grad, *_ = fence([heads_grad] + (keep if pair == 0 else []), everything)
            for f, _ in moves:
                f.send()
        d_qkv, weights = attend_back(
            qkv, key_bias, heads_grad, out, lse, turned, held, pair, pair % early, scale, 512, 1024
        )
        if fast:
            d_qkv, weights, heads_grad = fence([d_qkv, weights, heads_grad], everything)
            for f, _ in moves:
                f.add()
            if pair < 2:
                weight_falls.append(Falling(weights[:width].astype(bf16)))
            if pair == 0:
                moves = [(falls[0], "y"), (falls[1], "x"), (weight_falls[0], "x")]
            if pair == 1:
                both = jnp.concatenate([falls[0].value, falls[1].value], axis=2)
                falls = [Falling(both, ["z"])]
                moves = [(falls[0], "z"), (weight_falls[0], "y"), (weight_falls[1], "x")]
        held = [d_qkv]
        parts.append(weights)

    def place_share(part):
        empty = jnp.zeros((width,), f32)
        return lax.dynamic_update_slice_in_dim(empty, part, rank * share, 0)

    biases = jnp.stack([p[width].reshape(3, LANES) for p in parts], axis=1)
    biases = biases.reshape(3, pairs * LANES)[:, :share]
    sums = [
        place_share(biases[0]), place_share(biases[2]), grad_output_bias, grad_gain_one,
        grad_shift_one, grad_outer_bias, grad_gain_two, grad_shift_two, grad_inner_bias,
    ]
    sums = jnp.concatenate([s.reshape(devices, -1) for s in sums], axis=1)

    if fast:
        count = sums.shape[1]
        deep = 2 * count
        wide = 3 * LANES
        sums = jnp.pad(sums.reshape(16, deep), ((0, 0), (0, 8 * wide - deep)))
        last = jnp.concatenate(
            [parts[-1][:width].reshape(16, 2 * small, wide), sums.reshape(16, 8, wide)], axis=1
        )
        weight_falls.append(Falling(last.astype(bf16).reshape(-1, wide)))
        moves = [(weight_falls[1], "y"), (weight_falls[2], "x")]
        for f, name in moves:
            f.cut(name)
        (d_qkv,) = fence([d_qkv], weight_falls)
        for f, _ in moves:
            f.send()
        d_gathered = dot(d_qkv, qkv_weight, NT)
        (d_gathered,) = fence([d_gathered], weight_falls)
        for f, _ in moves:
            f.add()
        weight_falls[2].cut("y")
        (d_sent,) = fence([d_gathered[rows:].astype(bf16)], weight_falls)
        weight_falls[2].send()
        d_arrived = other(d_sent)
        (d_arrived,) = fence([d_arrived], weight_falls)
        weight_falls[2].add()
        grad_rows = (d_one + d_gathered[:rows] + d_arrived.astype(f32)).astype(bf16)
        three = Falling(
            jnp.concatenate(
                [jnp.concatenate([f.value[:, : 2 * small] for f in weight_falls], axis=2)]
                + [
                    jnp.pad(
                        weight_falls[2].value[:, 2 * small :],
                        ((0, 0), (0, 0), (0, (pairs - 1) * wide)),
                    )
                ],
                axis=1,
            ),
            ["z"],
        )
        three.cut("z")
        (grad_rows,) = fence([grad_rows], [three])
        three.send()
        input_grad, _ = swap_out(grad_rows)
        three.add()

        def settle(value):
            value = value.reshape(2, small, value.shape[1])
            return pick(value, 0, rank), other(pick(value, 0, 1 - rank))

        mine, theirs = settle(falls[0].value)
        whole = in_rank_order(mine[:, : hidden_units // 2], theirs[:, : hidden_units // 2], 1)
        grad_inner = whole
        grad_output = in_rank_order(mine[:, hidden_units // 2 :], theirs[:, hidden_units // 2 :], 1)
        own, theirs = settle(three.value[: 2 * small])
        own = own.reshape(small, pairs, 3, LANES)
        theirs = theirs.reshape(small, pairs, 3, LANES)
        value = in_rank_order(own, theirs, 1)
        grad_query, grad_key, grad_value = [
            value[:, :, n].reshape(small, width) for n in range(3)
        ]
        tail = three.value[2 * small :, :wide]
        sums = (tail + other(tail)).reshape(-1)[:deep].reshape(2, count)
        sums = pick(sums, 0, rank)
    else:
        d_gathered = dot(d_qkv, qkv_weight, NT)
        if ranks == 2:
            d_local = d_gathered[:rows] + other(d_gathered[rows:].astype(bf16)).astype(f32)
        else:
            d_local = lax.psum_scatter(
                d_gathered, "fsdp", scatter_dimension=0, tiled=True, axis_index_groups=groups
            )
        input_grad, _ = swap_out((d_one + d_local).astype(bf16))
        value = jnp.stack([p[:width].reshape(width, 3, LANES) for p in parts], axis=2)
        value = value.reshape(width, 3, pairs * LANES)[:, :, :share]
        empty = jnp.zeros((width, 3, width), f32)
        value = lax.dynamic_update_slice_in_dim(empty, value, rank * share, 2)
        grad_query, grad_key, grad_value = [
            lax.psum_scatter(value[:, n], BOTH, scatter_dimension=0, tiled=True)
            for n in range(3)
        ]
        sums = lax.psum_scatter(sums, BOTH, scatter_dimension=0, tiled=True).reshape(-1)
    split = []
    start = 0
    for vector in vectors:
        count = vector.shape[0]
        split.append(sums[start : start + count])
        start += count
    return (
        output, input_grad, grad_query, grad_key, grad_value, grad_output, grad_inner, grad_outer,
        split[0], split[1], split[2], split[3], split[4], split[8], split[5], split[6], split[7],
    )


def solution(mesh):
    act = P("dp", "fsdp", None)
    matrix = P(BOTH, None)
    vector = P(BOTH)
    return jax.shard_map(
        shards,
        mesh=mesh,
        in_specs=(act, act, P(), P()) + (matrix,) * 6 + (vector,) * 9,
        out_specs=(act, act) + (matrix,) * 6 + (vector,) * 9,
        check_vma=False,
    )
```

time: 611 us -> 511 us (0.84)
  waiting for transfers between devices: 159 us -> 56.1 us
  starting transfers between devices: 91.1 us -> 50.5 us
  Pallas kernels: 119 us -> 134 us
  between operations: 3.2 us -> 16.2 us
  local copies, waits for them, and re-layouts: 98.9 us -> 109 us
  other arithmetic: 45.2 us -> 53.2 us
    ppermute x74 -> x34, waiting for transfers between devices: 123 us -> 35.2 us  [the longest x9 18.8 us: along_z(): return lax.ppermute(value, BOTH, pairs)]
    ppermute x74 -> x34, starting transfers between devices: 79.5 us -> 34 us  [the longest x14 15.7 us: flip(): return lax.ppermute(value, BOTH, [(n, n ^ BITS[name]) for n in range(32)])]
    dynamic_update_slice x30 -> x2, local copies, waits for them, and re-layouts: 29.6 us -> 0.22 us  [place_share(): return lax.dynamic_update_slice_in_dim(empty, part, rank * share, 0)]
    slice x7 -> x25, local copies, waits for them, and re-layouts: 6.48 us -> 26.1 us  [the longest x1 5.06 us: shards(): late[:, (n + 1) * small:(n + 2) * small].reshape(width, width)]
    add x21 -> x5, other arithmetic: 16.9 us -> 1.36 us  [the longest x2 1.35 us: add(): total = total + part.astype(f32)]
    pallas_call x1 -> x3, Pallas kernels: 72.3 us -> 84.6 us  [attend_back(): pl.pallas_call(functools.partial(attend_back_kernel, scale=scale, block=b...]
    convert_element_type x4 -> x16, other arithmetic: 3.2 us -> 14.4 us  [the longest x10 6.49 us: add(): self.value = total.astype(bf16) if self.axes else total]
    convert_element_type x24 -> x9, local copies, waits for them, and re-layouts: 11.2 us -> 0.75 us  [shards(): unpacked.append(lines[:, start:start + count].reshape(-1).astype(f32))]
  transfers between devices with their start and end apart: 80 -> 41, of which waited for: 29 -> 13; matrix products, arithmetic and copies ran while one was open for 30% -> 38% of each run, Pallas kernels for 20% -> 27%
where the time goes in v2:
time: 511 us; the launch traced here: 504 us
  Pallas kernels  134 us (26%)
  local copies, waits for them, and re-layouts  109 us (21%)
  matrix products  84.6 us (17%)
  waiting for transfers between devices  56.1 us (11%)
  other arithmetic  53.2 us (10%)
  starting transfers between devices  50.5 us (10%)
  between operations  16.2 us (3%)
    pallas_call x3, Pallas kernels, attend_back(): pl.pallas_call(functools.partial(attend_back_kernel, scale=scale, block=b...  84.6 us
    dot_general x13, matrix products, dot(): lax.dot_general(left, right, dims, preferred_element_type=f32, precision=...  84.6 us
    pallas_call x2, Pallas kernels, attend(): pl.pallas_call(functools.partial(attend_kernel, scale=scale), grid=(count...  49.2 us
    unnamed x113, local copies, waits for them, and re-layouts  29.8 us
    ppermute x9, waiting for transfers between devices, along_z(): return lax.ppermute(value, BOTH, pairs)  18.8 us
    ppermute x14, starting transfers between devices, flip(): return lax.ppermute(value, BOTH, [(n, n ^ BITS[name]) for n in range(32)])  15.7 us
    ppermute x14, waiting for transfers between devices, flip(): return lax.ppermute(value, BOTH, [(n, n ^ BITS[name]) for n in range(32)])  15.2 us
    ppermute x9, starting transfers between devices, along_z(): return lax.ppermute(value, BOTH, pairs)  13.5 us
  transfers between devices with their start and end apart: 41, of which 13 were waited for; matrix products, arithmetic and copies ran while one was open for 38% of the time, Pallas kernels for 27%

profile of v2, /device:TPU:0, one launch (start us, length us, event | category | flops | bytes accessed | tf_op | source)
XLA Modules:
  0.0 503.6 jit_solution(13150401567979880756)
XLA Ops:
  27.2 2.6 collective-permute-start.4
  30.1 3.7 collective-permute-start.3
  34.8 3.9 collective-permute-done.3
  38.7 8.6 %collective-permute-done.2 = bf16[1,2,24,1280]{3,2,1,0:T(8,128)(2,1)S(1)} collective-permute-done((bf16[1,2,24,1280]{3,2,1,0:T(8,128)(2,1)S(1)}, bf16[1,2,24,1280]{3,2,1,0:T(8,128)(2,1)S(1)}, u32[]{:S(2)}, u32[]{:S(2)}) %collective-permute-start.2) | collective-permute-done | bytes 122912 | tf_op jit(solution)/shard_map/ppermute | solution.py:241
  51.3 1.8 collective-permute-start.5
  55.1 10.4 %collective-permute-done.5 = bf16[4,2,24,640]{3,2,1,0:T(8,128)(2,1)} collective-permute-done((bf16[4,2,24,640]{3,2,1,0:T(8,128)(2,1)}, bf16[4,2,24,640]{3,2,1,0:T(8,128)(2,1)}, u32[]{:S(2)}, u32[]{:S(2)}) %collective-permute-start.5) | collective-permute-done | bytes 245792 | tf_op jit(solution)/shard_map/ppermute | solution.py:211
  65.5 2.3 pad_maximum_fusion.9
  67.8 1.6 collective-permute-start.8
  70.9 2.8 copy.90
  73.6 5.8 %all-to-all-start = ((bf16[2,512,768]{2,0,1:T(2,128)(2,1)}), bf16[2,512,768]{2,0,1:T(2,128)(2,1)}, u32[]{:S(2)}, u32[]{:S(2)}) async-start(bf16[2,512,768]{2,0,1:T(2,128)(2,1)} %copy.90), calls=%async_computation | async-start | bytes 3145728 | tf_op jit(solution)/shard_map/all_to_all | solution.py:487
  83.7 2.2 pad_maximum_fusion.5
  85.9 2.8 gather_fusion.1
  88.7 2.2 pad_maximum_fusion.6
  90.9 2.9 gather_fusion.2
  98.9 7.4 %add_convert_fusion.q_ref.k_ref.v_ref = bf16[2048,1152]{1,0:T(8,128)(2,1)} fusion(bf16[2048,768]{0,1:T(8,128)(2,1)S(1)} %constant_dynamic-update-slice_fusion.24, f32[1152]{0:T(1024)S(1)} %add.431, bf16[768,1280]{1,0:T(8,128)(2,1)} %bitcast.182), kind=kOutput, calls=%fused_computation.12 | convolution fusion | flops 3628597248 | bytes 9638400 | tf_op jit(solution)/shard_map/dot_general | solution.py:25
  107.5 32.2 %attend.2 = (bf16[2048,256]{1,0:T(8,128)(2,1)}, f32[2,8,2048]{2,1,0:T(8,128)}) custom-call(bf16[2048,1152]{1,0:T(8,128)(2,1)} %add_convert_fusion.q_ref.k_ref.v_ref, bf16[2048,1152]{1,0:T(8,128)(2,1)} %add_convert_fusion.q_ref.k_ref.v_ref, bf16[2048,1152]{1,0:T(8,128)(2,1)} %add_convert_fusion.q_ref.k_ref.v_ref, bf16[2048,128]{1,0:T(8,128)(2,1)} %broadcast_in_dim.43.bias_ref), custom_call_target="tpu_custom_call" | custom-call | flops 17179869184 | bytes 4194304 | tf_op jit(solution)/shard_map/attend/pallas_call | solution.py:70
  139.7 3.4 all-to-all-done
  145.9 3.2 gather_fusion
  149.1 2.8 broadcast_select_fusion
  151.9 7.9 %all-to-all-start.1 = ((bf16[16,64,768]{2,1,0:T(8,128)(2,1)}), bf16[16,64,768]{2,1,0:T(8,128)(2,1)}, u32[]{:S(2)}, u32[]{:S(2)}) async-start(bf16[16,64,768]{2,1,0:T(8,128)(2,1)} %broadcast_select_fusion), calls=%async_computation.1 | async-start | bytes 3145728 | tf_op jit(solution)/shard_map/all_to_all | solution.py:508
  161.1 17.1 %attend.3 = (bf16[2048,128]{1,0:T(8,128)(2,1)}, f32[1,8,2048]{2,1,0:T(8,128)}) custom-call(bf16[2048,1152]{1,0:T(8,128)(2,1)} %add_convert_fusion.q_ref.k_ref.v_ref, bf16[2048,1152]{1,0:T(8,128)(2,1)} %add_convert_fusion.q_ref.k_ref.v_ref, bf16[2048,1152]{1,0:T(8,128)(2,1)} %add_convert_fusion.q_ref.k_ref.v_ref, bf16[2048,128]{1,0:T(8,128)(2,1)} %broadcast_in_dim.43.bias_ref), custom_call_target="tpu_custom_call" | custom-call | flops 8589934592 | bytes 2097152 | tf_op jit(solution)/shard_map/attend/pallas_call | solution.py:70
  182.6 1.9 concatenate.149.x_ref
  185.2 8.3 %all-to-all-done.1 = bf16[16,64,768]{2,1,0:T(8,128)(2,1)} async-done(((bf16[16,64,768]{2,1,0:T(8,128)(2,1)}), bf16[16,64,768]{2,1,0:T(8,128)(2,1)}, u32[]{:S(2)}, u32[]{:S(2)}) %all-to-all-start.1) | async-done | bytes 1572896 | tf_op jit(solution)/shard_map/all_to_all | solution.py:508
  193.5 2.7 copy.94
  196.2 4.8 slice.323
  201.0 5.1 %fusion.59 = (bf16[32,24,768]{2,1,0:T(8,128)(2,1)}, bf16[32,24,768]{2,1,0:T(8,128)(2,1)}, bf16[32,24,768]{2,1,0:T(8,128)(2,1)}, bf16[32,24,768]{2,1,0:T(8,128)(2,1)}, bf16[32,24,768]{2,1,0:T(8,128)(2,1)S(1)}) fusion(bf16[32,216,768]{2,1,0:T(8,128)(2,1)} %bitcast.167), kind=kLoop, calls=%fused_computation.290 | loop fusion | bytes 11796480 | tf_op jit(solution)/shard_map/slice | solution.py:476
  206.1 3.5 fusion.62
  210.0 1.7 add_convert_fusion.2
  212.9 2.3 copy.96
  216.7 12.2 %multiply_convert_fusion.1 = (bf16[1024,3072]{1,0:T(8,128)(2,1)S(1)}, f32[1024,3072]{1,0:T(8,128)}) fusion(f32[3072]{0:T(1024)S(1)} %reshape.440, bf16[1024,768]{0,1:T(8,128)(2,1)} %add_convert_fusion.2, bf16[768,768]{1,0:T(8,128)(2,1)} %bitcast.192, bf16[768,768]{1,0:T(8,128)(2,1)} %bitcast.194, bf16[768,768]{1,0:T(8,128)(2,1)} %bitcast.196, ...), kind=kOutput, calls=%fused_computation.10 | convolution fusion | flops 4869586944 | bytes 25178112 | tf_op jit(solution)/shard_map/dot_general | solution.py:25
  229.0 10.2 %fusion.63 = (f32[1024]{0:T(1024)S(1)}, f32[1024,768]{0,1:T(8,128)}) fusion(f32[768]{0:T(1024)S(1)} %reshape.441, bf16[1024,3072]{1,0:T(8,128)(2,1)S(1)} %get-tuple-element.408, bf16[3072,768]{1,0:T(8,128)(2,1)} %bitcast.176, bf16[1024,768]{0,1:T(8,128)(2,1)S(1)} %copy-done.12), kind=kOutput, calls=%fused_computation.294 | convolution fusion | flops 4834982912 | bytes 15735808 | tf_op jit(solution)/shard_map/dot_general | solution.py:25
  239.1 2.3 copy.95
  241.5 2.4 multiply_reduce_fusion.4
  244.3 4.4 fusion.56
  248.8 3.2 convert_reduce_fusion
  252.0 11.9 %fusion.64 = (bf16[3072]{0:T(1024)(128)(2,1)S(1)}, bf16[1024,3072]{1,0:T(8,128)(2,1)S(1)}) fusion(f32[1024,3072]{1,0:T(8,128)} %get-tuple-element.409, f32[3072]{0:T(1024)S(1)} %reshape.440, bf16[3072,768]{1,0:T(8,128)(2,1)S(1)} %bitcast.179, f32[1024,768]{0,1:T(8,128)S(1)} %get-tuple-element.331), kind=kOutput, calls=%fused_computation.295 | convolution fusion | flops 4876661760 | bytes 26757120 | tf_op jit(solution)/shard_map/dot_general | solution.py:25
  263.9 5.9 %multiply_reduce_fusion.1 = (bf16[768]{0:T(1024)(128)(2,1)S(1)}, f32[1024]{0:T(1024)S(1)}, f32[1024]{0:T(1024)S(1)}, bf16[768]{0:T(1024)(128)(2,1)S(1)}, f32[1024,768]{0,1:T(8,128)S(1)}) fusion(f32[1024,768]{0,1:T(8,128)S(1)} %get-tuple-element.407, f32[1024]{0:T(1024)S(1)} %add_rsqrt_fusion.1, f32[1024]{0:T(1024)S(1)} %broadcast_multiply_fusion.5, ...), kind=kOutput, calls=%fused_computation.22 | convolution fusion | flops 4858572800 | bytes 20469760 | tf_op jit(solution)/shard_map/dot_general | solution.py:25
  274.8 3.4 convolution_convert_fusion.3
  278.7 4.4 convolution_convert_fusion.1
  283.2 6.9 %convolution_convert_fusion = bf16[3072,768]{1,0:T(8,128)(2,1)} fusion(bf16[1024,3072]{1,0:T(8,128)(2,1)S(1)} %bitcast.226, f32[1024,768]{0,1:T(8,128)S(1)} %get-tuple-element.331), kind=kOutput, calls=%fused_computation.13 | convolution fusion | flops 4834983936 | bytes 14155776 | tf_op jit(solution)/shard_map/dot_general | solution.py:25
  290.7 2.6 slice_bitcast_fusion
  294.0 3.5 fusion.16
  297.5 2.6 pad_maximum_fusion.3.do_ref
  300.1 5.2 %add_convert_fusion.1 = bf16[768,1536]{1,0:T(8,128)(2,1)S(1)} fusion(bf16[768,1536]{1,0:T(8,128)(2,1)} %collective-permute-done.14, bf16[1024,768]{0,1:T(8,128)(2,1)S(1)} %copy-done.14, bf16[1024,3072]{1,0:T(8,128)(2,1)} %copy-done.35, s32[]{:T(128)S(6)} %select_n.227), kind=kOutput, calls=%fused_computation.15 | convolution fusion | flops 2419458048 | bytes 9437188 | tf_op jit(solution)/shard_map/dot_general | solution.py:25
  308.3 5.3 %collective-permute-done.11 = bf16[512,768]{0,1:T(8,128)(2,1)} collective-permute-done((bf16[512,768]{0,1:T(8,128)(2,1)}, bf16[512,768]{0,1:T(8,128)(2,1)}, u32[]{:S(2)}, u32[]{:S(2)}) %collective-permute-start.11) | collective-permute-done | bytes 786464 | tf_op jit(solution)/shard_map/ppermute | solution.py:368
  315.4 28.2 %attend_back.3 = (bf16[2048,1152]{1,0:T(8,128)(2,1)}, f32[784,384]{1,0:T(8,128)}) custom-call(bf16[2048,1152]{1,0:T(8,128)(2,1)} %add_convert_fusion.q_ref.k_ref.v_ref, bf16[2048,1152]{1,0:T(8,128)(2,1)} %add_convert_fusion.q_ref.k_ref.v_ref, bf16[2048,1152]{1,0:T(8,128)(2,1)} %add_convert_fusion.q_ref.k_ref.v_ref, ...), custom_call_target="tpu_custom_call" | custom-call | flops 21474836480 | bytes 4194304 | tf_op jit(solution)/shard_map/attend_back/pallas_call | solution.py:164
  350.3 28.3 %attend_back.4 = (bf16[2048,1152]{1,0:T(8,128)(2,1)}, f32[784,384]{1,0:T(8,128)}) custom-call(bf16[2048,1152]{1,0:T(8,128)(2,1)} %add_convert_fusion.q_ref.k_ref.v_ref, bf16[2048,1152]{1,0:T(8,128)(2,1)} %add_convert_fusion.q_ref.k_ref.v_ref, bf16[2048,1152]{1,0:T(8,128)(2,1)} %add_convert_fusion.q_ref.k_ref.v_ref, ...), custom_call_target="tpu_custom_call", output_to_operand_aliasing={{0}: (8, {})} | custom-call | flops 21474836480 | bytes 4194304 | tf_op jit(solution)/shard_map/attend_back/pallas_call | solution.py:164
  383.1 1.9 collective-permute-start.22
  385.0 1.9 collective-permute-start.23
  387.7 28.2 %attend_back.5 = (bf16[2048,1152]{1,0:T(8,128)(2,1)}, f32[784,384]{1,0:T(8,128)}) custom-call(bf16[2048,1152]{1,0:T(8,128)(2,1)} %add_convert_fusion.q_ref.k_ref.v_ref, bf16[2048,1152]{1,0:T(8,128)(2,1)} %add_convert_fusion.q_ref.k_ref.v_ref, bf16[2048,1152]{1,0:T(8,128)(2,1)} %add_convert_fusion.q_ref.k_ref.v_ref, ...), custom_call_target="tpu_custom_call", output_to_operand_aliasing={{0}: (8, {})} | custom-call | flops 21474836480 | bytes 4194304 | tf_op jit(solution)/shard_map/attend_back/pallas_call | solution.py:164
  418.2 2.2 slice.400
  428.8 8.7 %fusion.13 = f32[2048,768]{1,0:T(8,128)} fusion(bf16[2048,1152]{1,0:T(8,128)(2,1)} %get-tuple-element.193, bf16[768,1280]{1,0:T(8,128)(2,1)S(1)} %bitcast.183), kind=kOutput, calls=%fused_computation.52 | convolution fusion | flops 3623878656 | bytes 12779520 | tf_op jit(solution)/shard_map/dot_general | solution.py:25
  437.5 6.6 %copy.99 = f32[2048,768]{0,1:T(8,128)} copy(f32[2048,768]{1,0:T(8,128)} %fusion.13) | data formatting | bytes 12582912 | tf_op jit(solution)/shard_map/optimization_barrier | solution.py:303
  444.1 3.3 slice.399
  449.3 1.6 add_convert_fusion.11
  453.4 3.3 maximum_select_fusion.1
  456.7 2.6 copy.101
  463.2 3.7 collective-permute-done.29
  468.1 3.5 fusion.6
  473.8 2.8 collective-permute-start.33
  477.5 2.5 collective-permute-done.31
  480.0 3.8 collective-permute-done.32
  489.0 1.6 convert_element_type.387
  490.7 3.9 collective-permute-done.30
  (321 shorter events, 104.6 us)
Async XLA Ops:
  7.2 189.0 %all-gather.3.cloned.1.call-start = ((), (), s32[]{:S(2)}) async-start(), calls=%async_computation.4 | async-start | bytes 10948608 | tf_op jit(solution)/shard_map/all_gather | solution.py:472
  24.9 2.3 collective-permute-start
  27.2 20.8 %collective-permute-start.4 = (bf16[512,768]{0,1:T(8,128)(2,1)S(1)}, bf16[512,768]{0,1:T(8,128)(2,1)S(1)}, u32[]{:S(2)}, u32[]{:S(2)}) collective-permute-start(bf16[512,768]{0,1:T(8,128)(2,1)S(1)} %bitcast.199), channel_id=1, source_target_pairs={{0,2},{1,3},{2,0},{3,1},{4,6},{5,7},{6,4},{7,5},{8,10},{9,11},{10,... | collective-permute-start | bytes 2359304 | tf_op jit(solution)/shard_map/ppermute | solution.py:425
  29.8 21.2 %copy-start.33 = (s32[16]{0:T(128)S(1)}, s32[16]{0:T(128)}, u32[]{:S(2)}) copy-start(s32[16]{0:T(128)} %param.24) | copy-start | bytes 196
  29.8 24.7 %copy-start.34 = (s32[16]{0:T(128)S(1)}, s32[16]{0:T(128)}, u32[]{:S(2)}) copy-start(s32[16]{0:T(128)} %param.23) | copy-start | bytes 196
  30.1 8.6 %collective-permute-start.3 = (bf16[1,2,24,1280]{3,2,1,0:T(8,128)(2,1)S(1)}, bf16[1,2,24,1280]{3,2,1,0:T(8,128)(2,1)S(1)}, u32[]{:S(2)}, u32[]{:S(2)}) collective-permute-start(bf16[1,2,24,1280]{3,2,1,0:T(8,128)(2,1)S(1)} %maximum_select_fusion.5), channel_id=1, source_target_pairs={{0,24},{1,25},{2,26},{3,27},{4,28},{5,29},{6,30},{7,31},{8,0},{9,1... | collective-permute-start | bytes 368648 | tf_op jit(solution)/shard_map/ppermute | solution.py:241
  33.8 13.6 %collective-permute-start.2 = (bf16[1,2,24,1280]{3,2,1,0:T(8,128)(2,1)S(1)}, bf16[1,2,24,1280]{3,2,1,0:T(8,128)(2,1)S(1)}, u32[]{:S(2)}, u32[]{:S(2)}) collective-permute-start(bf16[1,2,24,1280]{3,2,1,0:T(8,128)(2,1)S(1)} %maximum_select_fusion.5), channel_id=1, source_target_pairs={{0,16},{1,17},{2,18},{3,19},{4,20},{5,21},{6,22},{7,23},{8,24},{9,... | collective-permute-start | bytes 368648 | tf_op jit(solution)/shard_map/ppermute | solution.py:241
  33.8 13.6 %collective-permute-start.1 = (bf16[1,2,24,1280]{3,2,1,0:T(8,128)(2,1)S(1)}, bf16[1,2,24,1280]{3,2,1,0:T(8,128)(2,1)S(1)}, u32[]{:S(2)}, u32[]{:S(2)}) collective-permute-start(bf16[1,2,24,1280]{3,2,1,0:T(8,128)(2,1)S(1)} %maximum_select_fusion.5), channel_id=1, source_target_pairs={{0,8},{1,9},{2,10},{3,11},{4,12},{5,13},{6,14},{7,15},{8,16},{9,17... | collective-permute-start | bytes 368648 | tf_op jit(solution)/shard_map/ppermute | solution.py:241
  50.2 23.4 %copy-start.4 = (bf16[1024,768]{0,1:T(8,128)(2,1)}, bf16[1024,768]{0,1:T(8,128)(2,1)S(1)}, u32[]{:S(2)}) copy-start(bf16[1024,768]{0,1:T(8,128)(2,1)S(1)} %pad_maximum_fusion.2) | copy-start | bytes 4718596
  50.2 20.6 %copy-start.11 = (bf16[2,512,768]{2,1,0:T(8,128)(2,1)S(1)}, bf16[2,512,768]{2,1,0:T(8,128)(2,1)}, u32[]{:S(2)}) copy-start(bf16[2,512,768]{2,1,0:T(8,128)(2,1)} %param.22) | copy-start | bytes 4718596
  51.0 14.5 %collective-permute-start.7 = (bf16[1024,768]{0,1:T(8,128)(2,1)S(1)}, bf16[1024,768]{0,1:T(8,128)(2,1)}, u32[]{:S(2)}, u32[]{:S(2)}) collective-permute-start(bf16[1024,768]{0,1:T(8,128)(2,1)S(1)} %pad_maximum_fusion.2), channel_id=1, source_target_pairs={{0,1},{1,0},{2,3},{3,2},{4,5},{5,4},{6,7},{7,6},{8,9},{9,8},{10,11... | collective-permute-start | bytes 4718600 | tf_op jit(solution)/shard_map/ppermute | solution.py:374
  51.3 14.3 %collective-permute-start.5 = (bf16[4,2,24,640]{3,2,1,0:T(8,128)(2,1)}, bf16[4,2,24,640]{3,2,1,0:T(8,128)(2,1)}, u32[]{:S(2)}, u32[]{:S(2)}) collective-permute-start(bf16[4,2,24,640]{3,2,1,0:T(8,128)(2,1)} %get-tuple-element.128), channel_id=1, source_target_pairs={{0,4},{1,5},{2,6},{3,7},{4,0},{5,1},{6,2},{7,3},{8,12},{9,13},{10,... | collective-permute-start | bytes 737288 | tf_op jit(solution)/shard_map/ppermute | solution.py:211
  53.0 12.5 %collective-permute-start.6 = (bf16[4,2,24,640]{3,2,1,0:T(8,128)(2,1)S(1)}, bf16[4,2,24,640]{3,2,1,0:T(8,128)(2,1)}, u32[]{:S(2)}, u32[]{:S(2)}) collective-permute-start(bf16[4,2,24,640]{3,2,1,0:T(8,128)(2,1)S(1)} %get-tuple-element.129), channel_id=1, source_target_pairs={{0,2},{1,3},{2,0},{3,1},{4,6},{5,7},{6,4},{7,5},{8,10},{9,11},{10,... | collective-permute-start | bytes 737288 | tf_op jit(solution)/shard_map/ppermute | solution.py:211
  67.8 15.8 %collective-permute-start.8 = (bf16[8,2,24,640]{3,2,1,0:T(8,128)(2,1)}, bf16[8,2,24,640]{3,2,1,0:T(8,128)(2,1)}, u32[]{:S(2)}, u32[]{:S(2)}) collective-permute-start(bf16[8,2,24,640]{3,2,1,0:T(8,128)(2,1)} %get-tuple-element.133), channel_id=1, source_target_pairs={{0,2},{1,3},{2,0},{3,1},{4,6},{5,7},{6,4},{7,5},{8,10},{9,11},{10,... | collective-permute-start | bytes 1474568 | tf_op jit(solution)/shard_map/ppermute | solution.py:211
  69.4 19.3 %collective-permute-start.9 = (bf16[8,2,24,640]{3,2,1,0:T(8,128)(2,1)}, bf16[8,2,24,640]{3,2,1,0:T(8,128)(2,1)}, u32[]{:S(2)}, u32[]{:S(2)}) collective-permute-start(bf16[8,2,24,640]{3,2,1,0:T(8,128)(2,1)} %get-tuple-element.134), channel_id=1, source_target_pairs={{0,4},{1,5},{2,6},{3,7},{4,0},{5,1},{6,2},{7,3},{8,12},{9,13},{10,... | collective-permute-start | bytes 1474568 | tf_op jit(solution)/shard_map/ppermute | solution.py:211
  73.6 69.4 %all-to-all-start = ((bf16[2,512,768]{2,0,1:T(2,128)(2,1)}), bf16[2,512,768]{2,0,1:T(2,128)(2,1)}, u32[]{:S(2)}, u32[]{:S(2)}) async-start(bf16[2,512,768]{2,0,1:T(2,128)(2,1)} %copy.90), calls=%async_computation | async-start | bytes 3145728 | tf_op jit(solution)/shard_map/all_to_all | solution.py:487
  151.9 41.6 %all-to-all-start.1 = ((bf16[16,64,768]{2,1,0:T(8,128)(2,1)}), bf16[16,64,768]{2,1,0:T(8,128)(2,1)}, u32[]{:S(2)}, u32[]{:S(2)}) async-start(bf16[16,64,768]{2,1,0:T(8,128)(2,1)} %broadcast_select_fusion), calls=%async_computation.1 | async-start | bytes 3145728 | tf_op jit(solution)/shard_map/all_to_all | solution.py:508
  159.7 329.3 %reduce-scatter.2.cloned.1.call-start = ((), (), s32[]{:S(2)}) async-start(), calls=%async_computation.3 | async-start | bytes 4866048 | tf_op jit(solution)/shard_map/reduce_scatter | solution.py:534
  180.6 25.4 %collective-permute-start.10 = (bf16[1024,384]{1,0:T(8,128)(2,1)}, bf16[1024,384]{1,0:T(8,128)(2,1)}, u32[]{:S(2)}, u32[]{:S(2)}) collective-permute-start(bf16[1024,384]{1,0:T(8,128)(2,1)} %get-tuple-element.355), channel_id=1, source_target_pairs={{0,1},{1,0},{2,3},{3,2},{4,5},{5,4},{6,7},{7,6},{8,9},{9,8},{10,11... | collective-permute-start | bytes 2359304 | tf_op jit(solution)/shard_map/ppermute | solution.py:374
  201.0 5.1 %copy-start.5 = (bf16[1024,768]{0,1:T(8,128)(2,1)S(1)}, bf16[1024,768]{0,1:T(8,128)(2,1)}, u32[]{:S(2)}) copy-start(bf16[1024,768]{0,1:T(8,128)(2,1)} %copy-done.4) | copy-start | bytes 4718596
  201.0 5.1 %copy-start.22 = (bf16[1024,384]{1,0:T(8,128)(2,1)S(1)}, bf16[1024,384]{1,0:T(8,128)(2,1)}, u32[]{:S(2)}) copy-start(bf16[1024,384]{1,0:T(8,128)(2,1)} %get-tuple-element.354) | copy-start | bytes 2359300
  206.1 3.5 copy-start.16
  215.2 28.7 %collective-permute-start.12 = (bf16[512,768]{0,1:T(8,128)(2,1)}, bf16[512,768]{0,1:T(8,128)(2,1)}, u32[]{:S(2)}, u32[]{:S(2)}) collective-permute-start(bf16[512,768]{0,1:T(8,128)(2,1)} %bitcast.200), channel_id=1, source_target_pairs={{0,2},{1,3},{2,0},{3,1},{4,6},{5,7},{6,4},{7,5},{8,10},{9,11},{10,... | collective-permute-start | bytes 2359304 | tf_op jit(solution)/shard_map/ppermute | solution.py:365
  216.7 12.2 %copy-start.12 = (bf16[1024,768]{0,1:T(8,128)(2,1)S(1)}, bf16[1024,768]{0,1:T(8,128)(2,1)}, u32[]{:S(2)}) copy-start(bf16[1024,768]{0,1:T(8,128)(2,1)} %add_convert_fusion.2) | copy-start | bytes 4718596
  229.0 10.2 %copy-start.36 = (bf16[1024,3072]{1,0:T(8,128)(2,1)}, bf16[1024,3072]{1,0:T(8,128)(2,1)S(1)}, u32[]{:S(2)}) copy-start(bf16[1024,3072]{1,0:T(8,128)(2,1)S(1)} %get-tuple-element.408) | copy-start | bytes 18874372
  244.3 4.4 copy-start.3
  244.3 7.6 %slice-start.1 = ((s8[4718592]{0:T(1024)(128)(4,1)}), s8[4194304]{0:T(1024)(128)(4,1)S(1)}, s32[]{:S(2)}) async-start(s8[4718592]{0:T(1024)(128)(4,1)} %bitcast.177), calls=%async_computation.6 | async-start | bytes 8388608
  252.0 11.9 %copy-start.18 = (bf16[32,24,768]{2,1,0:T(8,128)(2,1)S(1)}, bf16[32,24,768]{2,1,0:T(8,128)(2,1)}, u32[]{:S(2)}) copy-start(bf16[32,24,768]{2,1,0:T(8,128)(2,1)} %get-tuple-element.338) | copy-start | bytes 3538948
  252.0 11.9 %copy-start.19 = (bf16[32,24,768]{2,1,0:T(8,128)(2,1)S(1)}, bf16[32,24,768]{2,1,0:T(8,128)(2,1)}, u32[]{:S(2)}) copy-start(bf16[32,24,768]{2,1,0:T(8,128)(2,1)} %get-tuple-element.339) | copy-start | bytes 3538948
  252.0 11.9 %copy-start.20 = (bf16[32,24,768]{2,1,0:T(8,128)(2,1)S(1)}, bf16[32,24,768]{2,1,0:T(8,128)(2,1)}, u32[]{:S(2)}) copy-start(bf16[32,24,768]{2,1,0:T(8,128)(2,1)} %get-tuple-element.340) | copy-start | bytes 3538948
  252.0 11.9 %copy-start.21 = (bf16[32,24,768]{2,1,0:T(8,128)(2,1)S(1)}, bf16[32,24,768]{2,1,0:T(8,128)(2,1)}, u32[]{:S(2)}) copy-start(bf16[32,24,768]{2,1,0:T(8,128)(2,1)} %get-tuple-element.341) | copy-start | bytes 3538948
  263.9 14.9 %copy-start.35 = (bf16[1024,3072]{1,0:T(8,128)(2,1)}, bf16[1024,3072]{1,0:T(8,128)(2,1)S(1)}, u32[]{:S(2)}) copy-start(bf16[1024,3072]{1,0:T(8,128)(2,1)S(1)} %get-tuple-element.414) | copy-start | bytes 18874372
  274.8 3.9 copy-start.13
  278.2 15.7 %collective-permute-start.15 = (bf16[768,384]{1,0:T(8,128)(2,1)}, bf16[768,384]{1,0:T(8,128)(2,1)}, u32[]{:S(2)}, u32[]{:S(2)}) collective-permute-start(bf16[768,384]{1,0:T(8,128)(2,1)} %convolution_convert_fusion.3), channel_id=1, source_target_pairs={{0,1},{1,0},{2,3},{3,2},{4,5},{5,4},{6,7},{7,6},{8,9},{9,8},{10,11... | collective-permute-start | bytes 1769480 | tf_op jit(solution)/shard_map/ppermute | solution.py:374
  278.2 5.0 slice-start.3
  278.2 5.0 slice-start.4
  278.2 19.2 %collective-permute-start.13 = (bf16[1024,384]{1,0:T(8,128)(2,1)}, bf16[1024,384]{1,0:T(8,128)(2,1)}, u32[]{:S(2)}, u32[]{:S(2)}) collective-permute-start(bf16[1024,384]{1,0:T(8,128)(2,1)} %get-tuple-element.349), channel_id=1, source_target_pairs={{0,1},{1,0},{2,3},{3,2},{4,5},{5,4},{6,7},{7,6},{8,9},{9,8},{10,11... | collective-permute-start | bytes 2359304 | tf_op jit(solution)/shard_map/ppermute | solution.py:374
  283.1 16.9 %collective-permute-start.14 = (bf16[768,1536]{1,0:T(8,128)(2,1)}, bf16[768,1536]{1,0:T(8,128)(2,1)}, u32[]{:S(2)}, u32[]{:S(2)}) collective-permute-start(bf16[768,1536]{1,0:T(8,128)(2,1)} %convolution_convert_fusion.1), channel_id=1, source_target_pairs={{0,1},{1,0},{2,3},{3,2},{4,5},{5,4},{6,7},{7,6},{8,9},{9,8},{10,11... | collective-permute-start | bytes 7077896 | tf_op jit(solution)/shard_map/ppermute | solution.py:374
  293.4 20.2 %collective-permute-start.11 = (bf16[512,768]{0,1:T(8,128)(2,1)}, bf16[512,768]{0,1:T(8,128)(2,1)}, u32[]{:S(2)}, u32[]{:S(2)}) collective-permute-start(bf16[512,768]{0,1:T(8,128)(2,1)} %get-tuple-element.353), channel_id=1, source_target_pairs={{0,2},{1,3},{2,0},{3,1},{4,6},{5,7},{6,4},{7,5},{8,10},{9,11},{10,... | collective-permute-start | bytes 2359304 | tf_op jit(solution)/shard_map/ppermute | solution.py:368
  294.0 3.5 copy-start.8
  313.6 30.0 %collective-permute-start.17 = (bf16[4,2,48,896]{3,2,1,0:T(8,128)(2,1)S(1)}, bf16[4,2,48,896]{3,2,1,0:T(8,128)(2,1)}, u32[]{:S(2)}, u32[]{:S(2)}) collective-permute-start(bf16[4,2,48,896]{3,2,1,0:T(8,128)(2,1)S(1)} %get-tuple-element.148), channel_id=1, source_target_pairs={{0,2},{1,3},{2,0},{3,1},{4,6},{5,7},{6,4},{7,5},{8,10},{9,11},{10,... | collective-permute-start | bytes 2064392 | tf_op jit(solution)/shard_map/ppermute | solution.py:211
  314.1 29.5 %collective-permute-start.16 = (bf16[4,2,48,1024]{3,2,1,0:T(8,128)(2,1)S(1)}, bf16[4,2,48,1024]{3,2,1,0:T(8,128)(2,1)S(1)}, u32[]{:S(2)}, u32[]{:S(2)}) collective-permute-start(bf16[4,2,48,1024]{3,2,1,0:T(8,128)(2,1)S(1)} %get-tuple-element.146), channel_id=1, source_target_pairs={{0,4},{1,5},{2,6},{3,7},{4,0},{5,1},{6,2},{7,3},{8,12},{9,13},{10,... | collective-permute-start | bytes 2359304 | tf_op jit(solution)/shard_map/ppermute | solution.py:211
  346.7 32.6 %collective-permute-start.20 = (bf16[4,2,48,384]{3,2,1,0:T(8,128)(2,1)S(1)}, bf16[4,2,48,384]{3,2,1,0:T(8,128)(2,1)S(1)}, u32[]{:S(2)}, u32[]{:S(2)}) collective-permute-start(bf16[4,2,48,384]{3,2,1,0:T(8,128)(2,1)S(1)} %get-tuple-element.164), channel_id=1, source_target_pairs={{0,4},{1,5},{2,6},{3,7},{4,0},{5,1},{6,2},{7,3},{8,12},{9,13},{10,... | collective-permute-start | bytes 884744 | tf_op jit(solution)/shard_map/ppermute | solution.py:211
  347.5 31.8 %collective-permute-start.19 = (bf16[4,48,896]{2,1,0:T(8,128)(2,1)S(1)}, bf16[4,48,896]{2,1,0:T(8,128)(2,1)S(1)}, u32[]{:S(2)}, u32[]{:S(2)}) collective-permute-start(bf16[4,48,896]{2,1,0:T(8,128)(2,1)S(1)} %get-tuple-element.162), channel_id=1, source_target_pairs={{0,4},{1,5},{2,6},{3,7},{4,0},{5,1},{6,2},{7,3},{8,12},{9,13},{10,... | collective-permute-start | bytes 1032200 | tf_op jit(solution)/shard_map/ppermute | solution.py:211
  348.8 30.5 %collective-permute-start.18 = (bf16[4,48,1024]{2,1,0:T(8,128)(2,1)S(1)}, bf16[4,48,1024]{2,1,0:T(8,128)(2,1)S(1)}, u32[]{:S(2)}, u32[]{:S(2)}) collective-permute-start(bf16[4,48,1024]{2,1,0:T(8,128)(2,1)S(1)} %get-tuple-element.160), channel_id=1, source_target_pairs={{0,2},{1,3},{2,0},{3,1},{4,6},{5,7},{6,4},{7,5},{8,10},{9,11},{10,... | collective-permute-start | bytes 1179656 | tf_op jit(solution)/shard_map/ppermute | solution.py:211
  382.5 34.1 %collective-permute-start.24 = (bf16[4,48,384]{2,1,0:T(8,128)(2,1)S(1)}, bf16[4,48,384]{2,1,0:T(8,128)(2,1)S(1)}, u32[]{:S(2)}, u32[]{:S(2)}) collective-permute-start(bf16[4,48,384]{2,1,0:T(8,128)(2,1)S(1)} %get-tuple-element.183), channel_id=1, source_target_pairs={{0,2},{1,3},{2,0},{3,1},{4,6},{5,7},{6,4},{7,5},{8,10},{9,11},{10,... | collective-permute-start | bytes 442376 | tf_op jit(solution)/shard_map/ppermute | solution.py:211
  383.1 33.5 %collective-permute-start.21 = (bf16[48,1920]{1,0:T(8,128)(2,1)S(1)}, bf16[48,1920]{1,0:T(8,128)(2,1)S(1)}, u32[]{:S(2)}, u32[]{:S(2)}) collective-permute-start(bf16[48,1920]{1,0:T(8,128)(2,1)S(1)} %get-tuple-element.179), channel_id=1, source_target_pairs={{0,8},{1,9},{2,10},{3,11},{4,12},{5,13},{6,14},{7,15},{8,16},{9,17... | collective-permute-start | bytes 552968 | tf_op jit(solution)/shard_map/ppermute | solution.py:241
  383.1 33.5 %collective-permute-start.22 = (bf16[48,1920]{1,0:T(8,128)(2,1)S(1)}, bf16[48,1920]{1,0:T(8,128)(2,1)S(1)}, u32[]{:S(2)}, u32[]{:S(2)}) collective-permute-start(bf16[48,1920]{1,0:T(8,128)(2,1)S(1)} %get-tuple-element.180), channel_id=1, source_target_pairs={{0,16},{1,17},{2,18},{3,19},{4,20},{5,21},{6,22},{7,23},{8,24},{9,... | collective-permute-start | bytes 552968 | tf_op jit(solution)/shard_map/ppermute | solution.py:241
  385.0 31.7 %collective-permute-start.23 = (bf16[48,1920]{1,0:T(8,128)(2,1)S(1)}, bf16[48,1920]{1,0:T(8,128)(2,1)S(1)}, u32[]{:S(2)}, u32[]{:S(2)}) collective-permute-start(bf16[48,1920]{1,0:T(8,128)(2,1)S(1)} %get-tuple-element.181), channel_id=1, source_target_pairs={{0,24},{1,25},{2,26},{3,27},{4,28},{5,29},{6,30},{7,31},{8,0},{9,1... | collective-permute-start | bytes 552968 | tf_op jit(solution)/shard_map/ppermute | solution.py:241
  386.9 29.8 %collective-permute-start.25 = (bf16[4,2,48,384]{3,2,1,0:T(8,128)(2,1)S(1)}, bf16[4,2,48,384]{3,2,1,0:T(8,128)(2,1)}, u32[]{:S(2)}, u32[]{:S(2)}) collective-permute-start(bf16[4,2,48,384]{3,2,1,0:T(8,128)(2,1)S(1)} %get-tuple-element.185), channel_id=1, source_target_pairs={{0,4},{1,5},{2,6},{3,7},{4,0},{5,1},{6,2},{7,3},{8,12},{9,13},{10,... | collective-permute-start | bytes 884744 | tf_op jit(solution)/shard_map/ppermute | solution.py:211
  422.3 6.5 %copy-start.10 = (bf16[16,2,24,1280]{3,2,1,0:T(8,128)(2,1)S(1)}, bf16[16,2,24,1280]{3,2,1,0:T(8,128)(2,1)}, u32[]{:S(2)}) copy-start(bf16[16,2,24,1280]{3,2,1,0:T(8,128)(2,1)} %copy-done.9) | copy-start | bytes 5898244
  426.1 11.4 %collective-permute-start.26 = (bf16[4,48,384]{2,1,0:T(8,128)(2,1)S(1)}, bf16[4,48,384]{2,1,0:T(8,128)(2,1)}, u32[]{:S(2)}, u32[]{:S(2)}) collective-permute-start(bf16[4,48,384]{2,1,0:T(8,128)(2,1)S(1)} %get-tuple-element.195), channel_id=1, source_target_pairs={{0,2},{1,3},{2,0},{3,1},{4,6},{5,7},{6,4},{7,5},{8,10},{9,11},{10,... | collective-permute-start | bytes 442376 | tf_op jit(solution)/shard_map/ppermute | solution.py:211
  427.7 9.9 %collective-permute-start.27 = (bf16[4,2,56,384]{3,2,1,0:T(8,128)(2,1)S(1)}, bf16[4,2,56,384]{3,2,1,0:T(8,128)(2,1)}, u32[]{:S(2)}, u32[]{:S(2)}) collective-permute-start(bf16[4,2,56,384]{3,2,1,0:T(8,128)(2,1)S(1)} %get-tuple-element.197), channel_id=1, source_target_pairs={{0,4},{1,5},{2,6},{3,7},{4,0},{5,1},{6,2},{7,3},{8,12},{9,13},{10,... | collective-permute-start | bytes 1032200 | tf_op jit(solution)/shard_map/ppermute | solution.py:211
  444.1 5.1 %copy-start.26 = (bf16[4,48,384]{2,1,0:T(8,128)(2,1)S(1)}, bf16[4,48,384]{2,1,0:T(8,128)(2,1)}, u32[]{:S(2)}) copy-start(bf16[4,48,384]{2,1,0:T(8,128)(2,1)} %get-tuple-element.201) | copy-start | bytes 442372
  450.9 16.0 %collective-permute-start.28 = (bf16[1024,768]{0,1:T(8,128)(2,1)}, bf16[1024,768]{0,1:T(8,128)(2,1)}, u32[]{:S(2)}, u32[]{:S(2)}) collective-permute-start(bf16[1024,768]{0,1:T(8,128)(2,1)} %slice.399), channel_id=1, source_target_pairs={{0,1},{1,0},{2,3},{3,2},{4,5},{5,4},{6,7},{7,6},{8,9},{9,8},{10,11... | collective-permute-start | bytes 4718600 | tf_op jit(solution)/shard_map/ppermute | solution.py:374
  452.9 6.4 %collective-permute-start.35 = (f32[24,1920]{1,0:T(8,128)}, f32[24,1920]{1,0:T(8,128)}, u32[]{:S(2)}, u32[]{:S(2)}) collective-permute-start(f32[24,1920]{1,0:T(8,128)} %get-tuple-element.381), channel_id=1, source_target_pairs={{0,1},{1,0},{2,3},{3,2},{4,5},{5,4},{6,7},{7,6},{8,9},{9,8},{10,11... | collective-permute-start | bytes 552968 | tf_op jit(solution)/shard_map/ppermute | solution.py:374
  459.2 8.9 %copy-start.2 = (f32[1024,768]{0,1:T(8,128)S(1)}, f32[1024,768]{0,1:T(8,128)}, u32[]{:S(2)}) copy-start(f32[1024,768]{0,1:T(8,128)} %copy-done.1) | copy-start | bytes 9437188
  460.4 6.6 %collective-permute-start.29 = (bf16[4,56,384]{2,1,0:T(8,128)(2,1)}, bf16[4,56,384]{2,1,0:T(8,128)(2,1)S(1)}, u32[]{:S(2)}, u32[]{:S(2)}) collective-permute-start(bf16[4,56,384]{2,1,0:T(8,128)(2,1)} %get-tuple-element.208), channel_id=1, source_target_pairs={{0,2},{1,3},{2,0},{3,1},{4,6},{5,7},{6,4},{7,5},{8,10},{9,11},{10,... | collective-permute-start | bytes 516104 | tf_op jit(solution)/shard_map/ppermute | solution.py:211
  471.7 8.3 %collective-permute-start.31 = (bf16[56,1152]{1,0:T(8,128)(2,1)S(1)}, bf16[56,1152]{1,0:T(8,128)(2,1)S(1)}, u32[]{:S(2)}, u32[]{:S(2)}) collective-permute-start(bf16[56,1152]{1,0:T(8,128)(2,1)S(1)} %get-tuple-element.217), channel_id=1, source_target_pairs={{0,8},{1,9},{2,10},{3,11},{4,12},{5,13},{6,14},{7,15},{8,16},{9,17... | collective-permute-start | bytes 387080 | tf_op jit(solution)/shard_map/ppermute | solution.py:241
  472.3 11.4 %collective-permute-start.32 = (bf16[56,1152]{1,0:T(8,128)(2,1)S(1)}, bf16[56,1152]{1,0:T(8,128)(2,1)S(1)}, u32[]{:S(2)}, u32[]{:S(2)}) collective-permute-start(bf16[56,1152]{1,0:T(8,128)(2,1)S(1)} %get-tuple-element.218), channel_id=1, source_target_pairs={{0,16},{1,17},{2,18},{3,19},{4,20},{5,21},{6,22},{7,23},{8,24},{9,... | collective-permute-start | bytes 387080 | tf_op jit(solution)/shard_map/ppermute | solution.py:241
  473.8 9.9 %collective-permute-start.33 = (bf16[56,1152]{1,0:T(8,128)(2,1)S(1)}, bf16[56,1152]{1,0:T(8,128)(2,1)S(1)}, u32[]{:S(2)}, u32[]{:S(2)}) collective-permute-start(bf16[56,1152]{1,0:T(8,128)(2,1)S(1)} %get-tuple-element.219), channel_id=1, source_target_pairs={{0,24},{1,25},{2,26},{3,27},{4,28},{5,29},{6,30},{7,31},{8,0},{9,1... | collective-permute-start | bytes 387080 | tf_op jit(solution)/shard_map/ppermute | solution.py:241
  476.8 17.8 %collective-permute-start.30 = (bf16[512,768]{0,1:T(8,128)(2,1)S(1)}, bf16[512,768]{0,1:T(8,128)(2,1)S(1)}, u32[]{:S(2)}, u32[]{:S(2)}) collective-permute-start(bf16[512,768]{0,1:T(8,128)(2,1)S(1)} %get-tuple-element.345), channel_id=1, source_target_pairs={{0,2},{1,3},{2,0},{3,1},{4,6},{5,7},{6,4},{7,5},{8,10},{9,11},{10,... | collective-permute-start | bytes 2359304 | tf_op jit(solution)/shard_map/ppermute | solution.py:368
  483.8 1.2 collective-permute-start.36
  484.0 2.4 collective-permute-start.34
  (19 other events, 34.5 us)
Sparse Core Ops, SparseCore 0:
  12.9 129.2 all-gather.2
  290.3 110.7 reduce-scatter.1
